TPU v7x, 32 devices: a whole 2x2x4 slice. The times are simulated.
32 devices in a mesh: seq: 8 (over y, x, core), wt: 4 (over z).
Axes of the slice: x: 2, y: 2, z: 4, core: 2. Of those that a mesh axis runs over, the one named last changes fastest.
Arguments:
- tokens: bfloat16 [4, 1024, 2048], P('wt', 'seq'), may hold values from -6 to 6
- segment_ids: int32 [4, 1024], P('wt', 'seq'), may hold values from 0 to 15, never falling along the last dimension, each value on 1 to 512 neighbouring positions
- norm_gain: bfloat16 [2048], P('wt'), may hold values from 0.5 to 1.5
- in_weight: bfloat16 [8192, 2048], P('wt'), may hold values from -0.125 to 0.125
- conv_weight: bfloat16 [4, 4096], P(None, 'wt'), may hold values from -3 to 3
- conv_bias: bfloat16 [4096], P('wt'), may hold values from -3 to 3
- proj_weight: bfloat16 [4096, 160], P('wt'), may hold values from -0.09375 to 0.09375
- dt_weight: bfloat16 [4096, 128], P('wt'), may hold values from -0.5 to 0.5
- dt_bias: bfloat16 [4096], P('wt'), may hold values from -9 to 0
- skip_weight: bfloat16 [4096], P('wt'), may hold values from 0.5 to 1.5
- out_weight: bfloat16 [4096, 2048], P('wt'), may hold values from -0.1875 to 0.1875
- cotangent: bfloat16 [4, 1024, 2048], P('wt', 'seq'), may hold values from -6 to 6
Outputs:
- block_output: bfloat16 [4, 1024, 2048], P('wt', 'seq')
- token_grad: bfloat16 [4, 1024, 2048], P('wt', 'seq')
- gain_grad: float32 [2048], P('wt')
- in_grad: float32 [8192, 2048], P('wt')
- conv_weight_grad: float32 [4, 4096], P(None, 'wt')
- conv_bias_grad: float32 [4096], P('wt')
- proj_grad: float32 [4096, 160], P('wt')
- dt_grad: float32 [4096, 128], P('wt')
- dt_bias_grad: float32 [4096], P('wt')
- skip_grad: float32 [4096], P('wt')
- out_grad: float32 [4096, 2048], P('wt')
Inputs may be any that keep to these rules, and one draw needn't show every extreme that they name: `segment_ids`: within each sequence the ids never fall; every number of 0 to 15 marks one document of 1 to 512 tokens, and one document has exactly 512.
All inputs are finite; a program needn't handle non-finite values.
Results may differ from a plain program's by a relative error of at most 0.011.
Values may be sent and summed in bfloat16 or wider, within the bound.
No kernel may reach another device: no remote copies, remote signals or barrier semaphores. Data moves between devices by JAX's collectives and lax.ppermute only.
A program may use at most 248 MiB of HBM per device.

v0:
```python
import jax
import jax.numpy as jnp
from jax import lax
from jax.sharding import PartitionSpec as P

STATE = 16
KERNEL = 4


norm_eps = 1e-05


def shifted(value, axis, steps):
    count = lax.axis_size(axis)
    leading, last = (max(0, -steps), min(count, count - steps))
    return lax.ppermute(value, axis, [(source, source + steps) for source in range(leading, last)])


def entering(shard, axis, combine, identity, reverse):
    count, mine = (lax.axis_size(axis), lax.axis_index(axis))
    everything = jax.tree.map(lambda part: lax.all_gather(part, axis), shard)
    start = jax.tree.map(
        lambda part, zero: jnp.broadcast_to(jnp.asarray(zero, part.dtype), part.shape),
        shard,
        identity,
    )

    def step(k, before):
        at = count - 1 - k if reverse else k
        reached = at > mine if reverse else at < mine
        new = combine(before, jax.tree.map(lambda part: part[at], everything))
        return jax.tree.map(lambda a, b: jnp.where(reached, a, b), new, before)

    return lax.fori_loop(0, count, step, start)


def affine(earlier, later):
    return (later[0] * earlier[0], later[0] * earlier[1] + later[1])


def state_step(state_now, inputs):
    keep_now, rate_now, value_now, key_now, query_now = inputs
    decay = 1.0 - key_now[:, None] * key_now[:, None] * rate_now[None, :]
    state_now = keep_now * decay * state_now + key_now[:, None] * (rate_now * value_now)[None, :]
    return (state_now, jnp.sum(query_now[:, None] * state_now, axis=0))


def blocked_scan(state_now, inputs):
    return lax.scan(state_step, state_now, inputs)


def rate_terms(query_key, beta_pre, dt_bias32):
    query_vec = query_key[:, :STATE]
    key_vec = query_key[:, STATE:]
    beta_rate = jax.nn.softplus(beta_pre + dt_bias32)
    rate_vec = beta_rate / (1.0 + beta_rate * jnp.sum(key_vec * key_vec, axis=1, keepdims=True))
    return (query_vec, key_vec, rate_vec)


def mixer_core(state_in, conv_vals, query_key, beta_pre, dt_bias32, skip32, gate_pre, keep_mask):
    query_vec, key_vec, rate_vec = rate_terms(query_key, beta_pre, dt_bias32)
    state_end, core_out = blocked_scan(
        state_in, (keep_mask, rate_vec, conv_vals, key_vec, query_vec)
    )
    return ((core_out + skip32 * conv_vals) * jax.nn.silu(gate_pre), state_end)


def block_summary(keep_mask, rate_vec, conv_vals, key_vec):

    def summary_step(carry, inputs):
        decay_total, state_now = carry
        keep_now, rate_now, value_now, key_now = inputs
        decay = keep_now * (1.0 - key_now[:, None] * key_now[:, None] * rate_now[None, :])
        state_now = decay * state_now + key_now[:, None] * (rate_now * value_now)[None, :]
        return ((decay_total * decay, state_now), None)

    start = (
        jnp.ones((STATE, conv_vals.shape[1]), jnp.float32),
        jnp.zeros((STATE, conv_vals.shape[1]), jnp.float32),
    )
    carry, _ = lax.scan(summary_step, start, (keep_mask, rate_vec, conv_vals, key_vec))
    return carry


def adjoint_summary(keep_mask, rate_vec, key_vec, query_vec, d_mixed):

    def adjoint_step(carry, inputs):
        keep_now, rate_now, key_now, query_now, grad_now = inputs
        adjoint = carry + query_now[:, None] * grad_now[None, :]
        decay = keep_now * (1.0 - key_now[:, None] * key_now[:, None] * rate_now[None, :])
        return (decay * adjoint, None)

    start = jnp.zeros((STATE, d_mixed.shape[1]), jnp.float32)
    carry, _ = lax.scan(
        adjoint_step, start, (keep_mask, rate_vec, key_vec, query_vec, d_mixed), reverse=True
    )
    return carry


def normalize(features, gain32):
    inv_rms = lax.rsqrt(jnp.mean(features * features, axis=1, keepdims=True) + norm_eps)
    return features * inv_rms * gain32


def conv_silu(extended, conv_taps, bias32, same_doc):
    length = same_doc.shape[1]
    conv_sum = bias32
    for offset in range(conv_taps.shape[0]):
        conv_sum = (
            conv_sum
            + conv_taps[offset] * extended[offset : offset + length] * same_doc[offset][:, None]
        )
    return jax.nn.silu(conv_sum)


def forward_local(tokens_dev, segments, weights):
    (
        norm_gain,
        in_weight,
        conv_weight,
        conv_bias,
        proj_weight,
        dt_weight,
        dt_bias,
        skip_weight,
        out_weight,
    ) = weights
    inner_width = out_weight.shape[0]
    length = tokens_dev.shape[0]
    tail = length - KERNEL + 1
    features = tokens_dev.astype(jnp.float32)
    normed = normalize(features, norm_gain.astype(jnp.float32)).astype(jnp.bfloat16)
    projected_in = lax.dot_general(
        normed, in_weight, (((1,), (1,)), ((), ())), preferred_element_type=jnp.float32
    )
    value_rows = projected_in[:, :inner_width].astype(jnp.bfloat16)
    gate_pre = projected_in[:, inner_width:]
    tail_mask = (segments[tail:] == segments[length - 1]).astype(jnp.bfloat16)
    marker = jnp.full((1, inner_width), segments[length - 1], jnp.float32).astype(jnp.bfloat16)
    outgoing = jnp.concatenate([value_rows[tail:] * tail_mask[:, None], marker], axis=0)
    incoming = shifted(outgoing, "seq", 1)
    prior_doc = incoming[KERNEL - 1, 0].astype(jnp.int32)
    ext_ids = jnp.concatenate([jnp.full((KERNEL - 1,), prior_doc, jnp.int32), segments])
    same_doc = jnp.stack(
        [
            (ext_ids[offset : offset + length] == segments).astype(jnp.float32)
            for offset in range(KERNEL)
        ]
    )
    extended = jnp.concatenate([incoming[: KERNEL - 1], value_rows], axis=0)
    keep_mask = same_doc[KERNEL - 2]
    conv_out = conv_silu(
        extended.astype(jnp.float32),
        conv_weight.astype(jnp.float32),
        conv_bias.astype(jnp.float32),
        same_doc,
    ).astype(jnp.bfloat16)
    projected = jnp.dot(conv_out, proj_weight, preferred_element_type=jnp.float32)
    query_key = projected[:, : 2 * STATE]
    low_rank = projected[:, 2 * STATE :].astype(jnp.bfloat16)
    beta_pre = lax.dot_general(
        low_rank, dt_weight, (((1,), (1,)), ((), ())), preferred_element_type=jnp.float32
    )
    query_vec, key_vec, rate_vec = rate_terms(query_key, beta_pre, dt_bias.astype(jnp.float32))
    decay_total, state_local = block_summary(
        keep_mask, rate_vec, conv_out.astype(jnp.float32), key_vec
    )
    decay_before, state_in = entering(
        (decay_total, state_local),
        "seq",
        affine,
        (jnp.ones_like(decay_total), jnp.zeros_like(state_local)),
        False,
    )
    return (
        features,
        normed,
        gate_pre,
        extended,
        same_doc,
        tail_mask,
        conv_out,
        query_key,
        low_rank,
        beta_pre,
        keep_mask,
        decay_total,
        state_in,
    )


def block_result(features, gated, out_weight):
    return (features + jnp.dot(gated, out_weight, preferred_element_type=jnp.float32)).astype(
        jnp.bfloat16
    )


def forward_mixed(kept, weights):
    (
        features,
        normed,
        gate_pre,
        extended,
        same_doc,
        tail_mask,
        conv_out,
        query_key,
        low_rank,
        beta_pre,
        keep_mask,
        decay_total,
        state_in,
    ) = kept
    mixed_gate, _ = mixer_core(
        state_in,
        conv_out.astype(jnp.float32),
        query_key,
        beta_pre,
        weights[6].astype(jnp.float32),
        weights[7].astype(jnp.float32),
        gate_pre,
        keep_mask,
    )
    return block_result(features, mixed_gate.astype(jnp.bfloat16), weights[8])


def backward(kept, weights, cot_dev):
    (
        features,
        normed,
        gate_pre,
        extended,
        same_doc,
        tail_mask,
        conv_out,
        query_key,
        low_rank,
        beta_pre,
        keep_mask,
        decay_total,
        state_in,
    ) = kept
    (
        norm_gain,
        in_weight,
        conv_weight,
        conv_bias,
        proj_weight,
        dt_weight,
        dt_bias,
        skip_weight,
        out_weight,
    ) = weights
    length = features.shape[0]
    tail = length - KERNEL + 1
    conv_vals = conv_out.astype(jnp.float32)
    dt_bias32 = dt_bias.astype(jnp.float32)
    skip32 = skip_weight.astype(jnp.float32)
    d_gated = lax.dot_general(
        cot_dev, out_weight, (((1,), (1,)), ((), ())), preferred_element_type=jnp.float32
    )
    query_vec, key_vec, rate_vec = rate_terms(query_key, beta_pre, dt_bias32)
    local_grad = adjoint_summary(
        keep_mask, rate_vec, key_vec, query_vec, d_gated * jax.nn.silu(gate_pre)
    )
    decay_after, state_grad = entering(
        (decay_total, local_grad),
        "seq",
        affine,
        (jnp.ones_like(decay_total), jnp.zeros_like(local_grad)),
        True,
    )

    def mixer_part(state_start, values_in, query_key_in, beta_in, bias_in, skip_in, gate_in):
        return mixer_core(
            state_start, values_in, query_key_in, beta_in, bias_in, skip_in, gate_in, keep_mask
        )

    primal, pullback = jax.vjp(
        mixer_part, state_in, conv_vals, query_key, beta_pre, dt_bias32, skip32, gate_pre
    )
    gated = primal[0].astype(jnp.bfloat16)
    _, d_value, d_query_key, d_beta, d_dt_bias, d_skip, d_gate_pre = pullback((d_gated, state_grad))
    d_beta_low = d_beta.astype(jnp.bfloat16)
    d_low_rank = jnp.dot(d_beta_low, dt_weight, preferred_element_type=jnp.float32)
    d_dt = lax.dot_general(
        d_beta_low, low_rank, (((0,), (0,)), ((), ())), preferred_element_type=jnp.float32
    )
    d_projected = jnp.concatenate([d_query_key, d_low_rank], axis=1).astype(jnp.bfloat16)
    d_proj = lax.dot_general(
        conv_out, d_projected, (((0,), (0,)), ((), ())), preferred_element_type=jnp.float32
    )
    d_value = d_value + lax.dot_general(
        d_projected, proj_weight, (((1,), (1,)), ((), ())), preferred_element_type=jnp.float32
    )

    def conv_part(ext_in, taps_in, bias_in):
        return conv_silu(ext_in, taps_in, bias_in, same_doc)

    _, conv_pull = jax.vjp(
        conv_part,
        extended.astype(jnp.float32),
        conv_weight.astype(jnp.float32),
        conv_bias.astype(jnp.float32),
    )
    d_extended, d_conv_weight, d_conv_bias = conv_pull(d_value)
    returned = shifted(d_extended[: KERNEL - 1], "seq", -1)
    d_rows = d_extended[KERNEL - 1 :]
    d_rows = jnp.concatenate(
        [d_rows[:tail], d_rows[tail:] + returned * tail_mask.astype(jnp.float32)[:, None]], axis=0
    )
    d_both = jnp.concatenate([d_rows, d_gate_pre], axis=1).astype(jnp.bfloat16)
    d_normed = jnp.dot(d_both, in_weight, preferred_element_type=jnp.float32)
    _, norm_pull = jax.vjp(normalize, features, norm_gain.astype(jnp.float32))
    d_features, d_gain = norm_pull(d_normed)
    token_grad = (cot_dev.astype(jnp.float32) + d_features).astype(jnp.bfloat16)
    small_terms = (d_gain, d_conv_weight, d_conv_bias, d_proj, d_dt, d_dt_bias, d_skip)
    return (gated, d_both, token_grad, small_terms)


def on_device(
    tokens,
    segment_ids,
    norm_gain,
    in_weight,
    conv_weight,
    conv_bias,
    proj_weight,
    dt_weight,
    dt_bias,
    skip_weight,
    out_weight,
    cotangent,
):
    weights = (
        lax.all_gather(norm_gain, "wt", axis=0, tiled=True),
        lax.all_gather(in_weight, "wt", axis=0, tiled=True),
        lax.all_gather(conv_weight, "wt", axis=1, tiled=True),
        lax.all_gather(conv_bias, "wt", axis=0, tiled=True),
        lax.all_gather(proj_weight, "wt", axis=0, tiled=True),
        lax.all_gather(dt_weight, "wt", axis=0, tiled=True),
        lax.all_gather(dt_bias, "wt", axis=0, tiled=True),
        lax.all_gather(skip_weight, "wt", axis=0, tiled=True),
        lax.all_gather(out_weight, "wt", axis=0, tiled=True),
    )
    tokens_dev = tokens[0]
    segments = segment_ids[0]
    cot_dev = cotangent[0]
    kept = forward_local(tokens_dev, segments, weights)
    result = forward_mixed(kept, weights)
    weights = (
        lax.all_gather(norm_gain, "wt", axis=0, tiled=True),
        lax.all_gather(in_weight, "wt", axis=0, tiled=True),
        lax.all_gather(conv_weight, "wt", axis=1, tiled=True),
        lax.all_gather(conv_bias, "wt", axis=0, tiled=True),
        lax.all_gather(proj_weight, "wt", axis=0, tiled=True),
        lax.all_gather(dt_weight, "wt", axis=0, tiled=True),
        lax.all_gather(dt_bias, "wt", axis=0, tiled=True),
        lax.all_gather(skip_weight, "wt", axis=0, tiled=True),
        lax.all_gather(out_weight, "wt", axis=0, tiled=True),
    )
    kept = forward_local(tokens_dev, segments, weights)
    gated, d_both, token_grad, small_terms = backward(kept, weights, cot_dev)
    normed = kept[1]
    both_cols, gated_cols = (
        lax.all_to_all(d_both, "wt", split_axis=1, concat_axis=0, tiled=True),
        lax.all_to_all(gated, "wt", split_axis=1, concat_axis=0, tiled=True),
    )
    normed_all, cot_all = (
        lax.all_gather(normed, "wt", axis=0, tiled=True),
        lax.all_gather(cot_dev, "wt", axis=0, tiled=True),
    )
    in_share = lax.dot_general(
        both_cols, normed_all, (((0,), (0,)), ((), ())), preferred_element_type=jnp.float32
    )
    out_share = lax.dot_general(
        gated_cols, cot_all, (((0,), (0,)), ((), ())), preferred_element_type=jnp.float32
    )
    gain_part, conv_w_part, conv_b_part, proj_part, dt_part, dt_b_part, skip_part = (
        lax.psum_scatter(small_terms[0], "wt", scatter_dimension=0, tiled=True),
        lax.psum_scatter(small_terms[1], "wt", scatter_dimension=1, tiled=True),
        lax.psum_scatter(small_terms[2], "wt", scatter_dimension=0, tiled=True),
        lax.psum_scatter(small_terms[3], "wt", scatter_dimension=0, tiled=True),
        lax.psum_scatter(small_terms[4], "wt", scatter_dimension=0, tiled=True),
        lax.psum_scatter(small_terms[5], "wt", scatter_dimension=0, tiled=True),
        lax.psum_scatter(small_terms[6], "wt", scatter_dimension=0, tiled=True),
    )
    summed = lax.psum(
        (
            gain_part,
            in_share,
            conv_w_part,
            conv_b_part,
            proj_part,
            dt_part,
            dt_b_part,
            skip_part,
            out_share,
        ),
        "seq",
    )
    return (
        result[None],
        token_grad[None],
        summed[0],
        summed[1],
        summed[2],
        summed[3],
        summed[4],
        summed[5],
        summed[6],
        summed[7],
        summed[8],
    )


def solution(mesh):
    return jax.shard_map(
        on_device,
        mesh=mesh,
        in_specs=(
            P("wt", "seq", None),
            P("wt", "seq"),
            P("wt"),
            P("wt", None),
            P(None, "wt"),
            P("wt"),
            P("wt", None),
            P("wt", None),
            P("wt"),
            P("wt"),
            P("wt", None),
            P("wt", "seq", None),
        ),
        out_specs=(
            P("wt", "seq", None),
            P("wt", "seq", None),
            P("wt"),
            P("wt", None),
            P(None, "wt"),
            P("wt"),
            P("wt", None),
            P("wt", None),
            P("wt"),
            P("wt"),
            P("wt", None),
        ),
        check_vma=False,
    )
```

profile of v0, /device:TPU:0, one launch (start us, length us, event | category | flops | bytes accessed | tf_op | source)
XLA Modules:
  0.0 4538.3 jit_solution(16646252113238260085)
XLA Ops:
  12.6 13.5 all-gather.4
  26.9 15.3 all_gather.69
  42.4 531.6 %all-gather.15.cloned.1.call-done = bf16[8192,2048]{1,0:T(8,128)(2,1)} async-done(((bf16[2048,2048]{1,0:T(8,128)(2,1)}), bf16[8192,2048]{1,0:T(8,128)(2,1)}) %all-gather.15.cloned.1.call-update) | async-done | bytes 33554448 | tf_op jit(solution)/shard_map/all_gather | solution.py:337
  574.0 19.8 fusion.71
  596.1 16.7 all_gather.68
  612.8 22.7 all_gather.72
  637.8 2.9 maximum_convert_fusion.1
  640.7 220.1 %all-gather.21.cloned.1.call-done = bf16[4096,2048]{1,0:T(8,128)(2,1)} async-done(((bf16[1024,2048]{1,0:T(8,128)(2,1)}), bf16[4096,2048]{1,0:T(8,128)(2,1)}) %all-gather.21.cloned.1.call-update) | async-done | bytes 16777232 | tf_op jit(solution)/shard_map/all_gather | solution.py:344
  860.8 15.0 multiply_reduce_fusion.6
  877.4 15.9 all-gather.17.cloned.1.call-done
  895.2 26.4 all-gather.19.cloned.1.call-done
  921.6 4.9 fusion.36
  926.5 308.5 %while.137 = (s32[]{:T(128)}, f32[16,4096]{1,0:T(8,128)S(1)}, f32[16,4096]{1,0:T(8,128)S(1)}, f32[128]{0:T(128)S(1)}, f32[128,16]{1,0:T(8,128)S(1)}, /*index=5*/...) while((s32[]{:T(128)}, f32[16,4096]{1,0:T(8,128)S(1)}, f32[16,4096]{1,0:T(8,128)S(1)}, ...), condition=%wide.region_3.4_spmd.clone, body=%wide.region_2.3_spmd.clone.sunk | while | flops 593939 | bytes 1147335 | solution.py:81
  1236.4 307.2 %while.139 = (s32[]{:T(128)}, f32[16,4096]{1,0:T(8,128)S(1)}, f32[128]{0:T(128)S(1)}, f32[128,16]{1,0:T(8,128)S(1)}, f32[128,4096]{1,0:T(8,128)}, /*index=5*/f32...) while((s32[]{:T(128)}, f32[16,4096]{1,0:T(8,128)S(1)}, ...), condition=%wide.region_10.11_spmd.clone, body=%wide.region_9.10_spmd.clone.sunk | while | flops 458772 | bytes 623131 | solution.py:94
  1546.2 10.2 while.138
  1558.0 842.8 %while.135 = (s32[]{:T(128)}, f32[16,4096]{1,0:T(8,128)S(1)}, f32[128,4096]{1,0:T(8,128)}, f32[128,16,1]{1,2,0:T(1,128)S(1)}, f32[128,1,4096]{2,1,0:T(1,128)}, /...) while((s32[]{:T(128)}, f32[16,4096]{1,0:T(8,128)S(1)}, ...), condition=%wide.region_15.16_spmd, body=%wide.region_13.15_spmd.sunk | while | flops 725026 | bytes 1808021 | solution.py:49
  2401.4 10.2 while.140
  2414.7 1124.4 %while.136 = (s32[]{:T(128)}, f32[16,4096]{1,0:T(8,128)S(1)}, f32[128,4096]{1,0:T(8,128)}, f32[128,4096]{1,0:T(8,128)}, f32[128,16]{1,0:T(8,128)S(1)}, /*index=5...) while((s32[]{:T(128)}, f32[16,4096]{1,0:T(8,128)S(1)}, ...), condition=%wide.region_22.23_spmd, body=%wide.region_16.22_spmd.sunk | while | flops 1052675 | bytes 1656333 | solution.py:49
  2417.0 2.2 multiply_reduce_fusion.18
  2425.8 2.2 multiply_reduce_fusion.18
  2434.6 2.2 multiply_reduce_fusion.18
  2443.3 2.2 multiply_reduce_fusion.18
  2452.1 2.2 multiply_reduce_fusion.18
  2460.9 2.2 multiply_reduce_fusion.18
  2469.6 2.2 multiply_reduce_fusion.18
  2478.4 2.2 multiply_reduce_fusion.18
  2487.2 2.2 multiply_reduce_fusion.18
  2496.0 2.2 multiply_reduce_fusion.18
  2504.8 2.2 multiply_reduce_fusion.18
  2513.7 2.2 multiply_reduce_fusion.18
  2522.5 2.2 multiply_reduce_fusion.18
  2531.3 2.2 multiply_reduce_fusion.18
  2549.0 2.2 multiply_reduce_fusion.18
  2557.8 2.2 multiply_reduce_fusion.18
  2566.6 2.2 multiply_reduce_fusion.18
  2575.4 2.2 multiply_reduce_fusion.18
  2584.2 2.2 multiply_reduce_fusion.18
  2593.0 2.2 multiply_reduce_fusion.18
  2601.7 2.2 multiply_reduce_fusion.18
  2610.5 2.2 multiply_reduce_fusion.18
  2619.3 2.2 multiply_reduce_fusion.18
  2628.1 2.2 multiply_reduce_fusion.18
  2636.9 2.2 multiply_reduce_fusion.18
  2645.7 2.2 multiply_reduce_fusion.18
  2654.5 2.2 multiply_reduce_fusion.18
  2663.2 2.2 multiply_reduce_fusion.18
  3539.7 5.2 fusion.65
  3546.7 12.2 all_gather.77
  3563.9 9.0 multiply_reduce_fusion.10
  3578.8 5.3 multiply_convert_fusion
  3584.2 3.7 pad_add_fusion
  3590.3 4.3 all-to-all-start.1
  3599.3 46.1 %all-to-all-done.1 = bf16[128,4,1024]{2,0,1:T(8,128)(2,1)} async-done(((bf16[128,4,1024]{2,0,1:T(8,128)(2,1)}), bf16[128,4,1024]{2,0,1:T(8,128)(2,1)}, u32[]{:S(2)}, u32[]{:S(2)}) %all-to-all-start.1) | async-done | bytes 1048608 | tf_op jit(solution)/shard_map/all_to_all | solution.py:367
  3645.3 4.4 all-to-all-start
  3654.1 7.7 fusion.33
  3661.8 59.4 %all-to-all-done = bf16[128,4,2048]{2,0,1:T(8,128)(2,1)} async-done(((bf16[128,4,2048]{2,0,1:T(8,128)(2,1)}), bf16[128,4,2048]{2,0,1:T(8,128)(2,1)}, u32[]{:S(2)}, u32[]{:S(2)}) %all-to-all-start) | async-done | bytes 2097184 | tf_op jit(solution)/shard_map/all_to_all | solution.py:366
  3721.2 13.0 fusion.73
  3735.8 708.4 %while.134 = (s32[]{:T(128)}, f32[16,4096]{1,0:T(8,128)S(1)}, f32[128,4096]{1,0:T(8,128)}, f32[128]{0:T(128)S(1)}, f32[128,16]{1,0:T(8,128)}, /*index=5*/f32[128...) while((s32[]{:T(128)}, f32[16,4096]{1,0:T(8,128)S(1)}, ...), condition=%wide.region_8.9_spmd, body=%wide.region_6.8_spmd.sunk | while | flops 524306 | bytes 672397 | solution.py:49
  4444.3 10.6 fusion.20
  4454.9 13.2 fusion.40
  4468.1 16.9 all-reduce.18
  4487.5 25.3 all-reduce.16
  4512.8 13.5 copy.170
  4527.9 3.4 copy.173
  (4695 shorter events, 3284.6 us)
Async XLA Ops:
  7.2 566.8 %all-gather.15.cloned.1.call-start = ((), (), s32[]{:S(2)}) async-start(), calls=%async_computation.5 | async-start | bytes 41943040 | tf_op jit(solution)/shard_map/all_gather | solution.py:337
  7.9 2.2 copy-start.46
  7.9 4.6 copy-start.47
  7.9 18.2 copy-start.7
  7.9 18.9 copy-start.41
  8.0 852.8 %all-gather.21.cloned.1.call-start = ((), (), s32[]{:S(2)}) async-start(), calls=%async_computation.8 | async-start | bytes 20971520 | tf_op jit(solution)/shard_map/all_gather | solution.py:344
  8.7 884.6 %all-gather.17.cloned.1.call-start = ((), (), s32[]{:S(2)}) async-start(), calls=%async_computation.6 | async-start | bytes 1638400 | tf_op jit(solution)/shard_map/all_gather | solution.py:340
  9.4 912.2 %all-gather.19.cloned.1.call-start = ((), (), s32[]{:S(2)}) async-start(), calls=%async_computation.7 | async-start | bytes 1310720 | tf_op jit(solution)/shard_map/all_gather | solution.py:341
  10.0 1536.1 %all-gather.25.cloned.1.call-start = ((), (), s32[]{:S(2)}) async-start(), calls=%async_computation.12 | async-start | bytes 2359296 | tf_op jit(solution)/shard_map/all_gather | solution.py:21
  26.1 16.1 copy-start.23
  26.9 15.3 copy-start.42
  42.4 551.4 %copy-start.6 = (bf16[128,2048]{1,0:T(8,128)(2,1)}, bf16[128,2048]{1,0:T(8,128)(2,1)S(1)}, u32[]{:S(2)}) copy-start(bf16[128,2048]{1,0:T(8,128)(2,1)S(1)} %fusion.39) | copy-start | bytes 1572868
  42.4 553.7 %copy-start.44 = (bf16[1024]{0:T(1024)(128)(2,1)S(1)}, bf16[1024]{0:T(1024)(128)(2,1)}, u32[]{:S(2)}) copy-start(bf16[1024]{0:T(1024)(128)(2,1)} %param.31) | copy-start | bytes 6148
  42.4 570.4 %copy-start.45 = (bf16[1024]{0:T(1024)(128)(2,1)S(1)}, bf16[1024]{0:T(1024)(128)(2,1)}, u32[]{:S(2)}) copy-start(bf16[1024]{0:T(1024)(128)(2,1)} %param.34) | copy-start | bytes 6148
  593.9 42.6 collective-permute-start
  596.0 264.8 %copy-start.29 = (f32[1,4096]{1,0:T(1,128)}, f32[1,4096]{1,0:T(1,128)S(1)}, u32[]{:S(2)}) copy-start(f32[1,4096]{1,0:T(1,128)S(1)} %get-tuple-element.1442) | copy-start | bytes 49156
  596.0 264.8 %copy-start.31 = (f32[1,4096]{1,0:T(1,128)}, f32[1,4096]{1,0:T(1,128)S(1)}, u32[]{:S(2)}) copy-start(f32[1,4096]{1,0:T(1,128)S(1)} %get-tuple-element.1443) | copy-start | bytes 49156
  596.0 264.7 %copy-start.33 = (f32[1,4096]{1,0:T(1,128)}, f32[1,4096]{1,0:T(1,128)S(1)}, u32[]{:S(2)}) copy-start(f32[1,4096]{1,0:T(1,128)S(1)} %get-tuple-element.1444) | copy-start | bytes 49156
  596.0 264.7 %copy-start.35 = (f32[1,4096]{1,0:T(1,128)}, f32[1,4096]{1,0:T(1,128)S(1)}, u32[]{:S(2)}) copy-start(f32[1,4096]{1,0:T(1,128)S(1)} %get-tuple-element.1445) | copy-start | bytes 49156
  636.5 224.3 %copy-start.14 = (bf16[1,128,2048]{2,1,0:T(8,128)(2,1)S(1)}, bf16[1,128,2048]{2,1,0:T(8,128)(2,1)}, u32[]{:S(2)}) copy-start(bf16[1,128,2048]{2,1,0:T(8,128)(2,1)} %param.37) | copy-start | bytes 1572868
  637.8 238.0 %copy-start.53 = (f32[128]{0:T(128)}, f32[128]{0:T(128)S(1)}, u32[]{:S(2)}) copy-start(f32[128]{0:T(128)S(1)} %get-tuple-element.1446) | copy-start | bytes 1540
  637.8 238.0 %copy-start.55 = (f32[128]{0:T(128)}, f32[128]{0:T(128)S(1)}, u32[]{:S(2)}) copy-start(f32[128]{0:T(128)S(1)} %get-tuple-element.1448) | copy-start | bytes 1540
  1235.7 310.4 %all-gather.27.cloned.1.call-start = ((), (), s32[]{:S(2)}) async-start(), calls=%async_computation.13 | async-start | bytes 2359296 | tf_op jit(solution)/shard_map/all_gather | solution.py:21
  1236.3 1164.5 %all-gather.29.cloned.1.call-start = ((), (), s32[]{:S(2)}) async-start(), calls=%async_computation.14 | async-start | bytes 2359296 | tf_op jit(solution)/shard_map/all_gather | solution.py:21
  1544.3 2109.8 %all-gather.31.cloned.1.call-start = ((), (), s32[]{:S(2)}) async-start(), calls=%async_computation.15 | async-start | bytes 2621440 | tf_op jit(solution)/shard_map/all_gather | solution.py:371
  1545.0 2116.8 %all-gather.23.cloned.1.call-start = ((), (), s32[]{:S(2)}) async-start(), calls=%async_computation.9 | async-start | bytes 2621440 | tf_op jit(solution)/shard_map/all_gather | solution.py:370
  1545.8 2188.4 %reduce-scatter.8.cloned.1.call-start = ((), (), s32[]{:S(2)}) async-start(), calls=%async_computation.11 | async-start | bytes 2621440 | tf_op jit(solution)/shard_map/reduce_scatter | solution.py:384
  3539.1 5.8 copy-start.50
  3544.9 18.4 copy-start.17
  3546.7 187.5 %reduce-scatter.6.cloned.1.call-start = ((), (), s32[]{:S(2)}) async-start(), calls=%async_computation.10 | async-start | bytes 3276800 | tf_op jit(solution)/shard_map/reduce_scatter | solution.py:383
  3561.7 2.1 copy-start.16
  3561.7 2.1 copy-start.26
  3561.7 2.2 copy-start.30
  3561.7 2.2 copy-start.32
  3561.7 2.2 copy-start.34
  3561.7 2.2 copy-start.36
  3561.7 2.2 copy-start.51
  3561.7 2.2 copy-start.54
  3561.7 2.2 copy-start.56
  3572.9 2.0 copy-start.1
  3572.9 2.7 copy-start.2
  3575.6 19.0 collective-permute-start.1
  3590.3 55.1 %all-to-all-start.1 = ((bf16[128,4,1024]{2,0,1:T(8,128)(2,1)}), bf16[128,4,1024]{2,0,1:T(8,128)(2,1)}, u32[]{:S(2)}, u32[]{:S(2)}) async-start(bf16[128,4,1024]{2,0,1:T(8,128)(2,1)} %bitcast.261), calls=%async_computation.3 | async-start | bytes 2097152 | tf_op jit(solution)/shard_map/all_to_all | solution.py:367
  3599.2 50.8 %copy-start.57 = (u32[32]{0:T(128)S(1)}, u32[32]{0:T(128)}, u32[]{:S(2)}) copy-start(u32[32]{0:T(128)} %constant.320) | copy-start | bytes 388
  3599.3 52.7 %copy-start.37 = (f32[4096]{0:T(1024)S(1)}, f32[4096]{0:T(1024)}, u32[]{:S(2)}) copy-start(f32[4096]{0:T(1024)} %get-tuple-element.1236) | copy-start | bytes 49156
  3599.3 52.7 %copy-start.38 = (f32[4096]{0:T(1024)S(1)}, f32[4096]{0:T(1024)}, u32[]{:S(2)}) copy-start(f32[4096]{0:T(1024)} %get-tuple-element.1237) | copy-start | bytes 49156
  3599.3 52.7 %copy-start.39 = (f32[4096]{0:T(1024)S(1)}, f32[4096]{0:T(1024)}, u32[]{:S(2)}) copy-start(f32[4096]{0:T(1024)} %get-tuple-element.1238) | copy-start | bytes 49156
  3599.3 52.7 %copy-start.40 = (f32[4096]{0:T(1024)S(1)}, f32[4096]{0:T(1024)}, u32[]{:S(2)}) copy-start(f32[4096]{0:T(1024)} %get-tuple-element.1239) | copy-start | bytes 49156
  3645.3 75.9 %all-to-all-start = ((bf16[128,4,2048]{2,0,1:T(8,128)(2,1)}), bf16[128,4,2048]{2,0,1:T(8,128)(2,1)}, u32[]{:S(2)}, u32[]{:S(2)}) async-start(bf16[128,4,2048]{2,0,1:T(8,128)(2,1)} %pad_maximum_fusion), calls=%async_computation | async-start | bytes 4194304 | tf_op jit(solution)/shard_map/all_to_all | solution.py:366
  3649.8 836.5 %reduce-scatter.10.cloned.1.call-start = ((), (), s32[]{:S(2)}) async-start(), calls=%async_computation.16 | async-start | bytes 2621440
  3654.1 858.8 %all-reduce.21.cloned.1.call-start = ((), (), s32[]{:S(2)}) async-start(), calls=%async_computation.17 | async-start | bytes 52690944 | tf_op jit(solution)/shard_map/psum | solution.py:388
  3735.8 708.4 %copy-start.8 = (bf16[1,128,2048]{2,1,0:T(8,128)(2,1)S(1)}, bf16[1,128,2048]{2,1,0:T(8,128)(2,1)}, u32[]{:S(2)}) copy-start(bf16[1,128,2048]{2,1,0:T(8,128)(2,1)} %param.26) | copy-start | bytes 1572868
  4444.3 10.6 copy-start.13
  4444.3 10.6 copy-start.24
  4444.3 10.6 copy-start.43
  4454.8 13.2 copy-start.25
  4454.9 13.2 copy-start.27
  4454.9 13.2 copy-start.28
  4454.9 30.2 copy-start.49
  4454.9 30.3 copy-start.15
  4512.8 15.1 slice-start
  4512.8 13.5 copy-start.18
  4512.8 14.3 copy-start.19
  4512.8 15.1 slice-start.1
  (13 other events, 13.6 us)
Sparse Core Ops, SparseCore 0:
  9.6 564.3 all-gather.14
  575.5 285.1 all-gather.20
  862.3 30.8 all-gather.16
  894.7 26.9 all-gather.18
  1235.9 27.3 all-gather.24
  1265.6 27.9 all-gather.26
  1544.4 27.4 all-gather.28
  1573.4 45.9 all-gather.30
  1621.6 45.0 all-gather.22
  3546.8 43.4 reduce-scatter.7
  3592.7 82.3 reduce-scatter.5
  3677.3 66.1 reduce-scatter.9
  3749.0 321.8 all-reduce.20
where the time goes:
time: 4600 us; the launch traced here: 4540 us
  local copies, waits for them, and re-layouts  1680 us (37%)
  other arithmetic  1680 us (37%)
  waiting for transfers between devices  904 us (20%)
  blocking collectives  123 us (3%)
  matrix products  99.2 us (2%)
    dynamic_update_slice x768, local copies, waits for them, and re-layouts, blocked_scan(): return lax.scan(state_step, state_now, inputs)  833 us
    dynamic_slice x896, local copies, waits for them, and re-layouts, block_summary(): lax.scan(summary_step, start, (keep_mask, rate_vec, conv_vals, key_vec))  621 us
    all_gather x1, waiting for transfers between devices, on_device(): lax.all_gather(in_weight, 'wt', axis=0, tiled=True)  532 us
    dynamic_update_slice x384, other arithmetic, blocked_scan(): return lax.scan(state_step, state_now, inputs)  412 us
    reduce_sum x128, other arithmetic, state_step(): decay = 1.0 - key_now[:, None] * key_now[:, None] * rate_now[None, :]  281 us
    dynamic_slice x256, other arithmetic, block_summary(): lax.scan(summary_step, start, (keep_mask, rate_vec, conv_vals, key_vec))  256 us
    all_gather x1, waiting for transfers between devices, on_device(): lax.all_gather(out_weight, 'wt', axis=0, tiled=True)  220 us
    reduce_sum x256, other arithmetic, state_step(): return (state_now, jnp.sum(query_now[:, None] * state_now, axis=0))  134 us

commit v1 on v0

v1 whole, which is shorter than its diff:
```python
import jax
import jax.numpy as jnp
from jax import lax
from jax.experimental import pallas as pl
from jax.experimental.pallas import tpu as pltpu
from jax.sharding import PartitionSpec as P

STATE = 16
KERNEL = 4
HALO = KERNEL - 1
GROUP = 8
LANES = 128
PACKET = 16
EPS = 1e-05
F32 = jnp.float32
BF16 = jnp.bfloat16


def circular(value, axis, steps):
    count = lax.axis_size(axis)
    return lax.ppermute(value, axis, [(i, (i + steps) % count) for i in range(count)])


def small_gather(value, axis):
    return [value] + [circular(value, axis, k) for k in range(1, lax.axis_size(axis))]


def in_order(parts, axis):
    count, mine = lax.axis_size(axis), lax.axis_index(axis)
    out = jnp.zeros((count,) + parts[0].shape, parts[0].dtype)
    for k, part in enumerate(parts):
        out = lax.dynamic_update_index_in_dim(out, part, (mine - k) % count, 0)
    return out


def line_gather(value, axis):
    count, mine = lax.axis_size(axis), lax.axis_index(axis)
    up, down = [value], [value]
    for m in range(1, count):
        up.append(lax.ppermute(up[-1], axis, [(i, i + 1) for i in range(m - 1, count - 1)]))
        down.append(lax.ppermute(down[-1], axis, [(i, i - 1) for i in range(1, count - m + 1)]))
    return [value] + [jnp.where(mine >= k, up[k], down[count - k]) for k in range(1, count)]


def line_scatter(terms, axis):
    count, mine = lax.axis_size(axis), lax.axis_index(axis)
    parts = [lax.dynamic_index_in_dim(terms, (mine - k) % count, 0, keepdims=False) for k in range(count)]
    up = down = None
    for m in range(1, count):
        to_up = parts[m] if up is None else parts[m] + up.astype(F32)
        to_down = parts[count - m] if down is None else parts[count - m] + down.astype(F32)
        up = lax.ppermute(to_up.astype(BF16), axis, [(i, i + 1) for i in range(m)])
        down = lax.ppermute(to_down.astype(BF16), axis, [(i, i - 1) for i in range(count - m, count)])
    return parts[0] + up.astype(F32) + down.astype(F32)


def all_sum(value, axis):
    count = lax.axis_size(axis)
    bit = 1
    while bit < count:
        value = value + lax.ppermute(value, axis, [(i, i ^ bit) for i in range(count)])
        bit *= 2
    return value


def shifted(value, axis, steps):
    count = lax.axis_size(axis)
    leading, last = (max(0, -steps), min(count, count - steps))
    return lax.ppermute(value, axis, [(source, source + steps) for source in range(leading, last)])


def to_users(slots, axis):
    count, mine = lax.axis_size(axis), lax.axis_index(axis)
    half = count // 2
    first = lax.ppermute(
        jnp.where(mine < half, slots[0], slots[1]),
        axis,
        [(j, 2 * j if j < half else (2 * j + 1) % count) for j in range(count)],
    )
    second = lax.ppermute(
        jnp.where(mine < half, slots[1], slots[0]),
        axis,
        [(j, 2 * j + 1 if j < half else (2 * j) % count) for j in range(count)],
    )
    even = mine % 2 == 0
    return jnp.where(even, first, second), jnp.where(even, second, first)


def to_owners(block, axis, offset):
    count = lax.axis_size(axis)
    return [
        lax.ppermute(block, axis, [(w, offset + w // 2) for w in range(slot, count, 2)])
        for slot in range(2)
    ]


def tiles_of(width):
    return [pl.ds(at * LANES, LANES) for at in range(width // LANES)]


def row_sums(parts):
    row = lax.broadcasted_iota(jnp.int32, (GROUP, LANES), 0)
    low4, low2, low1 = row < 4, (row & 2) == 0, (row & 1) == 0
    fours = [
        jnp.where(low4, parts[j], parts[j + 4])
        + pltpu.roll(jnp.where(low4, parts[j + 4], parts[j]), 4, 0)
        for j in range(4)
    ]
    twos = [
        jnp.where(low2, fours[j] + pltpu.roll(fours[j], 6, 0), fours[j + 2] + pltpu.roll(fours[j + 2], 2, 0))
        for j in range(2)
    ]
    return jnp.where(low1, twos[0] + pltpu.roll(twos[0], 7, 0), twos[1] + pltpu.roll(twos[1], 1, 0))


def lane_sums(lanes_ref):
    ones = jnp.ones((GROUP, LANES), F32)
    return lax.dot_general(
        ones, lanes_ref[...], (((1,), (1,)), ((), ())), precision=lax.Precision.HIGHEST, preferred_element_type=F32
    )


def summary_kernel(key_ref, query_ref, keep_ref, rate_ref, feed_ref, grad_ref, decay_ref, state_ref, adjoint_ref):
    steps, width = rate_ref.shape
    tiles = tiles_of(width)
    keep0, key0 = keep_ref[...], key_ref[...]

    def body(i, carry):
        key, square, query, keep, decay, state, adjoint = carry
        decay, state, adjoint = list(decay), list(state), list(adjoint)
        rows = pl.ds(pl.multiple_of(i * GROUP, GROUP), GROUP)
        rate = [rate_ref[rows, tile] for tile in tiles]
        feed = [feed_ref[rows, tile] for tile in tiles]
        grad = [grad_ref[rows, tile] for tile in tiles]
        for j in range(GROUP):
            key_now, square_now = key[:, j : j + 1], square[:, j : j + 1]
            query_now, keep_now = query[:, j : j + 1], keep[:, j : j + 1]
            for at in range(len(tiles)):
                factor = keep_now - square_now * rate[at][j : j + 1]
                state[at] = factor * state[at] + key_now * feed[at][j : j + 1]
                decay[at] = factor * decay[at]
                adjoint[at] = adjoint[at] + decay[at] * (query_now * grad[at][j : j + 1])
        key, square, query, keep = (pltpu.roll(part, steps - GROUP, 1) for part in (key, square, query, keep))
        return key, square, query, keep, tuple(decay), tuple(state), tuple(adjoint)

    zero = jnp.zeros((STATE, LANES), F32)
    count = len(tiles)
    start = (key0, keep0 * key0 * key0, query_ref[...], keep0, (zero + 1.0,) * count, (zero,) * count, (zero,) * count)
    _, _, _, _, decay, state, adjoint = lax.fori_loop(0, steps // GROUP, body, start)
    for at, tile in enumerate(tiles):
        decay_ref[0, :, tile] = decay[at].astype(decay_ref.dtype)
        state_ref[0, :, tile] = state[at].astype(state_ref.dtype)
        adjoint_ref[0, :, tile] = adjoint[at].astype(adjoint_ref.dtype)


def forward_kernel(key_ref, query_ref, keep_ref, rate_ref, feed_ref, grad_ref, start_ref, out_ref, before_ref, dquery_ref, lanes_ref):
    steps, width = rate_ref.shape
    tiles = tiles_of(width)
    keep0, key0 = keep_ref[...], key_ref[...]

    def body(i, carry):
        key, square, query, keep, state = carry
        state = list(state)
        base = pl.multiple_of(i * GROUP, GROUP)
        rows = pl.ds(base, GROUP)
        rate = [rate_ref[rows, tile] for tile in tiles]
        feed = [feed_ref[rows, tile] for tile in tiles]
        grad = [grad_ref[rows, tile] for tile in tiles]
        weighed = [[] for _ in tiles]
        for j in range(GROUP):
            key_now, square_now = key[:, j : j + 1], square[:, j : j + 1]
            query_now, keep_now = query[:, j : j + 1], keep[:, j : j + 1]
            total = None
            for at, tile in enumerate(tiles):
                before_ref[0, 0, base + j, :, tile] = state[at]
                factor = keep_now - square_now * rate[at][j : j + 1]
                state[at] = factor * state[at] + key_now * feed[at][j : j + 1]
                out = query_now * state[at]
                weighed[at].append(out[:GROUP] + out[GROUP:])
                term = grad[at][j : j + 1] * state[at]
                total = term if total is None else total + term
            lanes_ref[pl.ds(pl.multiple_of((base + j) * STATE, STATE), STATE), :] = total
        for at, tile in enumerate(tiles):
            out_ref[rows, tile] = row_sums(weighed[at])
        key, square, query, keep = (pltpu.roll(part, steps - GROUP, 1) for part in (key, square, query, keep))
        return key, square, query, keep, tuple(state)

    start = tuple(start_ref[0, :, tile] for tile in tiles)
    carry = (key0, keep0 * key0 * key0, query_ref[...], keep0, start)
    lax.fori_loop(0, steps // GROUP, body, carry)
    dquery_ref[...] = lane_sums(lanes_ref)


def backward_kernel(key_ref, query_ref, keep_ref, rate_ref, feed_ref, grad_ref, before_ref, start_ref, along_ref, across_ref, dkey_ref, lanes_ref):
    steps, width = rate_ref.shape
    tiles = tiles_of(width)
    groups = steps // GROUP
    keep0, key0 = keep_ref[...], key_ref[...]

    def body(i, carry):
        key, square, twice, query, keep, adjoint = carry
        key, square, twice, query, keep = (pltpu.roll(part, GROUP, 1) for part in (key, square, twice, query, keep))
        adjoint = list(adjoint)
        base = pl.multiple_of((groups - 1 - i) * GROUP, GROUP)
        rows = pl.ds(base, GROUP)
        rate = [rate_ref[rows, tile] for tile in tiles]
        feed = [feed_ref[rows, tile] for tile in tiles]
        grad = [grad_ref[rows, tile] for tile in tiles]
        along, across = [[None] * GROUP for _ in tiles], [[None] * GROUP for _ in tiles]
        for j in reversed(range(GROUP)):
            key_now, square_now, twice_now = key[:, j : j + 1], square[:, j : j + 1], twice[:, j : j + 1]
            query_now, keep_now = query[:, j : j + 1], keep[:, j : j + 1]
            plain = crossed = None
            for at, tile in enumerate(tiles):
                rate_now = rate[at][j : j + 1]
                full = adjoint[at] + query_now * grad[at][j : j + 1]
                product = full * before_ref[0, 0, base + j, :, tile]
                one, two = key_now * full, square_now * product
                along[at][j] = one[:GROUP] + one[GROUP:]
                across[at][j] = two[:GROUP] + two[GROUP:]
                three, four = full * feed[at][j : j + 1], product * rate_now
                plain = three if plain is None else plain + three
                crossed = four if crossed is None else crossed + four
                adjoint[at] = (keep_now - square_now * rate_now) * full
            lanes_ref[pl.ds(pl.multiple_of((base + j) * STATE, STATE), STATE), :] = plain - twice_now * crossed
        for at, tile in enumerate(tiles):
            along_ref[rows, tile] = row_sums(along[at])
            across_ref[rows, tile] = row_sums(across[at])
        return key, square, twice, query, keep, tuple(adjoint)

    start = tuple(start_ref[0, :, tile] for tile in tiles)
    carry = (
        key0,
        keep0 * key0 * key0,
        2.0 * keep0 * key0,
        query_ref[...],
        keep0,
        start,
    )
    lax.fori_loop(0, groups, body, carry)
    dkey_ref[...] = lane_sums(lanes_ref)


class Mixer:
    def __init__(self, seqs, steps, width):
        self.seqs, self.steps, self.width = seqs, steps, width
        self.part = width
        self.grid = (seqs, width // self.part)
        self.column = pl.BlockSpec((STATE, steps), lambda i, e: (0, i))
        self.row = pl.BlockSpec((steps, self.part), lambda i, e: (i, e))
        self.state = pl.BlockSpec((1, STATE, self.part), lambda i, e: (i, 0, e))
        self.states = pl.BlockSpec((1, 1, steps, STATE, self.part), lambda i, e: (i, e, 0, 0, 0))
        self.sums = pl.BlockSpec((GROUP, steps * STATE), lambda i, e: (e, i))
        self.all_sums = jax.ShapeDtypeStruct((self.grid[1] * GROUP, seqs * steps * STATE), F32)
        self.lanes = pltpu.VMEM((steps * STATE, LANES), F32)
        self.rows = jax.ShapeDtypeStruct((seqs * steps, width), F32)

    def call(self, kernel, name, in_specs, out_specs, out_shape, ops, nbytes, scratch=()):
        elements = self.seqs * self.steps * STATE * self.width
        return pl.pallas_call(
            kernel,
            grid=self.grid,
            in_specs=in_specs,
            out_specs=out_specs,
            out_shape=out_shape,
            name=name,
            scratch_shapes=scratch,
            cost_estimate=pl.CostEstimate(flops=ops * elements, bytes_accessed=nbytes, transcendentals=0),
            compiler_params=pltpu.CompilerParams(
                dimension_semantics=("arbitrary", "arbitrary"), vmem_limit_bytes=48 * 1024 * 1024
            ),
        )

    def summary(self, *args):
        shape = jax.ShapeDtypeStruct((self.seqs, STATE, self.width), F32)
        specs = [self.column] * 3 + [self.row] * 3
        nbytes = 12 * self.seqs * self.steps * self.width
        return self.call(summary_kernel, "block_summary", specs, [self.state] * 3, [shape] * 3, 11, nbytes)(*args)

    def forward(self, *args):
        states = jax.ShapeDtypeStruct((self.seqs, self.grid[1], self.steps, STATE, self.part), F32)
        specs = [self.column] * 3 + [self.row] * 3 + [self.state]
        nbytes = (16 + 4 * STATE) * self.seqs * self.steps * self.width
        return self.call(
            forward_kernel,
            "states",
            specs,
            [self.row, self.states, self.sums],
            [self.rows, states, self.all_sums],
            10,
            nbytes,
            [self.lanes],
        )(*args)

    def columns(self, sums):
        return sum(sums[at * GROUP] for at in range(self.grid[1])).reshape(-1, STATE).T

    def backward(self, *args):
        specs = [self.column] * 3 + [self.row] * 3 + [self.states, self.state]
        nbytes = (20 + 4 * STATE) * self.seqs * self.steps * self.width
        return self.call(
            backward_kernel,
            "adjoints",
            specs,
            [self.row, self.row, self.sums],
            [self.rows, self.rows, self.all_sums],
            20,
            nbytes,
            [self.lanes],
        )(*args)


def dot(left, right, over_left, over_right):
    return lax.dot_general(left, right, (((over_left,), (over_right,)), ((), ())), preferred_element_type=F32)


def inverse_rms(features):
    return lax.rsqrt(jnp.mean(features * features, axis=1, keepdims=True) + EPS)


def on_device(
    tokens,
    segment_ids,
    norm_gain,
    in_weight,
    conv_weight,
    conv_bias,
    proj_weight,
    dt_weight,
    dt_bias,
    skip_weight,
    out_weight,
    cotangent,
):
    groups, blocks = lax.axis_size("wt"), lax.axis_size("seq")
    mine, block = lax.axis_index("wt"), lax.axis_index("seq")
    own, own_cot, own_ids = tokens[0], cotangent[0], segment_ids[0] + 1
    length, model = own.shape
    width = out_weight.shape[0]
    rows = groups * length
    taps, bias32 = conv_weight.astype(F32), conv_bias.astype(F32)
    dt_bias32, skip32 = dt_bias.astype(F32), skip_weight.astype(F32)

    edge_ids = jnp.pad(own_ids[length - HALO :].astype(BF16), (0, model - HALO))
    packet = jnp.concatenate([own[length - HALO :], edge_ids[None]], axis=0)
    packet = shifted(packet, "seq", 1)
    all_ids = jnp.concatenate([packet[HALO, :HALO], own_ids.astype(BF16)])
    packet = jnp.concatenate(
        [
            packet[:HALO],
            jnp.pad(all_ids, (0, model - HALO - length))[None],
            jnp.pad(norm_gain, (0, model - norm_gain.shape[0]))[None],
            jnp.zeros((PACKET - HALO - 2, model), BF16),
        ],
        axis=0,
    )
    packets = in_order(small_gather(packet, "wt"), "wt")

    chunk = width // blocks
    slots = [
        lax.dynamic_slice_in_dim(in_weight, slot * width + block * chunk, chunk, 0) for slot in range(2)
    ]
    value_chunk, gate_chunk = to_users(slots, "wt")
    value_weight = lax.all_gather(value_chunk, "seq", axis=0, tiled=True)
    gate_weight = lax.all_gather(gate_chunk, "seq", axis=0, tiled=True)

    gathered = in_order(line_gather(own, "wt"), "wt").reshape(rows, model)
    cots = in_order(line_gather(own_cot, "wt"), "wt").reshape(rows, model)

    gain32 = packets[:, HALO + 1, : model // groups].astype(F32).reshape(model)

    features = jnp.concatenate([gathered, packets.reshape(groups * PACKET, model)], axis=0).astype(F32)
    normed_all = (features * inverse_rms(features) * gain32).astype(BF16)
    normed = normed_all[:rows]
    values_all = dot(normed_all, value_weight, 1, 1).astype(BF16)
    gate_pre = dot(normed, gate_weight, 1, 1)
    extended = jnp.concatenate(
        [
            values_all[rows:].reshape(groups, PACKET, width)[:, :HALO],
            values_all[:rows].reshape(groups, length, width),
        ],
        axis=1,
    ).astype(F32)
    ids = packets[:, HALO, : HALO + length]
    same_doc = [(ids[:, k : k + length] == ids[:, HALO:]).astype(F32)[:, :, None] for k in range(KERNEL)]
    conv_sum = bias32 + sum(taps[k] * extended[:, k : k + length] * same_doc[k] for k in range(KERNEL))
    conv_out = jax.nn.silu(conv_sum).astype(BF16).reshape(rows, width)
    conv_vals = conv_out.astype(F32)

    projected = all_sum(dot(proj_weight, conv_out, 0, 1), "wt")
    query, key = projected[:STATE], projected[STATE : 2 * STATE]
    low_rank = projected[2 * STATE :].astype(BF16)
    keep = same_doc[KERNEL - 2].reshape(1, rows)
    keeps = jnp.broadcast_to(keep, (STATE, rows))
    key_square = jnp.sum(key * key, axis=0)[:, None]
    beta_in = dot(low_rank, dt_weight, 0, 1) + dt_bias32
    beta = jax.nn.softplus(beta_in)
    shrink = 1.0 / (1.0 + beta * key_square)
    rate = beta * shrink
    feed = rate * conv_vals
    d_gated = dot(cots, out_weight, 1, 1)
    sigma = jax.nn.sigmoid(gate_pre)
    gate = gate_pre * sigma
    d_mixed = d_gated * gate

    mixer = Mixer(groups, length, width)
    summary = jnp.stack([part.astype(BF16) for part in mixer.summary(key, query, keeps, rate, feed, d_mixed)])
    everything = lax.all_gather(summary, "seq").astype(F32)
    state_in = jnp.zeros((groups, STATE, width), F32)
    grad_in = jnp.zeros((groups, STATE, width), F32)
    for at in range(blocks):
        state_in = jnp.where(at < block, everything[at, 0] * state_in + everything[at, 1], state_in)
        back = blocks - 1 - at
        grad_in = jnp.where(back > block, everything[back, 0] * grad_in + everything[back, 2], grad_in)

    core_out, before, d_query = mixer.forward(key, query, keeps, rate, feed, d_mixed, state_in)
    d_query = mixer.columns(d_query)
    mixed = core_out + skip32 * conv_vals
    gated = (mixed * gate).astype(BF16)
    d_gate = (d_gated * mixed * (sigma * (1.0 + gate_pre * (1.0 - sigma)))).astype(BF16)
    skip_part = jnp.sum(d_mixed * conv_vals, axis=0)
    out_parts = dot(gated, out_weight, 1, 0).reshape(groups, length, model)
    block_output = (own.astype(F32) + line_scatter(out_parts, "wt")).astype(BF16)
    out_share = dot(gated, cots, 0, 0)
    out_chunk = lax.psum_scatter(out_share.astype(BF16), "seq", scatter_dimension=0, tiled=True)
    gate_share = dot(d_gate, normed, 0, 0)
    gate_part = lax.psum_scatter(gate_share.astype(BF16), "seq", scatter_dimension=0, tiled=True)
    gate_slots = to_owners(gate_part, "wt", groups // 2)

    along, across, d_key = mixer.backward(key, query, keeps, rate, feed, d_mixed, before, grad_in)
    d_key = mixer.columns(d_key)
    d_rate = conv_vals * along - across
    d_beta = d_rate * shrink * shrink
    from_square = jnp.sum(d_beta * beta * beta, axis=1)
    d_key = d_key - 2.0 * key * from_square
    d_bias = d_beta * jax.nn.sigmoid(beta_in)
    dt_bias_part = jnp.sum(d_bias, axis=0)
    d_beta_low = d_bias.astype(BF16)
    d_low_rank = dot(dt_weight, d_beta_low, 0, 1)
    d_projected = all_sum(jnp.concatenate([d_query, d_key, d_low_rank], axis=0), "wt").astype(BF16)
    dt_part = dot(d_beta_low, low_rank, 0, 1)
    proj_part = dot(conv_out, d_projected, 0, 1)
    d_value = d_mixed * skip32 + rate * along + dot(d_projected, proj_weight, 0, 1)

    sigma_conv = jax.nn.sigmoid(conv_sum)
    d_conv = d_value.reshape(groups, length, width) * (sigma_conv * (1.0 + conv_sum * (1.0 - sigma_conv)))
    conv_bias_part = jnp.sum(d_conv, axis=(0, 1))
    masked = [d_conv * same_doc[k] for k in range(KERNEL)]
    conv_part = jnp.stack([jnp.sum(masked[k] * extended[:, k : k + length], axis=(0, 1)) for k in range(KERNEL)])
    d_extended = sum(
        jnp.pad(taps[k] * masked[k], ((0, 0), (k, HALO - k), (0, 0))) for k in range(KERNEL)
    )
    returned = shifted(d_extended[:, :HALO], "seq", -1)
    d_rows = d_extended[:, HALO:] + jnp.pad(returned, ((0, 0), (length - HALO, 0), (0, 0)))
    d_rows = d_rows.astype(BF16).reshape(rows, width)

    value_share = dot(d_rows, normed, 0, 0)
    value_part = lax.psum_scatter(value_share.astype(BF16), "seq", scatter_dimension=0, tiled=True)
    value_slots = to_owners(value_part, "wt", 0)
    in_chunk = jnp.stack([value_slots[slot] + gate_slots[slot] for slot in range(2)])

    d_normed_parts = (dot(d_rows, value_weight, 1, 0) + dot(d_gate, gate_weight, 1, 0)).reshape(groups, length, model)
    d_normed = line_scatter(d_normed_parts, "wt")
    own32 = own.astype(F32)
    inv_rms = inverse_rms(own32)
    weighted = d_normed * gain32
    along_features = jnp.mean(own32 * weighted, axis=1, keepdims=True)
    token_grad = (own_cot.astype(F32) + inv_rms * weighted - own32 * (inv_rms * inv_rms * inv_rms) * along_features).astype(BF16)
    gain_part = jnp.sum(d_normed * own32 * inv_rms, axis=0)
    gain_part = lax.psum_scatter(gain_part, "wt", scatter_dimension=0, tiled=True)

    gain_grad, conv_grad, conv_bias_grad, proj_grad, dt_grad, dt_bias_grad, skip_grad = lax.psum(
        (gain_part, conv_part, conv_bias_part, proj_part, dt_part, dt_bias_part, skip_part), "seq"
    )
    out_grad = lax.all_gather(out_chunk, "seq", axis=0, tiled=True).astype(F32)
    in_grad = lax.all_gather(in_chunk, "seq", axis=1, tiled=True).astype(F32).reshape(2 * width, model)
    return (
        block_output[None],
        token_grad[None],
        gain_grad,
        in_grad,
        conv_grad,
        conv_bias_grad,
        proj_grad,
        dt_grad,
        dt_bias_grad,
        skip_grad,
        out_grad,
    )


def solution(mesh):
    return jax.shard_map(
        on_device,
        mesh=mesh,
        in_specs=(
            P("wt", "seq", None),
            P("wt", "seq"),
            P("wt"),
            P("wt", None),
            P(None, "wt"),
            P("wt"),
            P("wt", None),
            P("wt", None),
            P("wt"),
            P("wt"),
            P("wt", None),
            P("wt", "seq", None),
        ),
        out_specs=(
            P("wt", "seq", None),
            P("wt", "seq", None),
            P("wt"),
            P("wt", None),
            P(None, "wt"),
            P("wt"),
            P("wt", None),
            P("wt", None),
            P("wt"),
            P("wt"),
            P("wt", None),
        ),
        check_vma=False,
    )
```

time: 4600 us -> 639 us (0.14); the launches traced: 4540 us -> 634 us
  local copies, waits for them, and re-layouts: 1680 us -> 16.3 us
  other arithmetic: 1680 us -> 65.4 us
  waiting for transfers between devices: 904 us -> 273 us
  blocking collectives: 123 us -> 39.3 us
  starting transfers between devices: 12.9 us -> 95.3 us
  Pallas kernels: 0 us -> 77.7 us
  matrix products: 99.2 us -> 50.2 us
    dynamic_update_slice x768 -> x5, local copies, waits for them, and re-layouts: 833 us -> 1.96 us  [in_order(): out = lax.dynamic_update_index_in_dim(out, part, (mine - k) % count, 0)]
    all_gather x9 -> x5, waiting for transfers between devices: 794 us -> 30.3 us  [the longest x1 30.3 us: on_device(): everything = lax.all_gather(summary, 'seq').astype(F32)]
    dynamic_slice x1024 -> x0, local copies, waits for them, and re-layouts: 716 us -> none  [the longest x896 621 us: block_summary(): lax.scan(summary_step, start, (keep_mask, rate_vec, conv_vals, key_vec))]
    mul x897 -> x3, other arithmetic: 451 us -> 1.35 us  [the longest x1 0.8 us: on_device(): taps[k] * masked[k]]
    dynamic_update_slice x384 -> x7, other arithmetic: 412 us -> 5.37 us  [in_order(): out = lax.dynamic_update_index_in_dim(out, part, (mine - k) % count, 0)]
    reduce_sum x386 -> x7, other arithmetic: 419 us -> 13.8 us  [the longest x1 5.2 us: on_device(): dt_bias_part = jnp.sum(d_bias, axis=0)]
    dynamic_slice x256 -> x0, other arithmetic: 256 us -> none  [block_summary(): lax.scan(summary_step, start, (keep_mask, rate_vec, conv_vals, key_vec))]
    ppermute x0 -> x37, waiting for transfers between devices: none -> 137 us  [the longest x4 35 us: all_sum(): lax.ppermute(value, axis, [(i, i ^ bit) for i in range(count)])]
where the time goes in v1:
time: 639 us; the launch traced here: 634 us
  waiting for transfers between devices  273 us (43%)
  starting transfers between devices  95.3 us (15%)
  Pallas kernels  77.7 us (12%)
  other arithmetic  65.4 us (10%)
  matrix products  50.2 us (8%)
  blocking collectives  39.3 us (6%)
  local copies, waits for them, and re-layouts  16.3 us (3%)
  between operations  16.3 us (3%)
    reduce_scatter x1, waiting for transfers between devices, on_device(): lax.psum_scatter(value_share.astype(BF16), 'seq', scatter_dimension=0, ti...  54.5 us
    dot_general x15, matrix products, dot(): lax.dot_general(left, right, (((over_left,), (over_right,)), ((), ())), p...  50.2 us
    reduce_scatter x1, waiting for transfers between devices, on_device(): lax.psum_scatter(gate_share.astype(BF16), 'seq', scatter_dimension=0, til...  49.8 us
    pallas_call x1, Pallas kernels, backward(): self.call(backward_kernel, 'adjoints', specs, [self.row, self.row, self.s...  36 us
    ppermute x6, starting transfers between devices, line_scatter(): up = lax.ppermute(to_up.astype(BF16), axis, [(i, i + 1) for i in range(m)])  35.7 us
    ppermute x4, waiting for transfers between devices, all_sum(): lax.ppermute(value, axis, [(i, i ^ bit) for i in range(count)])  35 us
    ppermute x6, waiting for transfers between devices, line_gather(): lax.ppermute(down[-1], axis, [(i, i - 1) for i in range(1, count - m + 1)])  31.4 us
    all_gather x1, waiting for transfers between devices, on_device(): everything = lax.all_gather(summary, 'seq').astype(F32)  30.3 us
  transfers between devices with their start and end apart: 48, of which 24 were waited for; matrix products, arithmetic and copies ran while one was open for 15% of the time, Pallas kernels for 0%

profile of v1, /device:TPU:0, one launch (start us, length us, event | category | flops | bytes accessed | tf_op | source)
XLA Modules:
  0.0 633.8 jit_solution(16265996055474549366)
XLA Ops:
  8.8 3.1 collective-permute-start.11
  12.5 13.1 %collective-permute-done.11 = bf16[128,2048]{1,0:T(8,128)(2,1)S(1)} collective-permute-done((bf16[128,2048]{1,0:T(8,128)(2,1)S(1)}, bf16[128,2048]{1,0:T(8,128)(2,1)S(1)}, u32[]{:S(2)}, u32[]{:S(2)}) %collective-permute-start.11) | collective-permute-done | bytes 524320 | tf_op jit(solution)/shard_map/ppermute | solution.py:80
  26.7 14.0 %collective-permute-start = (bf16[128,2048]{1,0:T(8,128)(2,1)S(1)}, bf16[128,2048]{1,0:T(8,128)(2,1)}, u32[]{:S(2)}, u32[]{:S(2)}) collective-permute-start(bf16[128,2048]{1,0:T(8,128)(2,1)S(1)} %bitcast.353), channel_id=1, source_target_pairs={{0,1},{1,2},{2,3},{4,5},{5,6},{6,7},{8,9},{9,10},{10,11},{12,13},{... | collective-permute-start | bytes 1572872 | tf_op jit(solution)/shard_map/ppermute | solution.py:40
  43.3 6.0 collective-permute-start.14
  51.1 1.6 broadcast.82.clone.1
  52.7 1.9 constant_dynamic-update-slice_fusion
  57.5 11.9 %collective-permute-done.7 = bf16[16,2048]{1,0:T(8,128)(2,1)S(1)} collective-permute-done((bf16[16,2048]{1,0:T(8,128)(2,1)S(1)}, bf16[16,2048]{1,0:T(8,128)(2,1)S(1)}, u32[]{:S(2)}, u32[]{:S(2)}) %collective-permute-start.7) | collective-permute-done | bytes 65568 | tf_op jit(solution)/shard_map/ppermute | solution.py:21
  70.7 4.6 collective-permute-done.8
  78.8 7.7 %collective-permute-done.2 = bf16[128,2048]{1,0:T(8,128)(2,1)S(1)} collective-permute-done((bf16[128,2048]{1,0:T(8,128)(2,1)}, bf16[128,2048]{1,0:T(8,128)(2,1)S(1)}, u32[]{:S(2)}, u32[]{:S(2)}) %collective-permute-start.2) | collective-permute-done | bytes 524320 | tf_op jit(solution)/shard_map/ppermute | solution.py:41
  89.3 9.8 %collective-permute-done.16 = bf16[128,2048]{1,0:T(8,128)(2,1)S(1)} collective-permute-done((bf16[128,2048]{1,0:T(8,128)(2,1)}, bf16[128,2048]{1,0:T(8,128)(2,1)S(1)}, u32[]{:S(2)}, u32[]{:S(2)}) %collective-permute-start.16) | collective-permute-done | bytes 524320 | tf_op jit(solution)/shard_map/ppermute | solution.py:41
  100.4 1.7 collective-permute-start.19
  102.1 8.3 %collective-permute-done.3 = bf16[128,2048]{1,0:T(8,128)(2,1)S(1)} collective-permute-done((bf16[128,2048]{1,0:T(8,128)(2,1)S(1)}, bf16[128,2048]{1,0:T(8,128)(2,1)S(1)}, u32[]{:S(2)}, u32[]{:S(2)}) %collective-permute-start.3) | collective-permute-done | bytes 524320 | tf_op jit(solution)/shard_map/ppermute | solution.py:41
  112.4 5.7 collective-permute-done.17
  120.0 2.0 fusion.2
  122.0 5.5 convolution_convert_fusion.3
  128.4 3.0 multiply_convert_fusion.2
  132.6 2.0 bitcast_dynamic-update-slice_fusion
  134.5 4.7 collective-permute-done.12
  139.6 5.3 fusion.12
  144.9 7.3 %collective-permute-done.13 = f32[160,512]{1,0:T(8,128)S(1)} collective-permute-done((f32[160,512]{1,0:T(8,128)S(1)}, f32[160,512]{1,0:T(8,128)S(1)}, u32[]{:S(2)}, u32[]{:S(2)}) %collective-permute-start.13) | collective-permute-done | bytes 327712 | tf_op jit(solution)/shard_map/ppermute | solution.py:61
  153.0 8.4 %fusion.6 = (f32[1024]{0:T(1024)}, f32[512,1024]{1,0:T(8,128)}, f32[512,1024]{1,0:T(8,128)S(1)}, f32[512,1024]{1,0:T(8,128)S(1)}, f32[512,1024]{1,0:T(8,128)}) fusion(bf16[4,128,1024]{2,1,0:T(8,128)(2,1)S(1)} %get-tuple-element.52, f32[512,1024]{1,0:T(8,128)S(1)} %fusion.12, f32[512]{0:T(512)S(1)} %get-tuple-element.78, f32[512,1024]{1,0:T(8,128)S(1)} %fusion.70, ...), kind=kOutput, calls=%fused_computation.22 | convolution fusion | flops 2157968384 | bytes 19933184 | tf_op jit(solution)/shard_map/dot_general | solution.py:314
  161.4 17.9 %block_summary.1 = (f32[4,16,1024]{2,1,0:T(8,128)S(1)}, f32[4,16,1024]{2,1,0:T(8,128)S(1)}, f32[4,16,1024]{2,1,0:T(8,128)S(1)}) custom-call(f32[16,512]{1,0:T(8,128)S(1)} %get-tuple-element.80.key_ref, f32[16,512]{1,0:T(8,128)S(1)} %get-tuple-element.79.query_ref, f32[16,512]{1,0:T(8,128)S(1)} %broadcast_in_dim.88.keep_ref, ...), custom_call_target="tpu_custom_call" | custom-call | flops 92274688 | bytes 6291456 | tf_op jit(solution)/shard_map/block_summary/pallas_call | solution.py:278
  180.6 30.3 %all-gather.15.cloned.1.call-done = bf16[24,4,16,1024]{3,2,1,0:T(8,128)(2,1)} async-done(((bf16[3,4,16,1024]{3,2,1,0:T(8,128)(2,1)}), bf16[24,4,16,1024]{3,2,1,0:T(8,128)(2,1)}) %all-gather.15.cloned.1.call-update) | async-done | bytes 3145744 | tf_op jit(solution)/shard_map/all_gather | solution.py:408
  211.0 2.7 convert.10
  214.1 23.8 %states.1 = (f32[512,1024]{1,0:T(8,128)S(1)}, f32[4,1,128,16,1024]{4,3,2,1,0:T(8,128)}, f32[8,8192]{1,0:T(8,128)S(1)}) custom-call(f32[16,512]{1,0:T(8,128)S(1)} %get-tuple-element.80.key_ref, f32[16,512]{1,0:T(8,128)S(1)} %get-tuple-element.79.query_ref, f32[16,512]{1,0:T(8,128)S(1)} %broadcast_in_dim.88.keep_ref, ...), custom_call_target="tpu_custom_call" | custom-call | flops 83886080 | bytes 41943040 | tf_op jit(solution)/shard_map/states/pallas_call | solution.py:284
  238.3 36.0 %adjoints.1 = (f32[512,1024]{1,0:T(8,128)S(1)}, f32[512,1024]{1,0:T(8,128)S(1)}, f32[8,8192]{1,0:T(8,128)S(1)}) custom-call(f32[16,512]{1,0:T(8,128)S(1)} %get-tuple-element.80.key_ref, f32[16,512]{1,0:T(8,128)S(1)} %get-tuple-element.79.query_ref, f32[16,512]{1,0:T(8,128)S(1)} %broadcast_in_dim.88.keep_ref, f32[512,1024]{1,0:T(8,128)} %copy-done.2, ...), custom_call_target="tpu_custom_call" | custom-call | flops 167772160 | bytes 44040192 | tf_op jit(solution)/shard_map/adjoints/pallas_call | solution.py:301
  274.4 5.2 fusion.78
  280.6 6.0 convolution_convert_fusion
  286.7 6.3 convolution_convert_fusion.1
  294.8 4.2 fusion.3
  300.5 1.5 collective-permute-start.26
  302.0 8.4 %collective-permute-done.26 = f32[160,512]{1,0:T(8,128)S(1)} collective-permute-done((f32[160,512]{1,0:T(8,128)S(1)}, f32[160,512]{1,0:T(8,128)S(1)}, u32[]{:S(2)}, u32[]{:S(2)}) %collective-permute-start.26) | collective-permute-done | bytes 327712 | tf_op jit(solution)/shard_map/ppermute | solution.py:61
  310.5 2.5 collective-permute-start.27
  313.0 14.6 %collective-permute-done.27 = f32[160,512]{1,0:T(8,128)S(1)} collective-permute-done((f32[160,512]{1,0:T(8,128)S(1)}, f32[160,512]{1,0:T(8,128)S(1)}, u32[]{:S(2)}, u32[]{:S(2)}) %collective-permute-start.27) | collective-permute-done | bytes 327712 | tf_op jit(solution)/shard_map/ppermute | solution.py:61
  330.4 3.0 multiply_reduce_fusion.3
  338.7 4.4 convolution_convert_fusion.2
  343.9 49.8 %reduce-scatter.6.cloned.1.call-done = bf16[128,2048]{1,0:T(8,128)(2,1)} async-done(((bf16[1024,2048]{1,0:T(8,128)(2,1)}), bf16[128,2048]{1,0:T(8,128)(2,1)}) %reduce-scatter.6.cloned.1.call-update) | async-done | bytes 524304 | tf_op jit(solution)/shard_map/reduce_scatter | solution.py:427
  394.4 54.5 %reduce-scatter.4.cloned.1.call-done = bf16[128,2048]{1,0:T(8,128)(2,1)} async-done(((bf16[1024,2048]{1,0:T(8,128)(2,1)}), bf16[128,2048]{1,0:T(8,128)(2,1)}) %reduce-scatter.4.cloned.1.call-update) | async-done | bytes 524304 | tf_op jit(solution)/shard_map/reduce_scatter | solution.py:458
  450.1 3.7 collective-permute-start.36
  453.9 1.7 collective-permute-start.35
  455.6 9.0 %collective-permute-done.37 = bf16[128,2048]{1,0:T(8,128)(2,1)S(1)} collective-permute-done((bf16[128,2048]{1,0:T(8,128)(2,1)}, bf16[128,2048]{1,0:T(8,128)(2,1)S(1)}, u32[]{:S(2)}, u32[]{:S(2)}) %collective-permute-start.37) | collective-permute-done | bytes 524320 | tf_op jit(solution)/shard_map/ppermute | solution.py:92
  468.7 5.0 fusion.83
  473.7 2.4 convolution_add_fusion
  476.3 15.2 %collective-permute-start.29 = (bf16[128,2048]{1,0:T(8,128)(2,1)S(1)}, bf16[128,2048]{1,0:T(8,128)(2,1)S(1)}, u32[]{:S(2)}, u32[]{:S(2)}) collective-permute-start(bf16[128,2048]{1,0:T(8,128)(2,1)S(1)} %get-tuple-element.60), channel_id=1, source_target_pairs={{0,1},{4,5},{8,9},{12,13},{16,17},{20,21},{24,25},{28,29}} | collective-permute-start | bytes 1572872 | tf_op jit(solution)/shard_map/ppermute | solution.py:52
  491.5 2.4 fusion.82
  494.8 1.5 collective-permute-start.20
  497.1 6.6 %collective-permute-done.29 = bf16[128,2048]{1,0:T(8,128)(2,1)S(1)} collective-permute-done((bf16[128,2048]{1,0:T(8,128)(2,1)S(1)}, bf16[128,2048]{1,0:T(8,128)(2,1)S(1)}, u32[]{:S(2)}, u32[]{:S(2)}) %collective-permute-start.29) | collective-permute-done | bytes 524320 | tf_op jit(solution)/shard_map/ppermute | solution.py:52
  503.8 4.4 collective-permute-start.30
  510.2 4.7 collective-permute-done.20
  515.1 4.5 collective-permute-start.21
  519.7 6.5 %collective-permute-done.30 = bf16[128,2048]{1,0:T(8,128)(2,1)S(1)} collective-permute-done((bf16[128,2048]{1,0:T(8,128)(2,1)S(1)}, bf16[128,2048]{1,0:T(8,128)(2,1)S(1)}, u32[]{:S(2)}, u32[]{:S(2)}) %collective-permute-start.30) | collective-permute-done | bytes 524320 | tf_op jit(solution)/shard_map/ppermute | solution.py:52
  529.2 7.4 %collective-permute-done.21 = bf16[128,2048]{1,0:T(8,128)(2,1)S(1)} collective-permute-done((bf16[128,2048]{1,0:T(8,128)(2,1)S(1)}, bf16[128,2048]{1,0:T(8,128)(2,1)S(1)}, u32[]{:S(2)}, u32[]{:S(2)}) %collective-permute-start.21) | collective-permute-done | bytes 524320 | tf_op jit(solution)/shard_map/ppermute | solution.py:52
  536.6 1.9 fusion.30
  539.3 4.9 collective-permute-start.31
  546.8 5.2 collective-permute-start.22
  552.0 2.1 fusion.27
  556.5 5.3 collective-permute-done.34
  562.4 15.7 %all-reduce.8 = f32[2048]{0:T(1024)S(1)} all-reduce(f32[2048]{0:T(1024)S(1)} %get-tuple-element.34), channel_id=3, replica_groups=mesh['seq'=8,'wt'=4] {'wt'}, use_global_device_ids=true, to_apply=%region_6.7.clone | all-reduce | flops 2048 | bytes 16384
  578.3 23.5 %all-reduce.9 = (f32[512]{0:T(512)}, f32[4,1024]{1,0:T(4,128)}, f32[1024]{0:T(1024)}, f32[1024]{0:T(1024)}, f32[1024]{0:T(1024)}) all-reduce(f32[512]{0:T(512)S(1)} %dynamic-slice.1, f32[4,1024]{1,0:T(4,128)S(1)} %pad_maximum_fusion.5, f32[1024]{0:T(1024)S(1)} %get-tuple-element.33, ...), channel_id=1, replica_groups=mesh['seq'=8,'wt'=4] {'seq'}, use_global_device_ids=true, to_apply=%region_7.8 | all-reduce | flops 7680 | bytes 61440 | tf_op jit(solution)/shard_map/psum | solution.py:472
  601.8 2.9 fusion.32
  604.8 6.7 %convert_element_type.260 = f32[1024,2048]{1,0:T(8,128)} convert(bf16[1024,2048]{1,0:T(8,128)(2,1)} %all-gather.13.cloned.1.call-done) | non-fusion elementwise | flops 2097152 | bytes 12582912 | tf_op jit(solution)/shard_map/convert_element_type | solution.py:475
  611.4 11.7 %bitcast_convert_fusion = f32[2048,2048]{1,0:T(8,128)} fusion(bf16[2,1024,2048]{2,1,0:T(8,128)(2,1)} %all-gather.11.cloned.1.call-done), kind=kLoop, calls=%fused_computation | loop fusion | flops 4194304 | bytes 25165824 | tf_op jit(solution)/shard_map/reshape | solution.py:476
  623.1 2.0 copy.52
  625.1 1.9 copy.53
  (305 shorter events, 60.0 us)
Async XLA Ops:
  7.2 124.3 %copy-start = (bf16[1024,160]{0,1:T(8,128)(2,1)S(1)}, bf16[1024,160]{0,1:T(8,128)(2,1)}, u32[]{:S(2)}) copy-start(bf16[1024,160]{0,1:T(8,128)(2,1)} %param.18) | copy-start | bytes 983044
  7.2 114.8 %all-gather.7.cloned.1.call-start = ((), (), s32[]{:S(2)}) async-start(), calls=%async_computation.3 | async-start | bytes 4718592 | tf_op jit(solution)/shard_map/all_gather | solution.py:364
  7.3 42.0 %copy-start.71 = (s32[1,128]{1,0:T(1,128)S(1)}, s32[1,128]{1,0:T(1,128)}, u32[]{:S(2)}) copy-start(s32[1,128]{1,0:T(1,128)} %param.13) | copy-start | bytes 1540
  8.8 16.8 %collective-permute-start.11 = (bf16[128,2048]{1,0:T(8,128)(2,1)S(1)}, bf16[128,2048]{1,0:T(8,128)(2,1)S(1)}, u32[]{:S(2)}, u32[]{:S(2)}) collective-permute-start(bf16[128,2048]{1,0:T(8,128)(2,1)S(1)} %get-tuple-element.54), channel_id=1, source_target_pairs={{0,1},{1,3},{2,0},{3,2},{4,5},{5,7},{6,4},{7,6},{8,9},{9,11},{10,8... | collective-permute-start | bytes 1572872 | tf_op jit(solution)/shard_map/ppermute | solution.py:80
  11.8 13.8 %collective-permute-start.10 = (bf16[128,2048]{1,0:T(8,128)(2,1)S(1)}, bf16[128,2048]{1,0:T(8,128)(2,1)S(1)}, u32[]{:S(2)}, u32[]{:S(2)}) collective-permute-start(bf16[128,2048]{1,0:T(8,128)(2,1)S(1)} %get-tuple-element.55), channel_id=1, source_target_pairs={{0,0},{1,2},{2,1},{3,3},{4,4},{5,6},{6,5},{7,7},{8,8},{9,10},{10,9... | collective-permute-start | bytes 1572872 | tf_op jit(solution)/shard_map/ppermute | solution.py:75
  26.7 112.9 %all-gather.9.cloned.1.call-start = ((), (), s32[]{:S(2)}) async-start(), calls=%async_computation.4 | async-start | bytes 4718592 | tf_op jit(solution)/shard_map/all_gather | solution.py:365
  26.7 48.6 %collective-permute-start = (bf16[128,2048]{1,0:T(8,128)(2,1)S(1)}, bf16[128,2048]{1,0:T(8,128)(2,1)}, u32[]{:S(2)}, u32[]{:S(2)}) collective-permute-start(bf16[128,2048]{1,0:T(8,128)(2,1)S(1)} %bitcast.353), channel_id=1, source_target_pairs={{0,1},{1,2},{2,3},{4,5},{5,6},{6,7},{8,9},{9,10},{10,11},{12,13},{... | collective-permute-start | bytes 1572872 | tf_op jit(solution)/shard_map/ppermute | solution.py:40
  40.7 28.7 %collective-permute-start.1 = (bf16[128,2048]{1,0:T(8,128)(2,1)S(1)}, bf16[128,2048]{1,0:T(8,128)(2,1)}, u32[]{:S(2)}, u32[]{:S(2)}) collective-permute-start(bf16[128,2048]{1,0:T(8,128)(2,1)S(1)} %bitcast.354), channel_id=1, source_target_pairs={{1,0},{2,1},{3,2},{5,4},{6,5},{7,6},{9,8},{10,9},{11,10},{13,12},{... | collective-permute-start | bytes 1572872 | tf_op jit(solution)/shard_map/ppermute | solution.py:41
  42.0 34.1 %collective-permute-start.15 = (bf16[128,2048]{1,0:T(8,128)(2,1)}, bf16[128,2048]{1,0:T(8,128)(2,1)}, u32[]{:S(2)}, u32[]{:S(2)}) collective-permute-start(bf16[128,2048]{1,0:T(8,128)(2,1)} %bitcast.24), channel_id=1, source_target_pairs={{1,0},{2,1},{3,2},{5,4},{6,5},{7,6},{9,8},{10,9},{11,10},{13,12},{... | collective-permute-start | bytes 1572872 | tf_op jit(solution)/shard_map/ppermute | solution.py:41
  43.3 34.1 %collective-permute-start.14 = (bf16[128,2048]{1,0:T(8,128)(2,1)}, bf16[128,2048]{1,0:T(8,128)(2,1)}, u32[]{:S(2)}, u32[]{:S(2)}) collective-permute-start(bf16[128,2048]{1,0:T(8,128)(2,1)} %bitcast.24), channel_id=1, source_target_pairs={{0,1},{1,2},{2,3},{4,5},{5,6},{6,7},{8,9},{9,10},{10,11},{12,13},{... | collective-permute-start | bytes 1572872 | tf_op jit(solution)/shard_map/ppermute | solution.py:40
  49.4 6.5 %collective-permute-start.6 = (bf16[4,2048]{1,0:T(4,128)(2,1)S(1)}, bf16[4,2048]{1,0:T(4,128)(2,1)S(1)}, u32[]{:S(2)}, u32[]{:S(2)}) collective-permute-start(bf16[4,2048]{1,0:T(4,128)(2,1)S(1)} %pad_maximum_fusion.4), channel_id=1, source_target_pairs={{0,4},{4,8},{8,12},{12,16},{16,20},{20,24},{24,28},{1,5},{5,9},{9,... | collective-permute-start | bytes 49160 | tf_op jit(solution)/shard_map/ppermute | solution.py:69
  55.2 72.9 %copy-start.35 = (f32[1,1024]{1,0:T(1,128)}, f32[1,1024]{1,0:T(1,128)S(1)}, u32[]{:S(2)}) copy-start(f32[1,1024]{1,0:T(1,128)S(1)} %get-tuple-element.81) | copy-start | bytes 12292
  56.1 13.3 %collective-permute-start.7 = (bf16[16,2048]{1,0:T(8,128)(2,1)S(1)}, bf16[16,2048]{1,0:T(8,128)(2,1)S(1)}, u32[]{:S(2)}, u32[]{:S(2)}) collective-permute-start(bf16[16,2048]{1,0:T(8,128)(2,1)S(1)} %maximum_maximum_fusion), channel_id=1, source_target_pairs={{0,1},{1,2},{2,3},{3,0},{4,5},{5,6},{6,7},{7,4},{8,9},{9,10},{10,1... | collective-permute-start | bytes 196616 | tf_op jit(solution)/shard_map/ppermute | solution.py:21
  57.5 153.5 %all-gather.15.cloned.1.call-start = ((), (), s32[]{:S(2)}) async-start(), calls=%async_computation.10 | async-start | bytes 3538944 | tf_op jit(solution)/shard_map/all_gather | solution.py:408
  69.4 5.9 collective-permute-start.8
  69.4 17.1 %collective-permute-start.2 = (bf16[128,2048]{1,0:T(8,128)(2,1)}, bf16[128,2048]{1,0:T(8,128)(2,1)S(1)}, u32[]{:S(2)}, u32[]{:S(2)}) collective-permute-start(bf16[128,2048]{1,0:T(8,128)(2,1)} %collective-permute-done.1), channel_id=1, source_target_pairs={{1,0},{2,1},{5,4},{6,5},{9,8},{10,9},{13,12},{14,13},{17,16},{18,1... | collective-permute-start | bytes 1572872 | tf_op jit(solution)/shard_map/ppermute | solution.py:41
  75.3 12.6 %collective-permute-start.9 = (bf16[16,2048]{1,0:T(8,128)(2,1)S(1)}, bf16[16,2048]{1,0:T(8,128)(2,1)S(1)}, u32[]{:S(2)}, u32[]{:S(2)}) collective-permute-start(bf16[16,2048]{1,0:T(8,128)(2,1)S(1)} %maximum_maximum_fusion), channel_id=1, source_target_pairs={{0,3},{1,0},{2,1},{3,2},{4,7},{5,4},{6,5},{7,6},{8,11},{9,8},{10,9... | collective-permute-start | bytes 196616 | tf_op jit(solution)/shard_map/ppermute | solution.py:21
  75.4 13.3 %collective-permute-start.4 = (bf16[128,2048]{1,0:T(8,128)(2,1)}, bf16[128,2048]{1,0:T(8,128)(2,1)S(1)}, u32[]{:S(2)}, u32[]{:S(2)}) collective-permute-start(bf16[128,2048]{1,0:T(8,128)(2,1)} %collective-permute-done), channel_id=1, source_target_pairs={{1,2},{2,3},{5,6},{6,7},{9,10},{10,11},{13,14},{14,15},{17,18},{18... | collective-permute-start | bytes 1572872 | tf_op jit(solution)/shard_map/ppermute | solution.py:40
  76.1 23.1 %collective-permute-start.16 = (bf16[128,2048]{1,0:T(8,128)(2,1)}, bf16[128,2048]{1,0:T(8,128)(2,1)S(1)}, u32[]{:S(2)}, u32[]{:S(2)}) collective-permute-start(bf16[128,2048]{1,0:T(8,128)(2,1)} %collective-permute-done.15), channel_id=1, source_target_pairs={{1,0},{2,1},{5,4},{6,5},{9,8},{10,9},{13,12},{14,13},{17,16},{18,1... | collective-permute-start | bytes 1572872 | tf_op jit(solution)/shard_map/ppermute | solution.py:41
  77.4 23.0 %collective-permute-start.18 = (bf16[128,2048]{1,0:T(8,128)(2,1)}, bf16[128,2048]{1,0:T(8,128)(2,1)}, u32[]{:S(2)}, u32[]{:S(2)}) collective-permute-start(bf16[128,2048]{1,0:T(8,128)(2,1)} %collective-permute-done.14), channel_id=1, source_target_pairs={{1,2},{2,3},{5,6},{6,7},{9,10},{10,11},{13,14},{14,15},{17,18},{18... | collective-permute-start | bytes 1572872 | tf_op jit(solution)/shard_map/ppermute | solution.py:40
  86.5 23.9 %collective-permute-start.3 = (bf16[128,2048]{1,0:T(8,128)(2,1)S(1)}, bf16[128,2048]{1,0:T(8,128)(2,1)S(1)}, u32[]{:S(2)}, u32[]{:S(2)}) collective-permute-start(bf16[128,2048]{1,0:T(8,128)(2,1)S(1)} %collective-permute-done.2), channel_id=1, source_target_pairs={{1,0},{5,4},{9,8},{13,12},{17,16},{21,20},{25,24},{29,28}} | collective-permute-start | bytes 1572872 | tf_op jit(solution)/shard_map/ppermute | solution.py:41
  88.6 22.0 %collective-permute-start.5 = (bf16[128,2048]{1,0:T(8,128)(2,1)S(1)}, bf16[128,2048]{1,0:T(8,128)(2,1)S(1)}, u32[]{:S(2)}, u32[]{:S(2)}) collective-permute-start(bf16[128,2048]{1,0:T(8,128)(2,1)S(1)} %collective-permute-done.4), channel_id=1, source_target_pairs={{2,3},{6,7},{10,11},{14,15},{18,19},{22,23},{26,27},{30,31}} | collective-permute-start | bytes 1572872 | tf_op jit(solution)/shard_map/ppermute | solution.py:40
  99.1 19.0 %collective-permute-start.17 = (bf16[128,2048]{1,0:T(8,128)(2,1)S(1)}, bf16[128,2048]{1,0:T(8,128)(2,1)S(1)}, u32[]{:S(2)}, u32[]{:S(2)}) collective-permute-start(bf16[128,2048]{1,0:T(8,128)(2,1)S(1)} %collective-permute-done.16), channel_id=1, source_target_pairs={{1,0},{5,4},{9,8},{13,12},{17,16},{21,20},{25,24},{29,28}} | collective-permute-start | bytes 1572872 | tf_op jit(solution)/shard_map/ppermute | solution.py:41
  100.4 32.1 %collective-permute-start.19 = (bf16[128,2048]{1,0:T(8,128)(2,1)}, bf16[128,2048]{1,0:T(8,128)(2,1)}, u32[]{:S(2)}, u32[]{:S(2)}) collective-permute-start(bf16[128,2048]{1,0:T(8,128)(2,1)} %collective-permute-done.18), channel_id=1, source_target_pairs={{2,3},{6,7},{10,11},{14,15},{18,19},{22,23},{26,27},{30,31}} | collective-permute-start | bytes 1572872 | tf_op jit(solution)/shard_map/ppermute | solution.py:40
  131.9 7.3 %collective-permute-start.12 = (f32[160,512]{1,0:T(8,128)S(1)}, f32[160,512]{1,0:T(8,128)S(1)}, u32[]{:S(2)}, u32[]{:S(2)}) collective-permute-start(f32[160,512]{1,0:T(8,128)S(1)} %convolution_bitcast_fusion), channel_id=1, source_target_pairs={{0,1},{1,0},{2,3},{3,2},{4,5},{5,4},{6,7},{7,6},{8,9},{9,8},{10,11... | collective-permute-start | bytes 983048 | tf_op jit(solution)/shard_map/ppermute | solution.py:61
  139.3 13.0 %collective-permute-start.13 = (f32[160,512]{1,0:T(8,128)S(1)}, f32[160,512]{1,0:T(8,128)S(1)}, u32[]{:S(2)}, u32[]{:S(2)}) collective-permute-start(f32[160,512]{1,0:T(8,128)S(1)} %add.346), channel_id=1, source_target_pairs={{0,2},{1,3},{2,0},{3,1},{4,6},{5,7},{6,4},{7,5},{8,10},{9,11},{10,... | collective-permute-start | bytes 983048 | tf_op jit(solution)/shard_map/ppermute | solution.py:61
  161.4 52.7 %copy-start.2 = (f32[512,1024]{1,0:T(8,128)}, f32[512,1024]{1,0:T(8,128)S(1)}, u32[]{:S(2)}) copy-start(f32[512,1024]{1,0:T(8,128)S(1)} %get-tuple-element.73.rate_ref) | copy-start | bytes 6291460
  180.3 162.9 %reduce-scatter.8.cloned.1.call-start = ((), (), s32[]{:S(2)}) async-start(), calls=%async_computation.8 | async-start | bytes 4718592 | tf_op jit(solution)/shard_map/reduce_scatter | solution.py:425
  238.3 36.1 %copy-start.9 = (f32[512,1024]{1,0:T(8,128)S(1)}, f32[512,1024]{1,0:T(8,128)}, u32[]{:S(2)}) copy-start(f32[512,1024]{1,0:T(8,128)} %copy-done.8) | copy-start | bytes 6291460
  238.3 36.1 %copy-start.11 = (bf16[4,128,1024]{2,1,0:T(8,128)(2,1)S(1)}, bf16[4,128,1024]{2,1,0:T(8,128)(2,1)}, u32[]{:S(2)}) copy-start(bf16[4,128,1024]{2,1,0:T(8,128)(2,1)} %copy-done.10) | copy-start | bytes 3145732
  238.3 36.1 %copy-start.24 = (f32[512,1024]{1,0:T(8,128)S(1)}, f32[512,1024]{1,0:T(8,128)}, u32[]{:S(2)}) copy-start(f32[512,1024]{1,0:T(8,128)} %copy-done.23) | copy-start | bytes 6291460
  238.3 36.1 %copy-start.25 = (f32[512,1024]{1,0:T(8,128)S(1)}, f32[512,1024]{1,0:T(8,128)}, u32[]{:S(2)}) copy-start(f32[512,1024]{1,0:T(8,128)} %get-tuple-element.94) | copy-start | bytes 6291460
  238.3 36.1 %copy-start.59 = (f32[512]{0:T(512)S(1)}, f32[512]{0:T(512)}, u32[]{:S(2)}) copy-start(f32[512]{0:T(512)} %copy-done.58) | copy-start | bytes 6148
  286.6 107.0 %reduce-scatter.6.cloned.1.call-start = ((), (), s32[]{:S(2)}) async-start(), calls=%async_computation.6 | async-start | bytes 4718592 | tf_op jit(solution)/shard_map/reduce_scatter | solution.py:427
  293.0 155.8 %reduce-scatter.4.cloned.1.call-start = ((), (), s32[]{:S(2)}) async-start(), calls=%async_computation.5 | async-start | bytes 4718592 | tf_op jit(solution)/shard_map/reduce_scatter | solution.py:458
  294.8 32.8 %copy-start.7 = (f32[512,1024]{1,0:T(8,128)S(1)}, f32[512,1024]{1,0:T(8,128)}, u32[]{:S(2)}) copy-start(f32[512,1024]{1,0:T(8,128)} %get-tuple-element.44.grad_ref) | copy-start | bytes 6291460
  299.0 28.6 %copy-start.3 = (f32[512,1024]{1,0:T(8,128)S(1)}, f32[512,1024]{1,0:T(8,128)}, u32[]{:S(2)}) copy-start(f32[512,1024]{1,0:T(8,128)} %copy-done.2) | copy-start | bytes 6291460
  300.5 9.9 %collective-permute-start.26 = (f32[160,512]{1,0:T(8,128)S(1)}, f32[160,512]{1,0:T(8,128)S(1)}, u32[]{:S(2)}, u32[]{:S(2)}) collective-permute-start(f32[160,512]{1,0:T(8,128)S(1)} %pad_maximum_fusion.3), channel_id=1, source_target_pairs={{0,1},{1,0},{2,3},{3,2},{4,5},{5,4},{6,7},{7,6},{8,9},{9,8},{10,11... | collective-permute-start | bytes 983048 | tf_op jit(solution)/shard_map/ppermute | solution.py:61
  310.5 17.1 %collective-permute-start.27 = (f32[160,512]{1,0:T(8,128)S(1)}, f32[160,512]{1,0:T(8,128)S(1)}, u32[]{:S(2)}, u32[]{:S(2)}) collective-permute-start(f32[160,512]{1,0:T(8,128)S(1)} %fusion.76), channel_id=1, source_target_pairs={{0,2},{1,3},{2,0},{3,1},{4,6},{5,7},{6,4},{7,5},{8,10},{9,11},{10,... | collective-permute-start | bytes 983048 | tf_op jit(solution)/shard_map/ppermute | solution.py:61
  334.2 3.1 collective-permute-start.28
  343.1 261.7 %all-gather.13.cloned.1.call-start = ((), (), s32[]{:S(2)}) async-start(), calls=%async_computation.9 | async-start | bytes 4718592 | tf_op jit(solution)/shard_map/all_gather | solution.py:475
  343.9 267.6 %all-gather.11.cloned.1.call-start = ((), (), s32[]{:S(2)}) async-start(), calls=%async_computation.7 | async-start | bytes 9437184 | tf_op jit(solution)/shard_map/all_gather | solution.py:476
  393.7 61.9 %collective-permute-start.38 = (bf16[128,2048]{1,0:T(8,128)(2,1)}, bf16[128,2048]{1,0:T(8,128)(2,1)S(1)}, u32[]{:S(2)}, u32[]{:S(2)}) collective-permute-start(bf16[128,2048]{1,0:T(8,128)(2,1)} %reduce-scatter.6.cloned.1.call-done), channel_id=1, source_target_pairs={{1,2},{3,3},{5,6},{7,7},{9,10},{11,11},{13,14},{15,15},{17,18},{19... | collective-permute-start | bytes 1572872 | tf_op jit(solution)/shard_map/ppermute | solution.py:92
  448.8 15.7 %collective-permute-start.37 = (bf16[128,2048]{1,0:T(8,128)(2,1)}, bf16[128,2048]{1,0:T(8,128)(2,1)S(1)}, u32[]{:S(2)}, u32[]{:S(2)}) collective-permute-start(bf16[128,2048]{1,0:T(8,128)(2,1)} %reduce-scatter.4.cloned.1.call-done), channel_id=1, source_target_pairs={{1,0},{3,1},{5,4},{7,5},{9,8},{11,9},{13,12},{15,13},{17,16},{19,1... | collective-permute-start | bytes 1572872 | tf_op jit(solution)/shard_map/ppermute | solution.py:92
  450.1 15.2 %collective-permute-start.36 = (bf16[128,2048]{1,0:T(8,128)(2,1)}, bf16[128,2048]{1,0:T(8,128)(2,1)S(1)}, u32[]{:S(2)}, u32[]{:S(2)}) collective-permute-start(bf16[128,2048]{1,0:T(8,128)(2,1)} %reduce-scatter.6.cloned.1.call-done), channel_id=1, source_target_pairs={{0,2},{2,3},{4,6},{6,7},{8,10},{10,11},{12,14},{14,15},{16,18},{18... | collective-permute-start | bytes 1572872 | tf_op jit(solution)/shard_map/ppermute | solution.py:92
  453.9 11.4 %collective-permute-start.35 = (bf16[128,2048]{1,0:T(8,128)(2,1)}, bf16[128,2048]{1,0:T(8,128)(2,1)S(1)}, u32[]{:S(2)}, u32[]{:S(2)}) collective-permute-start(bf16[128,2048]{1,0:T(8,128)(2,1)} %reduce-scatter.4.cloned.1.call-done), channel_id=1, source_target_pairs={{0,0},{2,1},{4,4},{6,5},{8,8},{10,9},{12,12},{14,13},{16,16},{18,1... | collective-permute-start | bytes 1572872 | tf_op jit(solution)/shard_map/ppermute | solution.py:92
  466.5 156.7 %all-reduce.13.cloned.1.call-start = ((), (), s32[]{:S(2)}) async-start(), calls=%async_computation.11 | async-start | bytes 2359296 | tf_op jit(solution)/shard_map/psum | solution.py:472
  476.1 50.0 %copy-start.14 = (f32[512,2048]{1,0:T(8,128)}, f32[512,2048]{1,0:T(8,128)S(1)}, u32[]{:S(2)}) copy-start(f32[512,2048]{1,0:T(8,128)S(1)} %convolution_add_fusion) | copy-start | bytes 12582916
  476.3 27.4 %collective-permute-start.29 = (bf16[128,2048]{1,0:T(8,128)(2,1)S(1)}, bf16[128,2048]{1,0:T(8,128)(2,1)S(1)}, u32[]{:S(2)}, u32[]{:S(2)}) collective-permute-start(bf16[128,2048]{1,0:T(8,128)(2,1)S(1)} %get-tuple-element.60), channel_id=1, source_target_pairs={{0,1},{4,5},{8,9},{12,13},{16,17},{20,21},{24,25},{28,29}} | collective-permute-start | bytes 1572872 | tf_op jit(solution)/shard_map/ppermute | solution.py:52
  494.8 20.1 %collective-permute-start.20 = (bf16[128,2048]{1,0:T(8,128)(2,1)S(1)}, bf16[128,2048]{1,0:T(8,128)(2,1)S(1)}, u32[]{:S(2)}, u32[]{:S(2)}) collective-permute-start(bf16[128,2048]{1,0:T(8,128)(2,1)S(1)} %get-tuple-element.64), channel_id=1, source_target_pairs={{0,1},{4,5},{8,9},{12,13},{16,17},{20,21},{24,25},{28,29}} | collective-permute-start | bytes 1572872 | tf_op jit(solution)/shard_map/ppermute | solution.py:52
  496.4 23.3 %collective-permute-start.32 = (bf16[128,2048]{1,0:T(8,128)(2,1)S(1)}, bf16[128,2048]{1,0:T(8,128)(2,1)S(1)}, u32[]{:S(2)}, u32[]{:S(2)}) collective-permute-start(bf16[128,2048]{1,0:T(8,128)(2,1)S(1)} %get-tuple-element.61), channel_id=1, source_target_pairs={{3,2},{7,6},{11,10},{15,14},{19,18},{23,22},{27,26},{31,30}} | collective-permute-start | bytes 1572872 | tf_op jit(solution)/shard_map/ppermute | solution.py:53
  503.8 22.3 %collective-permute-start.30 = (bf16[128,2048]{1,0:T(8,128)(2,1)S(1)}, bf16[128,2048]{1,0:T(8,128)(2,1)S(1)}, u32[]{:S(2)}, u32[]{:S(2)}) collective-permute-start(bf16[128,2048]{1,0:T(8,128)(2,1)S(1)} %fusion.23), channel_id=1, source_target_pairs={{0,1},{1,2},{4,5},{5,6},{8,9},{9,10},{12,13},{13,14},{16,17},{17,1... | collective-permute-start | bytes 1572872 | tf_op jit(solution)/shard_map/ppermute | solution.py:52
  509.5 19.7 %collective-permute-start.23 = (bf16[128,2048]{1,0:T(8,128)(2,1)}, bf16[128,2048]{1,0:T(8,128)(2,1)S(1)}, u32[]{:S(2)}, u32[]{:S(2)}) collective-permute-start(bf16[128,2048]{1,0:T(8,128)(2,1)} %get-tuple-element.65), channel_id=1, source_target_pairs={{3,2},{7,6},{11,10},{15,14},{19,18},{23,22},{27,26},{31,30}} | collective-permute-start | bytes 1572872 | tf_op jit(solution)/shard_map/ppermute | solution.py:53
  515.1 21.5 %collective-permute-start.21 = (bf16[128,2048]{1,0:T(8,128)(2,1)S(1)}, bf16[128,2048]{1,0:T(8,128)(2,1)S(1)}, u32[]{:S(2)}, u32[]{:S(2)}) collective-permute-start(bf16[128,2048]{1,0:T(8,128)(2,1)S(1)} %fusion.28), channel_id=1, source_target_pairs={{0,1},{1,2},{4,5},{5,6},{8,9},{9,10},{12,13},{13,14},{16,17},{17,1... | collective-permute-start | bytes 1572872 | tf_op jit(solution)/shard_map/ppermute | solution.py:52
  526.5 17.7 %collective-permute-start.33 = (bf16[128,2048]{1,0:T(8,128)(2,1)S(1)}, bf16[128,2048]{1,0:T(8,128)(2,1)}, u32[]{:S(2)}, u32[]{:S(2)}) collective-permute-start(bf16[128,2048]{1,0:T(8,128)(2,1)S(1)} %get-tuple-element.59), channel_id=1, source_target_pairs={{2,1},{3,2},{6,5},{7,6},{10,9},{11,10},{14,13},{15,14},{18,17},{19... | collective-permute-start | bytes 1572872 | tf_op jit(solution)/shard_map/ppermute | solution.py:53
  538.6 13.4 %collective-permute-start.24 = (bf16[128,2048]{1,0:T(8,128)(2,1)S(1)}, bf16[128,2048]{1,0:T(8,128)(2,1)S(1)}, u32[]{:S(2)}, u32[]{:S(2)}) collective-permute-start(bf16[128,2048]{1,0:T(8,128)(2,1)S(1)} %get-tuple-element.63), channel_id=1, source_target_pairs={{2,1},{3,2},{6,5},{7,6},{10,9},{11,10},{14,13},{15,14},{18,17},{19... | collective-permute-start | bytes 1572872 | tf_op jit(solution)/shard_map/ppermute | solution.py:53
  539.3 22.5 %copy-start.62 = (f32[128]{0:T(128)S(1)}, f32[128]{0:T(128)}, u32[]{:S(2)}) copy-start(f32[128]{0:T(128)} %get-tuple-element.91) | copy-start | bytes 1540
  539.3 17.2 %collective-permute-start.31 = (bf16[128,2048]{1,0:T(8,128)(2,1)S(1)}, bf16[128,2048]{1,0:T(8,128)(2,1)S(1)}, u32[]{:S(2)}, u32[]{:S(2)}) collective-permute-start(bf16[128,2048]{1,0:T(8,128)(2,1)S(1)} %get-tuple-element.58), channel_id=1, source_target_pairs={{0,1},{1,2},{2,3},{4,5},{5,6},{6,7},{8,9},{9,10},{10,11},{12,13},{... | collective-permute-start | bytes 1572872 | tf_op jit(solution)/shard_map/ppermute | solution.py:52
  545.4 16.4 %collective-permute-start.34 = (bf16[128,2048]{1,0:T(8,128)(2,1)S(1)}, bf16[128,2048]{1,0:T(8,128)(2,1)S(1)}, u32[]{:S(2)}, u32[]{:S(2)}) collective-permute-start(bf16[128,2048]{1,0:T(8,128)(2,1)S(1)} %fusion.22), channel_id=1, source_target_pairs={{1,0},{2,1},{3,2},{5,4},{6,5},{7,6},{9,8},{10,9},{11,10},{13,12},{... | collective-permute-start | bytes 1572872 | tf_op jit(solution)/shard_map/ppermute | solution.py:53
  546.8 55.1 %collective-permute-start.22 = (bf16[128,2048]{1,0:T(8,128)(2,1)S(1)}, bf16[128,2048]{1,0:T(8,128)(2,1)S(1)}, u32[]{:S(2)}, u32[]{:S(2)}) collective-permute-start(bf16[128,2048]{1,0:T(8,128)(2,1)S(1)} %get-tuple-element.62), channel_id=1, source_target_pairs={{0,1},{1,2},{2,3},{4,5},{5,6},{6,7},{8,9},{9,10},{10,11},{12,13},{... | collective-permute-start | bytes 1572872 | tf_op jit(solution)/shard_map/ppermute | solution.py:52
  554.1 24.2 %copy-start.52 = (f32[1024]{0:T(1024)S(1)}, f32[1024]{0:T(1024)}, u32[]{:S(2)}) copy-start(f32[1024]{0:T(1024)} %get-tuple-element.45) | copy-start | bytes 12292
  554.1 24.2 %copy-start.61 = (f32[1024]{0:T(1024)S(1)}, f32[1024]{0:T(1024)}, u32[]{:S(2)}) copy-start(f32[1024]{0:T(1024)} %get-tuple-element.43) | copy-start | bytes 12292
  554.1 47.7 %copy-start.67 = (f32[128]{0:T(128)S(1)}, f32[128]{0:T(128)}, u32[]{:S(2)}) copy-start(f32[128]{0:T(128)} %get-tuple-element.90) | copy-start | bytes 1540
  554.1 47.7 %collective-permute-start.25 = (bf16[128,2048]{1,0:T(8,128)(2,1)}, bf16[128,2048]{1,0:T(8,128)(2,1)S(1)}, u32[]{:S(2)}, u32[]{:S(2)}) collective-permute-start(bf16[128,2048]{1,0:T(8,128)(2,1)} %fusion.27), channel_id=1, source_target_pairs={{1,0},{2,1},{3,2},{5,4},{6,5},{7,6},{9,8},{10,9},{11,10},{13,12},{... | collective-permute-start | bytes 1572872 | tf_op jit(solution)/shard_map/ppermute | solution.py:53
  (57 other events, 374.3 us)
Sparse Core Ops, SparseCore 0:
  26.8 47.5 all-gather.6
  76.8 36.7 all-gather.8
  180.4 30.5 all-gather.14
  286.8 51.3 reduce-scatter.7
  342.3 51.3 reduce-scatter.5
  397.5 51.3 reduce-scatter.3
  450.9 36.6 all-gather.12
  489.7 54.3 all-gather.10
  548.3 57.3 all-reduce.12

commit v2 on v1

--- a/solution.py
+++ b/solution.py
@@ -1,3 +1,5 @@
+import functools
+
 import jax
 import jax.numpy as jnp
 from jax import lax
@@ -12,6 +14,8 @@
 LANES = 128
 PACKET = 16
 EPS = 1e-05
+DEPTH = 4
+VECTOR_COST = 1
 F32 = jnp.float32
 BF16 = jnp.bfloat16
 
@@ -33,34 +37,96 @@
     return out
 
 
-def line_gather(value, axis):
+def tie(*values):
+    return lax.optimization_barrier(values)
+
+
+def far_gather(value, axis):
+    pieces = {0: value}
+    for bit in bits_of(axis)[:-1]:
+        pieces.update({r | bit: across_bit(part, axis, bit) for r, part in pieces.items()})
+    del pieces[0]
+    return pieces
+
+
+def near_gather(pieces, axis):
+    return {r | 1: across_bit(part, axis, 1) for r, part in pieces.items()}
+
+
+def near_sum(kept, comes):
+    return [kept[at] + comes[at].astype(F32) for at in range(kept.shape[0])]
+
+
+def far_sum(terms, axis, sent=None, hold=lambda part: part):
+    terms = {2 * at: part for at, part in enumerate(terms)}
+    for bit in reversed(bits_of(axis)[:-1]):
+        for r in sorted(terms):
+            if r & bit:
+                part = terms.pop(r)
+                part = part.astype(BF16) if sent is None or len(terms) > 1 else sent
+                terms[r ^ bit] = terms[r ^ bit] + hold(across_bit(part, axis, bit)).astype(F32)
+    return terms[0]
+
+
+def all_sum(value, sent, axis):
+    for k in range(1, lax.axis_size(axis)):
+        value = value + circular(sent, axis, k).astype(F32)
+    return value
+
+
+def direct_scatter(terms, axis):
     count, mine = lax.axis_size(axis), lax.axis_index(axis)
-    up, down = [value], [value]
-    for m in range(1, count):
-        up.append(lax.ppermute(up[-1], axis, [(i, i + 1) for i in range(m - 1, count - 1)]))
-        down.append(lax.ppermute(down[-1], axis, [(i, i - 1) for i in range(1, count - m + 1)]))
-    return [value] + [jnp.where(mine >= k, up[k], down[count - k]) for k in range(1, count)]
-
-
-def line_scatter(terms, axis):
-    count, mine = lax.axis_size(axis), lax.axis_index(axis)
-    parts = [lax.dynamic_index_in_dim(terms, (mine - k) % count, 0, keepdims=False) for k in range(count)]
-    up = down = None
-    for m in range(1, count):
-        to_up = parts[m] if up is None else parts[m] + up.astype(F32)
-        to_down = parts[count - m] if down is None else parts[count - m] + down.astype(F32)
-        up = lax.ppermute(to_up.astype(BF16), axis, [(i, i + 1) for i in range(m)])
-        down = lax.ppermute(to_down.astype(BF16), axis, [(i, i - 1) for i in range(count - m, count)])
-    return parts[0] + up.astype(F32) + down.astype(F32)
-
-
-def all_sum(value, axis):
+    parts = [lax.dynamic_index_in_dim(terms, (mine + k) % count, 0, keepdims=False) for k in range(count)]
+    return parts[0], [circular(parts[k].astype(BF16), axis, k) for k in range(1, count)]
+
+
+def across_bit(value, axis, bit):
+    return lax.ppermute(value, axis, [(i, i ^ bit) for i in range(lax.axis_size(axis))])
+
+
+def bits_of(axis):
     count = lax.axis_size(axis)
-    bit = 1
-    while bit < count:
-        value = value + lax.ppermute(value, axis, [(i, i ^ bit) for i in range(count)])
-        bit *= 2
-    return value
+    return [count >> (at + 1) for at in range(count.bit_length() - 1)]
+
+
+def bit_gather(value, axis):
+    first, second, *rest = bits_of(axis)
+    half = value.shape[-1] // 2
+    one, two = across_bit(value, axis, first), across_bit(value, axis, second)
+    pieces = [(0, 0, value), (first, 0, one), (second, 0, two)]
+    last = [
+        (first | second, 0, across_bit(one[..., :half], axis, second)),
+        (first | second, half, across_bit(two[..., half:], axis, first)),
+    ]
+    return spread(pieces, axis), last
+
+
+def spread(pieces, axis):
+    for bit in bits_of(axis)[2:]:
+        pieces = pieces + [(index | bit, column, across_bit(part, axis, bit)) for index, column, part in pieces]
+    return pieces
+
+
+def chunk_of(index, count):
+    return (index & 1) * (count // 2) + (index >> 1)
+
+
+def bit_scatter(kept, sent, axis, first_fill, second_fill):
+    mine = lax.axis_index(axis)
+    first, second = bits_of(axis)[:2]
+    ways = ((second, first), (first, second))
+    comes, first_fill = tie([across_bit(sent[half], axis, now) for half, (now, _) in enumerate(ways)], first_fill)
+    stays, comes_last = [], []
+    for half, (_, later) in enumerate(ways):
+        terms = kept[half] + comes[half].astype(F32)
+        is_set = (mine & later) // later
+        away = lax.dynamic_index_in_dim(terms, 1 - is_set, 0, keepdims=False).astype(BF16)
+        stays.append(lax.dynamic_index_in_dim(terms, is_set, 0, keepdims=False))
+        comes_last.append(across_bit(away, axis, later))
+    second_fill = second_fill(first_fill)
+    comes_last, second_fill = tie(comes_last, second_fill)
+    halves = [stay + come.astype(F32) for stay, come in zip(stays, comes_last)]
+    return jnp.concatenate(halves, axis=-1), first_fill, second_fill
 
 
 def shifted(value, axis, steps):
@@ -120,36 +186,57 @@
     )
 
 
-def summary_kernel(key_ref, query_ref, keep_ref, rate_ref, feed_ref, grad_ref, decay_ref, state_ref, adjoint_ref):
+def summary_kernel(key_ref, keep_ref, rate_ref, feed_ref, decay_ref, state_ref):
     steps, width = rate_ref.shape
     tiles = tiles_of(width)
     keep0, key0 = keep_ref[...], key_ref[...]
 
     def body(i, carry):
-        key, square, query, keep, decay, state, adjoint = carry
-        decay, state, adjoint = list(decay), list(state), list(adjoint)
+        key, square, keep, decay, state = carry
+        decay, state = list(decay), list(state)
         rows = pl.ds(pl.multiple_of(i * GROUP, GROUP), GROUP)
         rate = [rate_ref[rows, tile] for tile in tiles]
         feed = [feed_ref[rows, tile] for tile in tiles]
-        grad = [grad_ref[rows, tile] for tile in tiles]
         for j in range(GROUP):
-            key_now, square_now = key[:, j : j + 1], square[:, j : j + 1]
-            query_now, keep_now = query[:, j : j + 1], keep[:, j : j + 1]
+            key_now, square_now, keep_now = key[:, j : j + 1], square[:, j : j + 1], keep[:, j : j + 1]
             for at in range(len(tiles)):
                 factor = keep_now - square_now * rate[at][j : j + 1]
                 state[at] = factor * state[at] + key_now * feed[at][j : j + 1]
                 decay[at] = factor * decay[at]
-                adjoint[at] = adjoint[at] + decay[at] * (query_now * grad[at][j : j + 1])
-        key, square, query, keep = (pltpu.roll(part, steps - GROUP, 1) for part in (key, square, query, keep))
-        return key, square, query, keep, tuple(decay), tuple(state), tuple(adjoint)
+        key, square, keep = (pltpu.roll(part, steps - GROUP, 1) for part in (key, square, keep))
+        return key, square, keep, tuple(decay), tuple(state)
 
     zero = jnp.zeros((STATE, LANES), F32)
-    count = len(tiles)
-    start = (key0, keep0 * key0 * key0, query_ref[...], keep0, (zero + 1.0,) * count, (zero,) * count, (zero,) * count)
-    _, _, _, _, decay, state, adjoint = lax.fori_loop(0, steps // GROUP, body, start)
+    start = (key0, keep0 * key0 * key0, keep0, (zero + 1.0,) * len(tiles), (zero,) * len(tiles))
+    _, _, _, decay, state = lax.fori_loop(0, steps // GROUP, body, start)
     for at, tile in enumerate(tiles):
         decay_ref[0, :, tile] = decay[at].astype(decay_ref.dtype)
         state_ref[0, :, tile] = state[at].astype(state_ref.dtype)
+
+
+def adjoint_summary_kernel(key_ref, query_ref, keep_ref, rate_ref, grad_ref, adjoint_ref):
+    steps, width = rate_ref.shape
+    tiles = tiles_of(width)
+    groups = steps // GROUP
+    keep0, key0 = keep_ref[...], key_ref[...]
+
+    def body(i, carry):
+        square, query, keep, adjoint = carry
+        square, query, keep = (pltpu.roll(part, GROUP, 1) for part in (square, query, keep))
+        adjoint = list(adjoint)
+        rows = pl.ds(pl.multiple_of((groups - 1 - i) * GROUP, GROUP), GROUP)
+        rate = [rate_ref[rows, tile] for tile in tiles]
+        grad = [grad_ref[rows, tile] for tile in tiles]
+        for j in reversed(range(GROUP)):
+            square_now, query_now, keep_now = square[:, j : j + 1], query[:, j : j + 1], keep[:, j : j + 1]
+            for at in range(len(tiles)):
+                full = adjoint[at] + query_now * grad[at][j : j + 1]
+                adjoint[at] = (keep_now - square_now * rate[at][j : j + 1]) * full
+        return square, query, keep, tuple(adjoint)
+
+    start = (keep0 * key0 * key0, query_ref[...], keep0, (jnp.zeros((STATE, LANES), F32),) * len(tiles))
+    adjoint = lax.fori_loop(0, groups, body, start)[-1]
+    for at, tile in enumerate(tiles):
         adjoint_ref[0, :, tile] = adjoint[at].astype(adjoint_ref.dtype)
 
 
@@ -265,17 +352,23 @@
             out_shape=out_shape,
             name=name,
             scratch_shapes=scratch,
-            cost_estimate=pl.CostEstimate(flops=ops * elements, bytes_accessed=nbytes, transcendentals=0),
+            cost_estimate=pl.CostEstimate(flops=ops * VECTOR_COST * elements, bytes_accessed=nbytes, transcendentals=0),
             compiler_params=pltpu.CompilerParams(
                 dimension_semantics=("arbitrary", "arbitrary"), vmem_limit_bytes=48 * 1024 * 1024
             ),
         )
 
     def summary(self, *args):
-        shape = jax.ShapeDtypeStruct((self.seqs, STATE, self.width), F32)
-        specs = [self.column] * 3 + [self.row] * 3
-        nbytes = 12 * self.seqs * self.steps * self.width
-        return self.call(summary_kernel, "block_summary", specs, [self.state] * 3, [shape] * 3, 11, nbytes)(*args)
+        shape = jax.ShapeDtypeStruct((self.seqs, STATE, self.width), BF16)
+        specs = [self.column] * 2 + [self.row] * 2
+        nbytes = 8 * self.seqs * self.steps * self.width
+        return self.call(summary_kernel, "block_summary", specs, [self.state] * 2, [shape] * 2, 6, nbytes)(*args)
+
+    def adjoint_summary(self, *args):
+        shape = jax.ShapeDtypeStruct((self.seqs, STATE, self.width), BF16)
+        specs = [self.column] * 3 + [self.row] * 2
+        nbytes = 8 * self.seqs * self.steps * self.width
+        return self.call(adjoint_summary_kernel, "adjoint_summary", specs, self.state, shape, 6, nbytes)(*args)
 
     def forward(self, *args):
         states = jax.ShapeDtypeStruct((self.seqs, self.grid[1], self.steps, STATE, self.part), F32)
@@ -308,6 +401,532 @@
             nbytes,
             [self.lanes],
         )(*args)
+
+
+def copies(pairs, sems):
+    moves = [pltpu.make_async_copy(source, target, sems.at[at]) for at, (source, target) in enumerate(pairs)]
+    for move in moves:
+        move.start()
+    return moves
+
+
+def place_kernel(count, number, where_ref, *refs):
+    pieces, gain_ref = refs[:number], refs[number]
+    out_ref, raw_ref, normed_ref, sems = refs[-4:]
+    gain = gain_ref[...].astype(F32)
+    rows = pieces[0].shape[0]
+    length = rows - PACKET
+    moves = []
+    for at, piece_ref in enumerate(pieces):
+        for row in range(0, rows, 3 * PACKET):
+            piece = piece_ref[row : row + 3 * PACKET, :].astype(F32)
+            inverse = lax.rsqrt(jnp.mean(piece * piece, axis=1, keepdims=True) + EPS)
+            normed_ref[at, row : row + 3 * PACKET, :] = (piece * inverse * gain).astype(BF16)
+        first = pl.multiple_of(where_ref[at] * length, PACKET)
+        last = pl.multiple_of(count * length + where_ref[at] * PACKET, PACKET)
+        pairs = [
+            (normed_ref.at[at, pl.ds(0, length), :], out_ref.at[pl.ds(first, length), :]),
+            (normed_ref.at[at, pl.ds(length, PACKET), :], out_ref.at[pl.ds(last, PACKET), :]),
+            (piece_ref.at[pl.ds(length, PACKET), :], raw_ref.at[where_ref[at]]),
+        ]
+        moves += copies(pairs, sems.at[at])
+    for move in moves:
+        move.wait()
+
+
+def place(positions, pieces, gain, count, buffers=()):
+    rows, model = pieces[0].shape
+    number = len(pieces)
+    whole = pl.BlockSpec((rows, model), lambda i, where: (0, 0))
+    return pl.pallas_call(
+        functools.partial(place_kernel, count, number),
+        grid_spec=pltpu.PrefetchScalarGridSpec(
+            num_scalar_prefetch=1,
+            grid=(1,),
+            in_specs=[whole] * number
+            + [pl.BlockSpec((1, model), lambda i, where: (0, 0))]
+            + [pl.BlockSpec(memory_space=pl.ANY)] * len(buffers),
+            out_specs=[pl.BlockSpec(memory_space=pl.ANY)] * 2,
+            scratch_shapes=[pltpu.VMEM((number, rows, model), BF16), pltpu.SemaphoreType.DMA((number, 3))],
+        ),
+        out_shape=[
+            jax.ShapeDtypeStruct((count * rows, model), BF16),
+            jax.ShapeDtypeStruct((count, PACKET, model), BF16),
+        ],
+        input_output_aliases={2 + number + at: at for at in range(len(buffers))},
+        name="place",
+        cost_estimate=pl.CostEstimate(flops=rows * model * 8, bytes_accessed=rows * model * 4, transcendentals=rows),
+        compiler_params=pltpu.CompilerParams(vmem_limit_bytes=48 * 1024 * 1024),
+    )(jnp.stack(positions), *pieces, gain, *buffers)
+
+
+def project_kernel(plan, where_ref, *refs):
+    pieces, normed_ref = refs[: len(plan)], refs[len(plan)]
+    out_ref, weight_ref, joined_ref, sems, sem = refs[-5:]
+    chunk = pieces[0].shape[1]
+    pairs = [
+        (
+            piece.at[slot],
+            joined_ref.at[pl.ds(pl.multiple_of(where_ref[at] * chunk, PACKET), chunk), pl.ds(column, piece.shape[2])],
+        )
+        for at, (piece, (slot, column)) in enumerate(zip(pieces, plan))
+    ]
+    for move in copies(pairs, sems):
+        move.wait()
+    keep = pltpu.make_async_copy(joined_ref, weight_ref, sem)
+    keep.start()
+    width = joined_ref.shape[0]
+    part = min(2 * LANES, width)
+    for at in range(0, width, part):
+        out_ref[:, at : at + part] = lax.dot_general(
+            normed_ref[...], joined_ref[at : at + part, :], (((1,), (1,)), ((), ())), preferred_element_type=F32
+        ).astype(out_ref.dtype)
+    keep.wait()
+
+
+def project(slot, positions, pieces, normed, rows, width, dtype):
+    model = normed.shape[1]
+    plan = [(slot, column) for column, _ in pieces]
+    flat = lambda *shape: pl.BlockSpec(shape, lambda i, where: (0, 0))
+    return pl.pallas_call(
+        functools.partial(project_kernel, plan),
+        grid_spec=pltpu.PrefetchScalarGridSpec(
+            num_scalar_prefetch=1,
+            grid=(1,),
+            in_specs=[pl.BlockSpec(memory_space=pl.ANY)] * len(pieces) + [flat(rows, model)],
+            out_specs=[flat(rows, width), pl.BlockSpec(memory_space=pl.ANY)],
+            scratch_shapes=[
+                pltpu.VMEM((width, model), BF16),
+                pltpu.SemaphoreType.DMA((len(pieces),)),
+                pltpu.SemaphoreType.DMA,
+            ],
+        ),
+        out_shape=[jax.ShapeDtypeStruct((rows, width), dtype), jax.ShapeDtypeStruct((width, model), BF16)],
+        name="project",
+        cost_estimate=pl.CostEstimate(
+            flops=2 * rows * width * model, bytes_accessed=2 * (rows + 2 * width) * model, transcendentals=0
+        ),
+        compiler_params=pltpu.CompilerParams(vmem_limit_bytes=48 * 1024 * 1024),
+    )(jnp.stack(positions), *[piece for _, piece in pieces], normed)
+
+
+def join_kernel(number, where_ref, *refs):
+    pieces, weight_ref = refs[:number], refs[number]
+    out_ref, left_ref, joined_ref, sems, sem = refs[-5:]
+    rows = pieces[0].shape[0]
+    pairs = [
+        (piece, joined_ref.at[pl.ds(pl.multiple_of(where_ref[at] * rows, PACKET), rows), :])
+        for at, piece in enumerate(pieces)
+    ]
+    for move in copies(pairs, sems):
+        move.wait()
+    keep = pltpu.make_async_copy(joined_ref, left_ref, sem)
+    keep.start()
+    width = weight_ref.shape[0]
+    part = min(2 * LANES, width)
+    for at in range(0, width, part):
+        out_ref[:, at : at + part] = lax.dot_general(
+            joined_ref[...], weight_ref[at : at + part, :], (((1,), (1,)), ((), ())), preferred_element_type=F32
+        )
+    keep.wait()
+
+
+def join(positions, pieces, weight):
+    number = len(pieces)
+    rows, model = number * pieces[0].shape[0], pieces[0].shape[1]
+    width = weight.shape[0]
+    flat = lambda *shape: pl.BlockSpec(shape, lambda i, where: (0, 0))
+    return pl.pallas_call(
+        functools.partial(join_kernel, number),
+        grid_spec=pltpu.PrefetchScalarGridSpec(
+            num_scalar_prefetch=1,
+            grid=(1,),
+            in_specs=[pl.BlockSpec(memory_space=pl.ANY)] * number + [flat(width, model)],
+            out_specs=[flat(rows, width), pl.BlockSpec(memory_space=pl.ANY)],
+            scratch_shapes=[
+                pltpu.VMEM((rows, model), BF16),
+                pltpu.SemaphoreType.DMA((number,)),
+                pltpu.SemaphoreType.DMA,
+            ],
+        ),
+        out_shape=[jax.ShapeDtypeStruct((rows, width), F32), jax.ShapeDtypeStruct((rows, model), BF16)],
+        name="join",
+        cost_estimate=pl.CostEstimate(
+            flops=2 * rows * width * model, bytes_accessed=2 * (2 * rows + width) * model, transcendentals=0
+        ),
+        compiler_params=pltpu.CompilerParams(vmem_limit_bytes=48 * 1024 * 1024),
+    )(jnp.stack(positions), *pieces, weight)
+
+
+def widen_kernel(plan, where_ref, *refs):
+    pieces, (out_ref, extra_ref, in_ref, wide_ref, in_sems, out_sems, extra_sems) = refs[: len(plan)], refs[-7:]
+    rows = out_ref.shape[2]
+    steps = [(at, slot) for at in range(len(plan)) for slot in range(pieces[0].shape[0])]
+
+    def load(n):
+        at, slot = steps[n]
+        size = pieces[at].shape[2]
+        return pltpu.make_async_copy(pieces[at].at[slot], in_ref.at[n % DEPTH, :, pl.ds(0, size)], in_sems.at[n % DEPTH])
+
+    def save(n):
+        at, slot = steps[n]
+        size = pieces[at].shape[2]
+        source = wide_ref.at[n % DEPTH]
+        target = (slot, where_ref[at], slice(None), pl.ds(plan[at], size))
+        return (
+            pltpu.make_async_copy(source.at[pl.ds(0, rows), pl.ds(0, size)], out_ref.at[target], out_sems.at[n % DEPTH]),
+            pltpu.make_async_copy(
+                source.at[pl.ds(rows, extra_ref.shape[2]), pl.ds(0, size)], extra_ref.at[target], extra_sems.at[n % DEPTH]
+            ),
+        )
+
+    def wait(n):
+        for move in save(n):
+            move.wait()
+
+    for n in range(min(DEPTH, len(steps))):
+        load(n).start()
+    for n, (at, _) in enumerate(steps):
+        load(n).wait()
+        if n >= DEPTH:
+            wait(n - DEPTH)
+        size = pieces[at].shape[2]
+        wide_ref[n % DEPTH, :, :size] = in_ref[n % DEPTH, :, :size].astype(F32)
+        for move in save(n):
+            move.start()
+        if n + DEPTH < len(steps):
+            load(n + DEPTH).start()
+    for n in range(max(0, len(steps) - DEPTH), len(steps)):
+        wait(n)
+
+
+def widen(pieces, count, rows, buffers=()):
+    slots, deep, _ = pieces[0][2].shape
+    model = max(column + part.shape[2] for _, column, part in pieces)
+    plan = [column for _, column, _ in pieces]
+    number = len(pieces)
+    return pl.pallas_call(
+        functools.partial(widen_kernel, plan),
+        grid_spec=pltpu.PrefetchScalarGridSpec(
+            num_scalar_prefetch=1,
+            grid=(1,),
+            in_specs=[pl.BlockSpec(memory_space=pl.ANY)] * (number + len(buffers)),
+            out_specs=[pl.BlockSpec(memory_space=pl.ANY)] * 2,
+            scratch_shapes=[pltpu.VMEM((DEPTH, deep, model), BF16), pltpu.VMEM((DEPTH, deep, model), F32)]
+            + [pltpu.SemaphoreType.DMA((DEPTH,))] * 3,
+        ),
+        out_shape=[jax.ShapeDtypeStruct((slots, count, size, model), F32) for size in (rows, deep - rows)],
+        input_output_aliases={1 + number + at: at for at in range(len(buffers))},
+        name="widen",
+        cost_estimate=pl.CostEstimate(
+            flops=0, bytes_accessed=6 * sum(part.size for _, _, part in pieces), transcendentals=0
+        ),
+        compiler_params=pltpu.CompilerParams(vmem_limit_bytes=48 * 1024 * 1024),
+    )(jnp.stack([position for position, _, _ in pieces]), *[part for _, _, part in pieces], *buffers)
+
+
+def transposed_dot(left, right):
+    return lax.dot_general(left, right, (((0,), (0,)), ((), ())), preferred_element_type=F32)
+
+
+def shares_kernel(blocks, one_ref, two_ref, one_right_ref, two_right_ref, out_ref):
+    chunk = one_ref.shape[1] // blocks
+
+    def put(product):
+        for j in range(blocks):
+            at = chunk_of(j, blocks) * chunk
+            out_ref[0, j * chunk : (j + 1) * chunk, :] = product[at : at + chunk]
+
+    @pl.when(pl.program_id(0) == 0)
+    def _():
+        put(transposed_dot(one_ref[...], one_right_ref[...]).astype(BF16))
+
+    @pl.when(pl.program_id(0) == 1)
+    def _():
+        put(transposed_dot(two_ref[...], two_right_ref[...]).astype(BF16))
+
+
+def shares_of(one, two, one_right, two_right, blocks):
+    rows, width = one.shape
+    model = one_right.shape[1]
+    part = model // 2
+    last = model // part - 1
+    left = pl.BlockSpec((rows, width), lambda i, j: (0, 0))
+    return pl.pallas_call(
+        functools.partial(shares_kernel, blocks),
+        grid=(2, model // part),
+        in_specs=[
+            left,
+            left,
+            pl.BlockSpec((rows, part), lambda i, j: (0, j * (1 - i) + last * i)),
+            pl.BlockSpec((rows, part), lambda i, j: (0, j * i)),
+        ],
+        out_specs=pl.BlockSpec((1, width, part), lambda i, j: (i, 0, j)),
+        out_shape=jax.ShapeDtypeStruct((2, width, model), BF16),
+        name="shares",
+        cost_estimate=pl.CostEstimate(
+            flops=4 * rows * width * model, bytes_accessed=4 * (rows + width) * model, transcendentals=0
+        ),
+        compiler_params=pltpu.CompilerParams(vmem_limit_bytes=48 * 1024 * 1024),
+    )(one, two, one_right, two_right)
+
+
+def terms_kernel(number, groups, where_ref, *refs):
+    lefts, rights, (kept_ref, sent_ref, *along, product_ref) = refs[:number], refs[number : 2 * number], refs[2 * number :]
+    if along:
+        normed_ref, kept_ref, sent_ref, along_ref = kept_ref, sent_ref, *along
+    product = jnp.dot(lefts[0][...], rights[0][...], preferred_element_type=F32)
+    for left, right in zip(lefts[1:], rights[1:]):
+        product = product + jnp.dot(left[...], right[...], preferred_element_type=F32)
+    product_ref[...] = product
+    if along:
+        total = jnp.sum(product * normed_ref[...].astype(F32), axis=0, keepdims=True)
+        along_ref[...] = jnp.broadcast_to(total, along_ref.shape)
+    length = product_ref.shape[0] // groups
+    for r in range(groups):
+        part = product_ref[pl.ds(pl.multiple_of(where_ref[r] * length, GROUP), length), :]
+        if r % 2:
+            sent_ref[r // 2] = part.astype(BF16)
+        else:
+            kept_ref[r // 2] = part
+
+
+def terms_of(order, lefts, rights, normed=None):
+    groups, number = len(order), len(lefts)
+    rows, width = lefts[0].shape
+    model = rights[0].shape[1]
+    length, part = rows // groups, model // 4
+    rounds = pl.BlockSpec((groups // 2, length, part), lambda j, where: (0, 0, j))
+    out_specs, out_shape = [rounds, rounds], [
+        jax.ShapeDtypeStruct((groups // 2, length, model), dtype) for dtype in (F32, BF16)
+    ]
+    more = []
+    if normed is not None:
+        more = [pl.BlockSpec((rows, part), lambda j, where: (0, j))]
+        out_specs.append(pl.BlockSpec((GROUP, part), lambda j, where: (0, j)))
+        out_shape.append(jax.ShapeDtypeStruct((GROUP, model), F32))
+    return pl.pallas_call(
+        functools.partial(terms_kernel, number, groups),
+        grid_spec=pltpu.PrefetchScalarGridSpec(
+            num_scalar_prefetch=1,
+            grid=(model // part,),
+            in_specs=[pl.BlockSpec((rows, width), lambda j, where: (0, 0))] * number
+            + [pl.BlockSpec((width, part), lambda j, where: (0, j))] * number
+            + more,
+            out_specs=out_specs,
+            scratch_shapes=[pltpu.VMEM((rows, part), F32)],
+        ),
+        out_shape=out_shape,
+        name="terms",
+        cost_estimate=pl.CostEstimate(
+            flops=2 * number * rows * width * model,
+            bytes_accessed=number * 2 * (rows + model) * width + 3 * rows * model,
+            transcendentals=0,
+        ),
+        compiler_params=pltpu.CompilerParams(vmem_limit_bytes=48 * 1024 * 1024),
+    )(jnp.stack(order), *lefts, *rights, *([] if normed is None else [normed]))
+
+
+def reorder_kernel(in_ref, out_ref):
+    out_ref[...] = in_ref[0].astype(F32)
+
+
+def reorder(chunks):
+    count, rows, model = chunks.shape
+    half = count // 2
+    return pl.pallas_call(
+        reorder_kernel,
+        grid=(count,),
+        in_specs=[pl.BlockSpec((1, rows, model), lambda j: ((j % half) * 2 + j // half, 0, 0))],
+        out_specs=pl.BlockSpec((rows, model), lambda j: (j, 0)),
+        out_shape=jax.ShapeDtypeStruct((count * rows, model), F32),
+        name="reorder",
+        cost_estimate=pl.CostEstimate(flops=0, bytes_accessed=6 * chunks.size, transcendentals=0),
+    )(chunks)
+
+
+def away_kernel(where_ref, left_ref, right_ref, out_ref):
+    out_ref[...] = transposed_dot(left_ref[...], right_ref[...]).astype(out_ref.dtype)
+
+
+def away_product(which, left, right):
+    rows, width = left.shape
+    model = right.shape[1]
+    part, half = model // 2, width // 2
+    return pl.pallas_call(
+        away_kernel,
+        grid_spec=pltpu.PrefetchScalarGridSpec(
+            num_scalar_prefetch=1,
+            grid=(model // part,),
+            in_specs=[
+                pl.BlockSpec((rows, half), lambda j, where: (0, where[0])),
+                pl.BlockSpec((rows, part), lambda j, where: (0, j)),
+            ],
+            out_specs=pl.BlockSpec((half, part), lambda j, where: (0, j)),
+        ),
+        out_shape=jax.ShapeDtypeStruct((half, model), BF16),
+        name="away_product",
+        cost_estimate=pl.CostEstimate(
+            flops=2 * rows * half * model, bytes_accessed=2 * (rows + half) * model, transcendentals=0
+        ),
+        compiler_params=pltpu.CompilerParams(vmem_limit_bytes=48 * 1024 * 1024),
+    )(which.reshape(1), left, right)
+
+
+def stay_kernel(where_ref, left_ref, right_ref, away_ref, small_ref, small_away_ref, kept_ref, sent_ref):
+    product = transposed_dot(left_ref[...], right_ref[...]) + away_ref[...].astype(F32)
+    extra = small_ref[...] + small_away_ref[...].astype(F32)
+    chunk, more = product.shape[0] // 4, extra.shape[0] // 4
+    for at in range(4):
+        is_kept = jnp.where(pl.program_id(0) == 0, (at & 1) == where_ref[1], (at >> 1) == where_ref[2])
+        index = jnp.where(pl.program_id(0) == 0, at >> 1, at & 1)
+        rows = (product[at * chunk : (at + 1) * chunk], extra[at * more : (at + 1) * more])
+
+        @pl.when(is_kept)
+        def _():
+            kept_ref[0, index, :chunk, :], kept_ref[0, index, chunk:, :] = rows
+
+        @pl.when(jnp.logical_not(is_kept))
+        def _():
+            sent_ref[0, index, :chunk, :] = rows[0].astype(BF16)
+            sent_ref[0, index, chunk:, :] = rows[1].astype(BF16)
+
+
+def stay_product(which, left, right, away, small, small_away):
+    rows, width = left.shape
+    model = right.shape[1]
+    part, half = model // 2, width // 2
+    extra = small.shape[0] // 2
+    out = pl.BlockSpec((1, 2, (half + extra) // 4, part), lambda j, where: (j, 0, 0, 0))
+    column = lambda size: pl.BlockSpec((size, part), lambda j, where: (0, j))
+    return pl.pallas_call(
+        stay_kernel,
+        grid_spec=pltpu.PrefetchScalarGridSpec(
+            num_scalar_prefetch=1,
+            grid=(2,),
+            in_specs=[
+                pl.BlockSpec((rows, half), lambda j, where: (0, where[0])),
+                column(rows),
+                column(half),
+                pl.BlockSpec((extra, part), lambda j, where: (where[0], j)),
+                column(extra),
+            ],
+            out_specs=[out, out],
+        ),
+        out_shape=[jax.ShapeDtypeStruct((2, 2, (half + extra) // 4, part), dtype) for dtype in (F32, BF16)],
+        name="stay_product",
+        cost_estimate=pl.CostEstimate(
+            flops=2 * rows * half * model, bytes_accessed=2 * (rows + 4 * half) * model, transcendentals=0
+        ),
+        compiler_params=pltpu.CompilerParams(vmem_limit_bytes=48 * 1024 * 1024),
+    )(which, left, right, away, small, small_away)
+
+
+def terms_kernel(number, groups, where_ref, *refs):
+    lefts, rights, (kept_ref, sent_ref, *along, product_ref) = refs[:number], refs[number : 2 * number], refs[2 * number :]
+    if along:
+        normed_ref, kept_ref, sent_ref, along_ref = kept_ref, sent_ref, *along
+    product = jnp.dot(lefts[0][...], rights[0][...], preferred_element_type=F32)
+    for left, right in zip(lefts[1:], rights[1:]):
+        product = product + jnp.dot(left[...], right[...], preferred_element_type=F32)
+    product_ref[...] = product
+    if along:
+        total = jnp.sum(product * normed_ref[...].astype(F32), axis=0, keepdims=True)
+        along_ref[...] = jnp.broadcast_to(total, along_ref.shape)
+    length = product_ref.shape[0] // groups
+    for r in range(groups):
+        part = product_ref[pl.ds(pl.multiple_of(where_ref[r] * length, GROUP), length), :]
+        if r % 2:
+            sent_ref[r // 2] = part.astype(BF16)
+        else:
+            kept_ref[r // 2] = part
+
+
+def terms_of(order, lefts, rights, normed=None):
+    groups, number = len(order), len(lefts)
+    rows, width = lefts[0].shape
+    model = rights[0].shape[1]
+    length, part = rows // groups, model // 4
+    rounds = pl.BlockSpec((groups // 2, length, part), lambda j, where: (0, 0, j))
+    out_specs, out_shape = [rounds, rounds], [
+        jax.ShapeDtypeStruct((groups // 2, length, model), dtype) for dtype in (F32, BF16)
+    ]
+    more = []
+    if normed is not None:
+        more = [pl.BlockSpec((rows, part), lambda j, where: (0, j))]
+        out_specs.append(pl.BlockSpec((GROUP, part), lambda j, where: (0, j)))
+        out_shape.append(jax.ShapeDtypeStruct((GROUP, model), F32))
+    return pl.pallas_call(
+        functools.partial(terms_kernel, number, groups),
+        grid_spec=pltpu.PrefetchScalarGridSpec(
+            num_scalar_prefetch=1,
+            grid=(model // part,),
+            in_specs=[pl.BlockSpec((rows, width), lambda j, where: (0, 0))] * number
+            + [pl.BlockSpec((width, part), lambda j, where: (0, j))] * number
+            + more,
+            out_specs=out_specs,
+            scratch_shapes=[pltpu.VMEM((rows, part), F32)],
+        ),
+        out_shape=out_shape,
+        name="terms",
+        cost_estimate=pl.CostEstimate(
+            flops=2 * number * rows * width * model,
+            bytes_accessed=number * 2 * (rows + model) * width + 3 * rows * model,
+            transcendentals=0,
+        ),
+        compiler_params=pltpu.CompilerParams(vmem_limit_bytes=48 * 1024 * 1024),
+    )(jnp.stack(order), *lefts, *rights, *([] if normed is None else [normed]))
+
+
+def reorder_kernel(in_ref, out_ref):
+    out_ref[...] = in_ref[0].astype(F32)
+
+
+def reorder(chunks):
+    count, rows, model = chunks.shape
+    half = count // 2
+    return pl.pallas_call(
+        reorder_kernel,
+        grid=(count,),
+        in_specs=[pl.BlockSpec((1, rows, model), lambda j: ((j % half) * 2 + j // half, 0, 0))],
+        out_specs=pl.BlockSpec((rows, model), lambda j: (j, 0)),
+        out_shape=jax.ShapeDtypeStruct((count * rows, model), F32),
+        name="reorder",
+        cost_estimate=pl.CostEstimate(flops=0, bytes_accessed=6 * chunks.size, transcendentals=0),
+    )(chunks)
+
+
+def half_kernel(where_ref, left_ref, right_ref, *refs):
+    product = transposed_dot(left_ref[...], right_ref[...])
+    if len(refs) > 1:
+        product = product + refs[0][...].astype(F32)
+    refs[-1][...] = product.astype(refs[-1].dtype)
+
+
+def half_product(which, left, right, dtype, *addend):
+    rows, width = left.shape
+    model = right.shape[1]
+    part, half = model // 2, width // 2
+    out = pl.BlockSpec((half, part), lambda j, where: (0, j))
+    return pl.pallas_call(
+        half_kernel,
+        grid_spec=pltpu.PrefetchScalarGridSpec(
+            num_scalar_prefetch=1,
+            grid=(model // part,),
+            in_specs=[
+                pl.BlockSpec((rows, half), lambda j, where: (0, where[0])),
+                pl.BlockSpec((rows, part), lambda j, where: (0, j)),
+            ]
+            + [out] * len(addend),
+            out_specs=out,
+        ),
+        out_shape=jax.ShapeDtypeStruct((half, model), dtype),
+        name="half_product",
+        cost_estimate=pl.CostEstimate(
+            flops=2 * rows * half * model, bytes_accessed=2 * (rows + half) * model, transcendentals=0
+        ),
+        compiler_params=pltpu.CompilerParams(vmem_limit_bytes=48 * 1024 * 1024),
+    )(which.reshape(1), left, right, *addend)
 
 
 def dot(left, right, over_left, over_right):
@@ -341,39 +960,32 @@
     taps, bias32 = conv_weight.astype(F32), conv_bias.astype(F32)
     dt_bias32, skip32 = dt_bias.astype(F32), skip_weight.astype(F32)
 
+    gain = in_order(small_gather(norm_gain[None], "wt"), "wt").reshape(1, model)
+    gain32 = gain.astype(F32)
+    chunk = width // blocks
+    slots = [lax.dynamic_slice_in_dim(in_weight, slot * width + block * chunk, chunk, 0) for slot in range(2)]
     edge_ids = jnp.pad(own_ids[length - HALO :].astype(BF16), (0, model - HALO))
     packet = jnp.concatenate([own[length - HALO :], edge_ids[None]], axis=0)
+    packet, slots = tie(packet, slots)
     packet = shifted(packet, "seq", 1)
     all_ids = jnp.concatenate([packet[HALO, :HALO], own_ids.astype(BF16)])
-    packet = jnp.concatenate(
-        [
-            packet[:HALO],
-            jnp.pad(all_ids, (0, model - HALO - length))[None],
-            jnp.pad(norm_gain, (0, model - norm_gain.shape[0]))[None],
-            jnp.zeros((PACKET - HALO - 2, model), BF16),
-        ],
-        axis=0,
-    )
-    packets = in_order(small_gather(packet, "wt"), "wt")
-
-    chunk = width // blocks
-    slots = [
-        lax.dynamic_slice_in_dim(in_weight, slot * width + block * chunk, chunk, 0) for slot in range(2)
-    ]
+    ids_row = jnp.pad(all_ids, (0, model - HALO - length))[None]
+    sent = jnp.concatenate([own, packet[:HALO], ids_row, jnp.zeros((PACKET - KERNEL, model), BF16)], axis=0)
+
     value_chunk, gate_chunk = to_users(slots, "wt")
-    value_weight = lax.all_gather(value_chunk, "seq", axis=0, tiled=True)
-    gate_weight = lax.all_gather(gate_chunk, "seq", axis=0, tiled=True)
-
-    gathered = in_order(line_gather(own, "wt"), "wt").reshape(rows, model)
-    cots = in_order(line_gather(own_cot, "wt"), "wt").reshape(rows, model)
-
-    gain32 = packets[:, HALO + 1, : model // groups].astype(F32).reshape(model)
-
-    features = jnp.concatenate([gathered, packets.reshape(groups * PACKET, model)], axis=0).astype(F32)
-    normed_all = (features * inverse_rms(features) * gain32).astype(BF16)
-    normed = normed_all[:rows]
-    values_all = dot(normed_all, value_weight, 1, 1).astype(BF16)
-    gate_pre = dot(normed, gate_weight, 1, 1)
+    near_tokens = across_bit(sent, "wt", 1)
+    far_tokens = far_gather(sent, "wt")
+    value_chunk, near_tokens = tie(value_chunk, near_tokens)
+    first_pieces, last_pieces = bit_gather(jnp.stack([value_chunk, gate_chunk]), "seq")
+    weight_pieces = first_pieces + spread(last_pieces, "seq")
+    chunks = [block ^ r for r, _, _ in weight_pieces]
+    parts = [(column, part) for _, column, part in weight_pieces]
+    buffers = place([mine, mine ^ 1], [sent, near_tokens], gain, groups)
+    far_tokens, buffers = tie(far_tokens, buffers)
+    far_tokens.update(near_gather(far_tokens, "wt"))
+    order = [mine ^ r for r in range(groups)]
+    normed_all, raw_packets = place([mine ^ r for r in far_tokens], list(far_tokens.values()), gain, groups, buffers)
+    values_all, value_weight = project(0, chunks, parts, normed_all, normed_all.shape[0], width, BF16)
     extended = jnp.concatenate(
         [
             values_all[rows:].reshape(groups, PACKET, width)[:, :HALO],
@@ -381,13 +993,18 @@
         ],
         axis=1,
     ).astype(F32)
-    ids = packets[:, HALO, : HALO + length]
+    ids = raw_packets[:, HALO, : HALO + length]
     same_doc = [(ids[:, k : k + length] == ids[:, HALO:]).astype(F32)[:, :, None] for k in range(KERNEL)]
     conv_sum = bias32 + sum(taps[k] * extended[:, k : k + length] * same_doc[k] for k in range(KERNEL))
     conv_out = jax.nn.silu(conv_sum).astype(BF16).reshape(rows, width)
     conv_vals = conv_out.astype(F32)
 
-    projected = all_sum(dot(proj_weight, conv_out, 0, 1), "wt")
+    projected = dot(proj_weight, conv_out, 0, 1)
+    projected_sent, late_normed, cot_sent = tie(projected.astype(BF16), normed_all, own_cot)
+    projected = all_sum(projected, projected_sent, "wt")
+    gate_pre, gate_weight = project(1, chunks, parts, late_normed, rows, width, F32)
+    projected, gate_pre = tie(projected, gate_pre)
+    cot_pieces = {k: circular(cot_sent, "wt", k) if k else own_cot for k in range(groups)}
     query, key = projected[:STATE], projected[STATE : 2 * STATE]
     low_rank = projected[2 * STATE :].astype(BF16)
     keep = same_doc[KERNEL - 2].reshape(1, rows)
@@ -398,36 +1015,41 @@
     shrink = 1.0 / (1.0 + beta * key_square)
     rate = beta * shrink
     feed = rate * conv_vals
-    d_gated = dot(cots, out_weight, 1, 1)
+    mixer = Mixer(groups, length, width)
+    own_map = jnp.stack(mixer.summary(key, keeps, rate, feed))
+    cot_pieces, own_map = tie(cot_pieces, own_map)
+    maps = lax.all_gather(own_map, "seq")
+    d_gated, cots = join([(mine - k) % groups for k in cot_pieces], list(cot_pieces.values()), out_weight)
     sigma = jax.nn.sigmoid(gate_pre)
     gate = gate_pre * sigma
     d_mixed = d_gated * gate
-
-    mixer = Mixer(groups, length, width)
-    summary = jnp.stack([part.astype(BF16) for part in mixer.summary(key, query, keeps, rate, feed, d_mixed)])
-    everything = lax.all_gather(summary, "seq").astype(F32)
+    adjoint = mixer.adjoint_summary(key, query, keeps, rate, d_mixed)
+    adjoints = lax.all_gather(adjoint, "seq")
     state_in = jnp.zeros((groups, STATE, width), F32)
+    for at in range(blocks):
+        step = maps[at, 0].astype(F32) * state_in + maps[at, 1].astype(F32)
+        state_in = jnp.where(at < block, step, state_in)
+
+    core_out, before, d_query = mixer.forward(key, query, keeps, rate, feed, d_mixed, state_in)
+    adjoints, core_out = tie(adjoints, core_out)
     grad_in = jnp.zeros((groups, STATE, width), F32)
-    for at in range(blocks):
-        state_in = jnp.where(at < block, everything[at, 0] * state_in + everything[at, 1], state_in)
-        back = blocks - 1 - at
-        grad_in = jnp.where(back > block, everything[back, 0] * grad_in + everything[back, 2], grad_in)
-
-    core_out, before, d_query = mixer.forward(key, query, keeps, rate, feed, d_mixed, state_in)
+    for at in reversed(range(blocks)):
+        step = maps[at, 0].astype(F32) * grad_in + adjoints[at].astype(F32)
+        grad_in = jnp.where(at > block, step, grad_in)
     d_query = mixer.columns(d_query)
     mixed = core_out + skip32 * conv_vals
     gated = (mixed * gate).astype(BF16)
     d_gate = (d_gated * mixed * (sigma * (1.0 + gate_pre * (1.0 - sigma)))).astype(BF16)
     skip_part = jnp.sum(d_mixed * conv_vals, axis=0)
-    out_parts = dot(gated, out_weight, 1, 0).reshape(groups, length, model)
-    block_output = (own.astype(F32) + line_scatter(out_parts, "wt")).astype(BF16)
-    out_share = dot(gated, cots, 0, 0)
-    out_chunk = lax.psum_scatter(out_share.astype(BF16), "seq", scatter_dimension=0, tiled=True)
-    gate_share = dot(d_gate, normed, 0, 0)
-    gate_part = lax.psum_scatter(gate_share.astype(BF16), "seq", scatter_dimension=0, tiled=True)
+    shares = shares_of(gated, d_gate, cots, normed_all, blocks)
+    out_kept, out_sent = terms_of(order, [gated], [out_weight])
+    shares, out_sent, grad_in = tie(shares, out_sent, grad_in)
+    out_chunk, gate_part = lax.psum_scatter(shares, "seq", scatter_dimension=1, tiled=True)
+    out_comes = across_bit(out_sent, "wt", 1)
     gate_slots = to_owners(gate_part, "wt", groups // 2)
 
     along, across, d_key = mixer.backward(key, query, keeps, rate, feed, d_mixed, before, grad_in)
+    along, across, d_key, out_comes = tie(along, across, d_key, out_comes)
     d_key = mixer.columns(d_key)
     d_rate = conv_vals * along - across
     d_beta = d_rate * shrink * shrink
@@ -437,9 +1059,12 @@
     dt_bias_part = jnp.sum(d_bias, axis=0)
     d_beta_low = d_bias.astype(BF16)
     d_low_rank = dot(dt_weight, d_beta_low, 0, 1)
-    d_projected = all_sum(jnp.concatenate([d_query, d_key, d_low_rank], axis=0), "wt").astype(BF16)
-    dt_part = dot(d_beta_low, low_rank, 0, 1)
-    proj_part = dot(conv_out, d_projected, 0, 1)
+    d_projected = jnp.concatenate([d_query, d_key, d_low_rank], axis=0)
+    out_terms = near_sum(out_kept, out_comes)
+    d_projected = all_sum(d_projected, d_projected.astype(BF16), "wt").astype(BF16)
+    d_projected, out_sent = tie(d_projected, out_terms[-1].astype(BF16))
+    dt_part = dot(low_rank, d_beta_low, 1, 0)
+    proj_part = dot(d_projected, conv_out, 1, 0)
     d_value = d_mixed * skip32 + rate * along + dot(d_projected, proj_weight, 0, 1)
 
     sigma_conv = jax.nn.sigmoid(conv_sum)
@@ -454,26 +1079,75 @@
     d_rows = d_extended[:, HALO:] + jnp.pad(returned, ((0, 0), (length - HALO, 0), (0, 0)))
     d_rows = d_rows.astype(BF16).reshape(rows, width)
 
-    value_share = dot(d_rows, normed, 0, 0)
-    value_part = lax.psum_scatter(value_share.astype(BF16), "seq", scatter_dimension=0, tiled=True)
-    value_slots = to_owners(value_part, "wt", 0)
-    in_chunk = jnp.stack([value_slots[slot] + gate_slots[slot] for slot in range(2)])
-
-    d_normed_parts = (dot(d_rows, value_weight, 1, 0) + dot(d_gate, gate_weight, 1, 0)).reshape(groups, length, model)
-    d_normed = line_scatter(d_normed_parts, "wt")
+    upper, lower, lowest = (block & (blocks // 2)) // (blocks // 2), (block & (blocks // 4)) // (blocks // 4), block & 1
+    away = across_bit(away_product(1 - lowest, d_rows, normed_all), "seq", 1)
+    one_rows = jnp.concatenate([conv_part, jnp.stack([conv_bias_part, dt_bias_part, skip_part, jnp.zeros_like(skip_part)])])
+    deep, folds = PACKET * 2 * blocks, model // width
+    flat = jnp.concatenate([proj_part, dt_part, one_rows], axis=0)
+    flat = jnp.pad(flat, ((0, folds * deep - flat.shape[0]), (0, 0)))
+    small = jnp.concatenate([flat[at * deep : (at + 1) * deep] for at in range(folds)], axis=1)
+    small_sent = lax.dynamic_slice_in_dim(small, (1 - lowest) * (deep // 2), deep // 2, 0).astype(BF16)
+    small_away = across_bit(small_sent, "seq", 1)
+    which = jnp.stack([lowest, lower, upper])
+    kept, sent = stay_product(which, d_rows, normed_all, away, small, small_away)
+    late_rows, kept = tie(d_rows, kept)
+    d_normed_terms = terms_of(order, [late_rows, d_gate], [value_weight, gate_weight], normed_all)
+
+    def then_output(_):
+        return (own.astype(F32) + far_sum(out_terms, "wt", out_sent)).astype(BF16)
+
+    summed, d_normed_terms, block_output = bit_scatter(kept, sent, "seq", d_normed_terms, then_output)
+    d_normed_kept, d_normed_sent, gain_part = d_normed_terms
+    own_rows = (width // 8, deep // 8)
+    for bit in bits_of("seq")[2:-1]:
+        is_set = (block & bit) // bit
+        terms = [summed[: own_rows[0]], summed[own_rows[0] :]]
+        own_rows = (own_rows[0] // 2, own_rows[1] // 2)
+        pick = lambda want: jnp.concatenate(
+            [lax.dynamic_slice_in_dim(part, want * size, size, 0) for part, size in zip(terms, own_rows)]
+        )
+        summed = pick(is_set) + across_bit(pick(1 - is_set).astype(BF16), "seq", bit).astype(F32)
+    summed = summed.astype(BF16)
+    value_slots = to_owners(summed[:chunk], "wt", 0)
+    small_slots = summed[chunk:].reshape(2, PACKET, model)
+
+    d_normed_comes = across_bit(d_normed_sent, "wt", 1)
+
+    value_slots, d_normed_comes = tie(value_slots, d_normed_comes)
+    in_chunk = jnp.stack([jnp.concatenate([value_slots[slot] + gate_slots[slot], small_slots[slot]]) for slot in range(2)])
+    placed = lambda pieces: [(chunk_of(block ^ r, blocks), column, part) for r, column, part in pieces]
+    first_pieces, last_pieces = bit_gather(in_chunk, "seq")
+    buffers = widen(placed(first_pieces), blocks, chunk)
+
+    held = []
+
+    def hold(part):
+        part, *rest = tie(part, *(held or buffers))
+        held[:] = rest
+        return part
+
+    d_normed = far_sum(near_sum(d_normed_kept, d_normed_comes), "wt", hold=hold)
+    buffers = held
     own32 = own.astype(F32)
     inv_rms = inverse_rms(own32)
     weighted = d_normed * gain32
     along_features = jnp.mean(own32 * weighted, axis=1, keepdims=True)
     token_grad = (own_cot.astype(F32) + inv_rms * weighted - own32 * (inv_rms * inv_rms * inv_rms) * along_features).astype(BF16)
-    gain_part = jnp.sum(d_normed * own32 * inv_rms, axis=0)
-    gain_part = lax.psum_scatter(gain_part, "wt", scatter_dimension=0, tiled=True)
-
-    gain_grad, conv_grad, conv_bias_grad, proj_grad, dt_grad, dt_bias_grad, skip_grad = lax.psum(
-        (gain_part, conv_part, conv_bias_part, proj_part, dt_part, dt_bias_part, skip_part), "seq"
-    )
-    out_grad = lax.all_gather(out_chunk, "seq", axis=0, tiled=True).astype(F32)
-    in_grad = lax.all_gather(in_chunk, "seq", axis=1, tiled=True).astype(F32).reshape(2 * width, model)
+    gain_part = gain_part[0] / gain32[0]
+    gain_stays, gain_comes = direct_scatter(gain_part.reshape(groups, 1, model // groups), "wt")
+    gain_grad = (gain_stays + sum(part.astype(F32) for part in gain_comes))[0]
+    for bit in bits_of("seq"):
+        gain_grad = gain_grad + across_bit(gain_grad, "seq", bit)
+    out_grad = reorder(lax.all_gather(out_chunk, "seq"))
+    last_parts, *buffers, out_grad = tie([part for _, _, part in last_pieces], *buffers, out_grad)
+    last_pieces = [(r, column, part) for (r, column, _), part in zip(last_pieces, last_parts)]
+    in_grad, small = widen(placed(spread(last_pieces, "seq")), blocks, chunk, buffers)
+    in_grad = in_grad.reshape(2 * width, model)
+    small = small.transpose(1, 0, 2, 3).reshape(deep, model)
+    flat = jnp.concatenate([small[:, at * width : (at + 1) * width] for at in range(folds)], axis=0)
+    ranks, low_ranks = proj_part.shape[0], dt_part.shape[0]
+    proj_grad, dt_grad, small = flat[:ranks].T, flat[ranks : ranks + low_ranks].T, flat[ranks + low_ranks :]
+    conv_grad, conv_bias_grad, dt_bias_grad, skip_grad = small[:KERNEL], small[KERNEL], small[KERNEL + 1], small[KERNEL + 2]
     return (
         block_output[None],
         token_grad[None],

time: 639 us -> 526 us (0.82)
  waiting for transfers between devices: 273 us -> 159 us
  Pallas kernels: 77.7 us -> 164 us
  matrix products: 50.2 us -> 8.35 us
  blocking collectives: 39.3 us -> 0 us
  local copies, waits for them, and re-layouts: 16.3 us -> 44.3 us
  other arithmetic: 65.4 us -> 45.6 us
  starting transfers between devices: 95.3 us -> 80.2 us
    reduce_scatter x3 -> x1, waiting for transfers between devices: 104 us -> 0.01 us  [on_device(): lax.psum_scatter(shares, 'seq', scatter_dimension=1, tiled=True)]
    pallas_call x1 -> x15, Pallas kernels: 17.9 us -> 104 us  [the longest x2 15.7 us: project(): pl.pallas_call(functools.partial(project_kernel, plan), grid_spec=pltpu.P...]
    ppermute x28 -> x34, starting transfers between devices: 79.1 us -> 30.9 us  [across_bit(): lax.ppermute(value, axis, [(i, i ^ bit) for i in range(lax.axis_size(axis...]
    dot_general x15 -> x6, matrix products: 50.2 us -> 8.35 us  [dot(): lax.dot_general(left, right, (((over_left,), (over_right,)), ((), ())), p...]
    ppermute x3 -> x15, starting transfers between devices: 1.28 us -> 30 us  [circular(): lax.ppermute(value, axis, [(i, (i + steps) % count) for i in range(count)])]
    ppermute x28 -> x34, waiting for transfers between devices: 98 us -> 69.4 us  [across_bit(): lax.ppermute(value, axis, [(i, i ^ bit) for i in range(lax.axis_size(axis...]
    ppermute x3 -> x15, waiting for transfers between devices: 16.6 us -> 41.2 us  [circular(): lax.ppermute(value, axis, [(i, (i + steps) % count) for i in range(count)])]
    psum x1 -> x0, blocking collectives: 23.5 us -> none  [on_device(): lax.psum((gain_part, conv_part, conv_bias_part, proj_part, dt_part, dt_bi...]
  transfers between devices with their start and end apart: 48 -> 61, of which waited for: 24 -> 23; matrix products, arithmetic and copies ran while one was open for 15% -> 12% of each run, Pallas kernels for 0% -> 26%
where the time goes in v2:
time: 526 us; the launch traced here: 516 us
  Pallas kernels  164 us (31%)
  waiting for transfers between devices  159 us (30%)
  starting transfers between devices  80.2 us (15%)
  other arithmetic  45.6 us (9%)
  local copies, waits for them, and re-layouts  44.3 us (8%)
  between operations  15.5 us (3%)
  matrix products  8.35 us (2%)
    ppermute x34, waiting for transfers between devices, across_bit(): lax.ppermute(value, axis, [(i, i ^ bit) for i in range(lax.axis_size(axis...  69.4 us
    ppermute x15, waiting for transfers between devices, circular(): lax.ppermute(value, axis, [(i, (i + steps) % count) for i in range(count)])  41.2 us
    pallas_call x1, Pallas kernels, backward(): self.call(backward_kernel, 'adjoints', specs, [self.row, self.row, self.s...  36 us
    ppermute x34, starting transfers between devices, across_bit(): lax.ppermute(value, axis, [(i, i ^ bit) for i in range(lax.axis_size(axis...  30.9 us
    ppermute x15, starting transfers between devices, circular(): lax.ppermute(value, axis, [(i, (i + steps) % count) for i in range(count)])  30 us
    pallas_call x1, Pallas kernels, forward(): self.call(forward_kernel, 'states', specs, [self.row, self.states, self.s...  23.7 us
    ppermute x1, waiting for transfers between devices, to_users(): lax.ppermute(jnp.where(mine < half, slots[1], slots[0]), axis, [(j, 2 * j...  20.9 us
    unnamed x144, local copies, waits for them, and re-layouts  17 us
  transfers between devices with their start and end apart: 61, of which 23 were waited for; matrix products, arithmetic and copies ran while one was open for 12% of the time, Pallas kernels for 26%

profile of v2, /device:TPU:0, one launch (start us, length us, event | category | flops | bytes accessed | tf_op | source)
XLA Modules:
  0.0 516.4 jit_solution(9611244364806022832)
XLA Ops:
  10.2 2.4 collective-permute-start.2
  13.3 5.2 %collective-permute-start.1 = (bf16[128,2048]{1,0:T(8,128)(2,1)S(1)}, bf16[128,2048]{1,0:T(8,128)(2,1)}, u32[]{:S(2)}, u32[]{:S(2)}) collective-permute-start(bf16[128,2048]{1,0:T(8,128)(2,1)S(1)} %get-tuple-element.241), channel_id=1, source_target_pairs={{0,1},{1,3},{2,0},{3,2},{4,5},{5,7},{6,4},{7,6},{8,9},{9,11},{10,8... | collective-permute-start | bytes 1572872 | tf_op jit(solution)/shard_map/ppermute | solution.py:146
  19.1 1.9 collective-permute-start.13
  20.9 20.9 %collective-permute-done.1 = bf16[128,2048]{1,0:T(8,128)(2,1)} collective-permute-done((bf16[128,2048]{1,0:T(8,128)(2,1)S(1)}, bf16[128,2048]{1,0:T(8,128)(2,1)}, u32[]{:S(2)}, u32[]{:S(2)}) %collective-permute-start.1) | collective-permute-done | bytes 524320 | tf_op jit(solution)/shard_map/ppermute | solution.py:146
  43.0 6.3 %collective-permute-done.3.refs_1_ = bf16[144,2048]{1,0:T(8,128)(2,1)S(1)} collective-permute-done((bf16[144,2048]{1,0:T(8,128)(2,1)S(1)}, bf16[144,2048]{1,0:T(8,128)(2,1)S(1)}, u32[]{:S(2)}, u32[]{:S(2)}) %collective-permute-start.3) | collective-permute-done | bytes 589856 | tf_op jit(solution)/shard_map/ppermute | solution.py:84
  50.4 1.9 collective-permute-start.4
  52.4 2.0 collective-permute-start.15
  54.5 3.4 collective-permute-done.14
  58.0 9.2 %collective-permute-done.15 = bf16[1,512]{1,0:T(2,128)(2,1)S(1)} collective-permute-done((bf16[1,512]{1,0:T(2,128)(2,1)S(1)}, bf16[1,512]{1,0:T(2,128)(2,1)S(1)}, u32[]{:S(2)}, u32[]{:S(2)}) %collective-permute-start.15) | collective-permute-done | bytes 1056 | tf_op jit(solution)/shard_map/ppermute | solution.py:25
  71.0 2.5 collective-permute-start.17
  73.5 2.8 collective-permute-done.4.refs_1_
  79.8 1.9 slice.369
  82.5 5.3 %collective-permute-done.17.refs_1_ = bf16[144,2048]{1,0:T(8,128)(2,1)S(1)} collective-permute-done((bf16[144,2048]{1,0:T(8,128)(2,1)}, bf16[144,2048]{1,0:T(8,128)(2,1)S(1)}, u32[]{:S(2)}, u32[]{:S(2)}) %collective-permute-start.17) | collective-permute-done | bytes 589856 | tf_op jit(solution)/shard_map/ppermute | solution.py:84
  91.9 3.2 collective-permute-done.10.refs_7_
  97.0 2.6 place.3
  101.2 7.9 %project.2 = (bf16[576,1024]{1,0:T(8,128)(2,1)}, bf16[1024,2048]{1,0:T(8,128)(2,1)}) custom-call(s32[10]{0:T(128)S(1)} %stack.190.where_ref, bf16[2,128,2048]{2,1,0:T(8,128)(2,1)} %pad_maximum_fusion.2.refs_0_, bf16[2,128,2048]{2,1,0:T(8,128)(2,1)} %collective-permute-done.4.refs_1_, bf16[2,128,2048]{2,1,0:T(8,128)(2,1)} %collective-permute-done.5.refs_2_, ...), custom_call_target="tpu_custom_call" | custom-call | flops 2415919104 | bytes 10747904 | tf_op jit(solution)/shard_map/project/pallas_call | solution.py:491
  111.8 3.0 multiply_convert_fusion.2
  117.1 2.0 collective-permute-start.23
  121.1 7.8 %project.3 = (f32[512,1024]{1,0:T(8,128)}, bf16[1024,2048]{1,0:T(8,128)(2,1)}) custom-call(s32[10]{0:T(128)S(1)} %stack.190.where_ref, bf16[2,128,2048]{2,1,0:T(8,128)(2,1)} %pad_maximum_fusion.2.refs_0_, bf16[2,128,2048]{2,1,0:T(8,128)(2,1)} %collective-permute-done.4.refs_1_, bf16[2,128,2048]{2,1,0:T(8,128)(2,1)} %collective-permute-done.5.refs_2_, ...), custom_call_target="tpu_custom_call" | custom-call | flops 2147483648 | bytes 10485760 | tf_op jit(solution)/shard_map/project/pallas_call | solution.py:491
  129.0 3.1 collective-permute-start.20
  132.3 3.1 convert_multiply_fusion.3
  135.4 11.6 %block_summary.1 = (bf16[4,16,1024]{2,1,0:T(8,128)(2,1)S(1)}, bf16[4,16,1024]{2,1,0:T(8,128)(2,1)S(1)}) custom-call(f32[16,512]{1,0:T(8,128)S(1)} %get-tuple-element.244.key_ref, f32[16,512]{1,0:T(8,128)S(1)} %broadcast_in_dim.63.keep_ref, f32[512,1024]{1,0:T(8,128)S(1)} %get-tuple-element.216.rate_ref, f32[512,1024]{1,0:T(8,128)S(1)} %get-tuple-element.215.feed_ref), custom_call_target="tpu_custom_call" | custom-call | flops 50331648 | bytes 4194304 | tf_op jit(solution)/shard_map/block_summary/pallas_call | solution.py:365
  147.8 19.9 %collective-permute-done.19.refs_2_ = bf16[128,2048]{1,0:T(8,128)(2,1)} collective-permute-done((bf16[128,2048]{1,0:T(8,128)(2,1)S(1)}, bf16[128,2048]{1,0:T(8,128)(2,1)}, u32[]{:S(2)}, u32[]{:S(2)}) %collective-permute-start.19) | collective-permute-done | bytes 524320 | tf_op jit(solution)/shard_map/ppermute | solution.py:25
  167.8 6.8 %join.1 = (f32[512,1024]{1,0:T(8,128)S(1)}, bf16[512,2048]{1,0:T(8,128)(2,1)}) custom-call(s32[4]{0:T(128)S(1)} %pad_add_fusion.2.where_ref, bf16[128,2048]{1,0:T(8,128)(2,1)S(1)} %bitcast.299, bf16[128,2048]{1,0:T(8,128)(2,1)} %collective-permute-done.18.refs_1_, bf16[128,2048]{1,0:T(8,128)(2,1)} %collective-permute-done.19.refs_2_, ...), custom_call_target="tpu_custom_call" | custom-call | flops 2147483648 | bytes 8388608 | tf_op jit(solution)/shard_map/join/pallas_call | solution.py:539
  176.2 15.2 %adjoint_summary.1 = bf16[4,16,1024]{2,1,0:T(8,128)(2,1)} custom-call(f32[16,512]{1,0:T(8,128)S(1)} %get-tuple-element.244.key_ref, f32[16,512]{1,0:T(8,128)S(1)} %get-tuple-element.242.query_ref, f32[16,512]{1,0:T(8,128)S(1)} %broadcast_in_dim.63.keep_ref, f32[512,1024]{1,0:T(8,128)S(1)} %get-tuple-element.216.rate_ref, ...), custom_call_target="tpu_custom_call" | custom-call | flops 50331648 | bytes 4194304 | tf_op jit(solution)/shard_map/adjoint_summary/pallas_call | solution.py:371
  192.9 11.0 %all-gather.8.cloned.1.call-done = bf16[16,4,16,1024]{3,2,1,0:T(8,128)(2,1)} async-done(((bf16[2,4,16,1024]{3,2,1,0:T(8,128)(2,1)}), bf16[16,4,16,1024]{3,2,1,0:T(8,128)(2,1)}) %all-gather.8.cloned.1.call-update) | async-done | bytes 2097168 | tf_op jit(solution)/shard_map/all_gather | solution.py:1021
  203.9 2.0 fusion.62.start_ref
  205.8 23.7 %states.1 = (f32[512,1024]{1,0:T(8,128)S(1)}, f32[4,1,128,16,1024]{4,3,2,1,0:T(8,128)}, f32[8,8192]{1,0:T(8,128)S(1)}) custom-call(f32[16,512]{1,0:T(8,128)S(1)} %get-tuple-element.244.key_ref, f32[16,512]{1,0:T(8,128)S(1)} %get-tuple-element.242.query_ref, f32[16,512]{1,0:T(8,128)S(1)} %broadcast_in_dim.63.keep_ref, ...), custom_call_target="tpu_custom_call" | custom-call | flops 83886080 | bytes 41943040 | tf_op jit(solution)/shard_map/states/pallas_call | solution.py:377
  230.9 4.4 multiply_convert_fusion
  235.3 6.8 %terms.2 = (f32[2,128,2048]{2,1,0:T(8,128)S(1)}, bf16[2,128,2048]{2,1,0:T(8,128)(2,1)}) custom-call(s32[4]{0:T(128)S(1)} %pad_add_fusion.5.where_ref, bf16[512,1024]{1,0:T(8,128)(2,1)S(1)} %get-tuple-element.222.one_ref.refs_0_, bf16[1024,2048]{1,0:T(8,128)(2,1)} %refs_1_.1), custom_call_target="tpu_custom_call" | custom-call | flops 2147483648 | bytes 8388608 | tf_op jit(solution)/shard_map/terms/pallas_call | solution.py:859
  243.4 8.7 %shares.1 = bf16[2,1024,2048]{2,1,0:T(8,128)(2,1)} custom-call(bf16[512,1024]{1,0:T(8,128)(2,1)S(1)} %get-tuple-element.222.one_ref.refs_0_, bf16[512,1024]{1,0:T(8,128)(2,1)S(1)} %get-tuple-element.221.two_ref.refs_1_, bf16[512,2048]{1,0:T(8,128)(2,1)S(1)} %copy-done.24, bf16[576,2048]{1,0:T(8,128)(2,1)} %copy-done.2), custom_call_target="tpu_custom_call" | custom-call | flops 4294967296 | bytes 12582912 | tf_op jit(solution)/shard_map/shares/pallas_call | solution.py:655
  255.7 36.0 %adjoints.1 = (f32[512,1024]{1,0:T(8,128)S(1)}, f32[512,1024]{1,0:T(8,128)S(1)}, f32[8,8192]{1,0:T(8,128)S(1)}) custom-call(f32[16,512]{1,0:T(8,128)S(1)} %get-tuple-element.244.key_ref, f32[16,512]{1,0:T(8,128)S(1)} %get-tuple-element.242.query_ref, f32[16,512]{1,0:T(8,128)S(1)} %broadcast_in_dim.63.keep_ref, f32[512,1024]{1,0:T(8,128)} %copy-done.4, ...), custom_call_target="tpu_custom_call" | custom-call | flops 167772160 | bytes 44040192 | tf_op jit(solution)/shard_map/adjoints/pallas_call | solution.py:394
  293.7 4.9 fusion.82
  301.8 2.4 collective-permute-start.26
  304.2 2.4 collective-permute-start.27
  306.7 2.0 fusion.23
  310.3 5.9 %collective-permute-done.26 = bf16[160,512]{1,0:T(8,128)(2,1)S(1)} collective-permute-done((bf16[160,512]{1,0:T(8,128)(2,1)S(1)}, bf16[160,512]{1,0:T(8,128)(2,1)S(1)}, u32[]{:S(2)}, u32[]{:S(2)}) %collective-permute-start.26) | collective-permute-done | bytes 163872 | tf_op jit(solution)/shard_map/ppermute | solution.py:25
  318.8 2.4 multiply_reduce_fusion
  329.8 2.5 fusion.27
  333.5 5.2 %concatenate.43 = f32[296,1024]{1,0:T(8,128)} concatenate(f32[160,1024]{1,0:T(8,128)} %fusion.90, f32[128,1024]{1,0:T(8,128)} %fusion.27, f32[1,1024]{1,0:T(1,128)S(1)} %bitcast.339, f32[1,1024]{1,0:T(1,128)S(1)} %bitcast.338, f32[1,1024]{1,0:T(1,128)S(1)} %bitcast.337, f32[1,1024]{1,0:T(1,128)S(1)} %bitcast.336, f32[1,1024]{1,0:T(1,128)S(1)} %bitcast.340, ...), dimensions={0} | concatenate | bytes 2424832 | tf_op jit(solution)/shard_map/concatenate | solution.py:1086
  342.4 2.3 fusion.86
  344.9 5.3 %stay_product.1 = (f32[2,2,160,1024]{3,2,1,0:T(8,128)}, bf16[2,2,160,1024]{3,2,1,0:T(8,128)(2,1)S(1)}) custom-call(s32[3]{0:T(128)S(1)} %pad_add_fusion.6.where_ref, bf16[512,1024]{1,0:T(8,128)(2,1)S(1)} %bitcast.293, bf16[576,2048]{1,0:T(8,128)(2,1)} %copy-done.2, bf16[512,2048]{1,0:T(8,128)(2,1)} %collective-permute-done.29.away_ref, ...), custom_call_target="tpu_custom_call" | custom-call | flops 1073741824 | bytes 10485760 | tf_op jit(solution)/shard_map/stay_product/pallas_call | solution.py:802
  353.3 3.0 collective-permute-start.35
  357.5 8.4 %terms.3 = (f32[2,128,2048]{2,1,0:T(8,128)S(1)}, bf16[2,128,2048]{2,1,0:T(8,128)(2,1)S(1)}, f32[8,2048]{1,0:T(8,128)S(1)}) custom-call(s32[4]{0:T(128)S(1)} %pad_add_fusion.5.where_ref, bf16[512,1024]{1,0:T(8,128)(2,1)S(1)} %bitcast.294, bf16[512,1024]{1,0:T(8,128)(2,1)S(1)} %copy-done.17, bf16[1024,2048]{1,0:T(8,128)(2,1)} %get-tuple-element.139.refs_2_, ...), custom_call_target="tpu_custom_call" | custom-call | flops 4294967296 | bytes 13631488 | tf_op jit(solution)/shard_map/terms/pallas_call | solution.py:859
  366.0 8.5 %collective-permute-done.31 = bf16[2,160,1024]{2,1,0:T(8,128)(2,1)} collective-permute-done((bf16[2,160,1024]{2,1,0:T(8,128)(2,1)}, bf16[2,160,1024]{2,1,0:T(8,128)(2,1)}, u32[]{:S(2)}, u32[]{:S(2)}) %collective-permute-start.31) | collective-permute-done | bytes 655392 | tf_op jit(solution)/shard_map/ppermute | solution.py:84
  375.8 2.0 bitcast_add_fusion
  379.7 2.1 fusion.10
  381.9 4.2 collective-permute-start.38
  386.1 8.1 %collective-permute-done.34 = bf16[160,1024]{1,0:T(8,128)(2,1)S(1)} collective-permute-done((bf16[160,1024]{1,0:T(8,128)(2,1)S(1)}, bf16[160,1024]{1,0:T(8,128)(2,1)S(1)}, u32[]{:S(2)}, u32[]{:S(2)}) %collective-permute-start.34) | collective-permute-done | bytes 327712 | tf_op jit(solution)/shard_map/ppermute | solution.py:84
  396.4 6.4 %collective-permute-start.40 = (bf16[128,2048]{1,0:T(8,128)(2,1)S(1)}, bf16[128,2048]{1,0:T(8,128)(2,1)S(1)}, u32[]{:S(2)}, u32[]{:S(2)}) collective-permute-start(bf16[128,2048]{1,0:T(8,128)(2,1)S(1)} %copy-done.46), channel_id=1, source_target_pairs={{0,2},{2,3},{4,6},{6,7},{8,10},{10,11},{12,14},{14,15},{16,18},{18... | collective-permute-start | bytes 1572872 | tf_op jit(solution)/shard_map/ppermute | solution.py:158
  403.5 15.8 %collective-permute-done.37 = bf16[128,2048]{1,0:T(8,128)(2,1)S(1)} collective-permute-done((bf16[128,2048]{1,0:T(8,128)(2,1)S(1)}, bf16[128,2048]{1,0:T(8,128)(2,1)S(1)}, u32[]{:S(2)}, u32[]{:S(2)}) %collective-permute-start.37) | collective-permute-done | bytes 524320 | tf_op jit(solution)/shard_map/ppermute | solution.py:158
  423.6 24.8 %collective-permute-done.42.refs_1_ = bf16[2,144,2048]{2,1,0:T(8,128)(2,1)} collective-permute-done((bf16[2,144,2048]{2,1,0:T(8,128)(2,1)}, bf16[2,144,2048]{2,1,0:T(8,128)(2,1)}, u32[]{:S(2)}, u32[]{:S(2)}) %collective-permute-start.42) | collective-permute-done | bytes 1179680 | tf_op jit(solution)/shard_map/ppermute | solution.py:84
  449.8 8.4 %collective-permute-start.47 = (bf16[1,512]{1,0:T(2,128)(2,1)S(1)}, bf16[1,512]{1,0:T(2,128)(2,1)S(1)}, u32[]{:S(2)}, u32[]{:S(2)}) collective-permute-start(bf16[1,512]{1,0:T(2,128)(2,1)S(1)} %get-tuple-element.245), channel_id=1, source_target_pairs={{0,1},{1,2},{2,3},{3,0},{4,5},{5,6},{6,7},{7,4},{8,9},{9,10},{10,1... | collective-permute-start | bytes 3080 | tf_op jit(solution)/shard_map/ppermute | solution.py:25
  458.2 2.0 collective-permute-start.48
  460.2 3.2 collective-permute-start.49
  463.4 1.9 fusion.24
  467.3 2.3 collective-permute-done.50
  470.8 2.4 collective-permute-done.51
  473.4 1.9 slice.404
  475.3 1.9 slice.405
  480.3 8.5 %widen.2 = (f32[2,8,128,2048]{3,2,1,0:T(8,128)}, f32[2,8,16,2048]{3,2,1,0:T(8,128)}) custom-call(s32[6]{0:T(128)S(1)} %stack.221.where_ref, bf16[2,144,2048]{2,1,0:T(8,128)(2,1)} %pad_maximum_fusion.1.refs_0_, bf16[2,144,2048]{2,1,0:T(8,128)(2,1)} %collective-permute-done.42.refs_1_, bf16[2,144,2048]{2,1,0:T(8,128)(2,1)} %collective-permute-done.43.refs_2_, ...), custom_call_target="tpu_custom_call" | custom-call | bytes 21233664 | tf_op jit(solution)/shard_map/widen/pallas_call | solution.py:608
  491.4 7.4 %reorder.1 = f32[1024,2048]{1,0:T(8,128)} custom-call(bf16[8,128,2048]{2,1,0:T(8,128)(2,1)} %all-gather.6.cloned.1.call-done.in_ref), custom_call_target="tpu_custom_call" | custom-call | bytes 12582912 | tf_op jit(solution)/shard_map/reorder/pallas_call | solution.py:888
  499.4 2.7 fusion.25
  502.1 3.7 widen.3
  (340 shorter events, 91.6 us)
Async XLA Ops:
  7.2 107.5 %copy-start = (bf16[1024,160]{0,1:T(8,128)(2,1)S(1)}, bf16[1024,160]{0,1:T(8,128)(2,1)}, u32[]{:S(2)}) copy-start(bf16[1024,160]{0,1:T(8,128)(2,1)} %param.18) | copy-start | bytes 983044
  7.2 196.7 %all-gather.8.cloned.1.call-start = ((), (), s32[]{:S(2)}) async-start(), calls=%async_computation.3 | async-start | bytes 2359296 | tf_op jit(solution)/shard_map/all_gather | solution.py:1021
  10.2 8.5 %collective-permute-start.2 = (bf16[4,2048]{1,0:T(4,128)(2,1)S(1)}, bf16[4,2048]{1,0:T(4,128)(2,1)S(1)}, u32[]{:S(2)}, u32[]{:S(2)}) collective-permute-start(bf16[4,2048]{1,0:T(4,128)(2,1)S(1)} %pad_maximum_fusion.6), channel_id=1, source_target_pairs={{0,4},{4,8},{8,12},{12,16},{16,20},{20,24},{24,28},{1,5},{5,9},{9,... | collective-permute-start | bytes 49160 | tf_op jit(solution)/shard_map/ppermute | solution.py:135
  12.6 8.3 %collective-permute-start = (bf16[128,2048]{1,0:T(8,128)(2,1)S(1)}, bf16[128,2048]{1,0:T(8,128)(2,1)S(1)}, u32[]{:S(2)}, u32[]{:S(2)}) collective-permute-start(bf16[128,2048]{1,0:T(8,128)(2,1)S(1)} %get-tuple-element.240), channel_id=1, source_target_pairs={{0,0},{1,2},{2,1},{3,3},{4,4},{5,6},{6,5},{7,7},{8,8},{9,10},{10,9... | collective-permute-start | bytes 1572872 | tf_op jit(solution)/shard_map/ppermute | solution.py:141
  13.3 28.5 %collective-permute-start.1 = (bf16[128,2048]{1,0:T(8,128)(2,1)S(1)}, bf16[128,2048]{1,0:T(8,128)(2,1)}, u32[]{:S(2)}, u32[]{:S(2)}) collective-permute-start(bf16[128,2048]{1,0:T(8,128)(2,1)S(1)} %get-tuple-element.241), channel_id=1, source_target_pairs={{0,1},{1,3},{2,0},{3,2},{4,5},{5,7},{6,4},{7,6},{8,9},{9,11},{10,8... | collective-permute-start | bytes 1572872 | tf_op jit(solution)/shard_map/ppermute | solution.py:146
  19.0 30.3 %collective-permute-start.3 = (bf16[144,2048]{1,0:T(8,128)(2,1)S(1)}, bf16[144,2048]{1,0:T(8,128)(2,1)S(1)}, u32[]{:S(2)}, u32[]{:S(2)}) collective-permute-start(bf16[144,2048]{1,0:T(8,128)(2,1)S(1)} %maximum_maximum_fusion.refs_0_), channel_id=1, source_target_pairs={{0,1},{1,0},{2,3},{3,2},{4,5},{5,4},{6,7},{7,6},{8,9},{9,8},{10,11... | collective-permute-start | bytes 1769480 | tf_op jit(solution)/shard_map/ppermute | solution.py:84
  19.0 33.3 %copy-start.68 = (bf16[512]{0:T(512)(128)(2,1)S(1)}, bf16[512]{0:T(512)(128)(2,1)}, u32[]{:S(2)}) copy-start(bf16[512]{0:T(512)(128)(2,1)} %param.14) | copy-start | bytes 3076
  19.1 51.9 %collective-permute-start.13 = (bf16[144,2048]{1,0:T(8,128)(2,1)S(1)}, bf16[144,2048]{1,0:T(8,128)(2,1)}, u32[]{:S(2)}, u32[]{:S(2)}) collective-permute-start(bf16[144,2048]{1,0:T(8,128)(2,1)S(1)} %maximum_maximum_fusion.refs_0_), channel_id=1, source_target_pairs={{0,2},{1,3},{2,0},{3,1},{4,6},{5,7},{6,4},{7,5},{8,10},{9,11},{10,... | collective-permute-start | bytes 1769480 | tf_op jit(solution)/shard_map/ppermute | solution.py:84
  50.4 25.8 %collective-permute-start.4 = (bf16[2,128,2048]{2,1,0:T(8,128)(2,1)}, bf16[2,128,2048]{2,1,0:T(8,128)(2,1)}, u32[]{:S(2)}, u32[]{:S(2)}) collective-permute-start(bf16[2,128,2048]{2,1,0:T(8,128)(2,1)} %pad_maximum_fusion.2.refs_0_), channel_id=1, source_target_pairs={{0,16},{4,20},{8,24},{12,28},{16,0},{20,4},{24,8},{28,12},{1,17},{... | collective-permute-start | bytes 3145736 | tf_op jit(solution)/shard_map/ppermute | solution.py:84
  52.3 27.5 %collective-permute-start.5 = (bf16[2,128,2048]{2,1,0:T(8,128)(2,1)}, bf16[2,128,2048]{2,1,0:T(8,128)(2,1)}, u32[]{:S(2)}, u32[]{:S(2)}) collective-permute-start(bf16[2,128,2048]{2,1,0:T(8,128)(2,1)} %pad_maximum_fusion.2.refs_0_), channel_id=1, source_target_pairs={{0,8},{4,12},{8,0},{12,4},{16,24},{20,28},{24,16},{28,20},{1,9},{5... | collective-permute-start | bytes 3145736 | tf_op jit(solution)/shard_map/ppermute | solution.py:84
  52.3 5.6 %collective-permute-start.14 = (bf16[1,512]{1,0:T(2,128)(2,1)S(1)}, bf16[1,512]{1,0:T(2,128)(2,1)S(1)}, u32[]{:S(2)}, u32[]{:S(2)}) collective-permute-start(bf16[1,512]{1,0:T(2,128)(2,1)S(1)} %broadcast_in_dim.58), channel_id=1, source_target_pairs={{0,1},{1,2},{2,3},{3,0},{4,5},{5,6},{6,7},{7,4},{8,9},{9,10},{10,1... | collective-permute-start | bytes 3080 | tf_op jit(solution)/shard_map/ppermute | solution.py:25
  52.4 14.8 %collective-permute-start.15 = (bf16[1,512]{1,0:T(2,128)(2,1)S(1)}, bf16[1,512]{1,0:T(2,128)(2,1)S(1)}, u32[]{:S(2)}, u32[]{:S(2)}) collective-permute-start(bf16[1,512]{1,0:T(2,128)(2,1)S(1)} %broadcast_in_dim.58), channel_id=1, source_target_pairs={{0,2},{1,3},{2,0},{3,1},{4,6},{5,7},{6,4},{7,5},{8,10},{9,11},{10,... | collective-permute-start | bytes 3080 | tf_op jit(solution)/shard_map/ppermute | solution.py:25
  57.9 10.4 %collective-permute-start.16 = (bf16[1,512]{1,0:T(2,128)(2,1)S(1)}, bf16[1,512]{1,0:T(2,128)(2,1)S(1)}, u32[]{:S(2)}, u32[]{:S(2)}) collective-permute-start(bf16[1,512]{1,0:T(2,128)(2,1)S(1)} %broadcast_in_dim.58), channel_id=1, source_target_pairs={{0,3},{1,0},{2,1},{3,2},{4,7},{5,4},{6,5},{7,6},{8,11},{9,8},{10,9... | collective-permute-start | bytes 3080 | tf_op jit(solution)/shard_map/ppermute | solution.py:25
  71.0 16.8 %collective-permute-start.17 = (bf16[144,2048]{1,0:T(8,128)(2,1)}, bf16[144,2048]{1,0:T(8,128)(2,1)S(1)}, u32[]{:S(2)}, u32[]{:S(2)}) collective-permute-start(bf16[144,2048]{1,0:T(8,128)(2,1)} %collective-permute-done.13.refs_0_), channel_id=1, source_target_pairs={{0,1},{1,0},{2,3},{3,2},{4,5},{5,4},{6,7},{7,6},{8,9},{9,8},{10,11... | collective-permute-start | bytes 1769480 | tf_op jit(solution)/shard_map/ppermute | solution.py:84
  78.1 13.7 %collective-permute-start.9 = (bf16[2,128,1024]{2,1,0:T(8,128)(2,1)}, bf16[2,128,1024]{2,1,0:T(8,128)(2,1)S(1)}, u32[]{:S(2)}, u32[]{:S(2)}) collective-permute-start(bf16[2,128,1024]{2,1,0:T(8,128)(2,1)} %slice.368), channel_id=1, source_target_pairs={{0,8},{4,12},{8,0},{12,4},{16,24},{20,28},{24,16},{28,20},{1,9},{5... | collective-permute-start | bytes 1572872 | tf_op jit(solution)/shard_map/ppermute | solution.py:84
  81.7 13.3 %collective-permute-start.10 = (bf16[2,128,1024]{2,1,0:T(8,128)(2,1)}, bf16[2,128,1024]{2,1,0:T(8,128)(2,1)}, u32[]{:S(2)}, u32[]{:S(2)}) collective-permute-start(bf16[2,128,1024]{2,1,0:T(8,128)(2,1)} %slice.369), channel_id=1, source_target_pairs={{0,16},{4,20},{8,24},{12,28},{16,0},{20,4},{24,8},{28,12},{1,17},{... | collective-permute-start | bytes 1572872 | tf_op jit(solution)/shard_map/ppermute | solution.py:84
  82.0 19.2 %collective-permute-start.6 = (bf16[2,128,2048]{2,1,0:T(8,128)(2,1)}, bf16[2,128,2048]{2,1,0:T(8,128)(2,1)}, u32[]{:S(2)}, u32[]{:S(2)}) collective-permute-start(bf16[2,128,2048]{2,1,0:T(8,128)(2,1)} %pad_maximum_fusion.2.refs_0_), channel_id=1, source_target_pairs={{0,4},{4,0},{8,12},{12,8},{16,20},{20,16},{24,28},{28,24},{1,5},{5... | collective-permute-start | bytes 3145736 | tf_op jit(solution)/shard_map/ppermute | solution.py:84
  82.0 19.2 %collective-permute-start.7 = (bf16[2,128,2048]{2,1,0:T(8,128)(2,1)}, bf16[2,128,2048]{2,1,0:T(8,128)(2,1)}, u32[]{:S(2)}, u32[]{:S(2)}) collective-permute-start(bf16[2,128,2048]{2,1,0:T(8,128)(2,1)} %collective-permute-done.4.refs_1_), channel_id=1, source_target_pairs={{0,4},{4,0},{8,12},{12,8},{16,20},{20,16},{24,28},{28,24},{1,5},{5... | collective-permute-start | bytes 3145736 | tf_op jit(solution)/shard_map/ppermute | solution.py:84
  88.6 12.6 %collective-permute-start.8 = (bf16[2,128,2048]{2,1,0:T(8,128)(2,1)}, bf16[2,128,2048]{2,1,0:T(8,128)(2,1)}, u32[]{:S(2)}, u32[]{:S(2)}) collective-permute-start(bf16[2,128,2048]{2,1,0:T(8,128)(2,1)} %collective-permute-done.5.refs_2_), channel_id=1, source_target_pairs={{0,4},{4,0},{8,12},{12,8},{16,20},{20,16},{24,28},{28,24},{1,5},{5... | collective-permute-start | bytes 3145736 | tf_op jit(solution)/shard_map/ppermute | solution.py:84
  91.9 9.3 %collective-permute-start.11 = (bf16[2,128,1024]{2,1,0:T(8,128)(2,1)S(1)}, bf16[2,128,1024]{2,1,0:T(8,128)(2,1)S(1)}, u32[]{:S(2)}, u32[]{:S(2)}) collective-permute-start(bf16[2,128,1024]{2,1,0:T(8,128)(2,1)S(1)} %collective-permute-done.9.refs_6_), channel_id=1, source_target_pairs={{0,4},{4,0},{8,12},{12,8},{16,20},{20,16},{24,28},{28,24},{1,5},{5... | collective-permute-start | bytes 1572872 | tf_op jit(solution)/shard_map/ppermute | solution.py:84
  95.0 6.2 %collective-permute-start.12 = (bf16[2,128,1024]{2,1,0:T(8,128)(2,1)}, bf16[2,128,1024]{2,1,0:T(8,128)(2,1)S(1)}, u32[]{:S(2)}, u32[]{:S(2)}) collective-permute-start(bf16[2,128,1024]{2,1,0:T(8,128)(2,1)} %collective-permute-done.10.refs_7_), channel_id=1, source_target_pairs={{0,4},{4,0},{8,12},{12,8},{16,20},{20,16},{24,28},{28,24},{1,5},{5... | collective-permute-start | bytes 1572872 | tf_op jit(solution)/shard_map/ppermute | solution.py:84
  115.2 13.7 %collective-permute-start.21 = (bf16[160,512]{1,0:T(8,128)(2,1)S(1)}, bf16[160,512]{1,0:T(8,128)(2,1)S(1)}, u32[]{:S(2)}, u32[]{:S(2)}) collective-permute-start(bf16[160,512]{1,0:T(8,128)(2,1)S(1)} %get-tuple-element.104), channel_id=1, source_target_pairs={{0,1},{1,2},{2,3},{3,0},{4,5},{5,6},{6,7},{7,4},{8,9},{9,10},{10,1... | collective-permute-start | bytes 491528 | tf_op jit(solution)/shard_map/ppermute | solution.py:25
  115.3 16.8 %collective-permute-start.22 = (bf16[160,512]{1,0:T(8,128)(2,1)S(1)}, bf16[160,512]{1,0:T(8,128)(2,1)S(1)}, u32[]{:S(2)}, u32[]{:S(2)}) collective-permute-start(bf16[160,512]{1,0:T(8,128)(2,1)S(1)} %get-tuple-element.104), channel_id=1, source_target_pairs={{0,2},{1,3},{2,0},{3,1},{4,6},{5,7},{6,4},{7,5},{8,10},{9,11},{10,... | collective-permute-start | bytes 491528 | tf_op jit(solution)/shard_map/ppermute | solution.py:25
  117.1 15.0 %collective-permute-start.23 = (bf16[160,512]{1,0:T(8,128)(2,1)S(1)}, bf16[160,512]{1,0:T(8,128)(2,1)S(1)}, u32[]{:S(2)}, u32[]{:S(2)}) collective-permute-start(bf16[160,512]{1,0:T(8,128)(2,1)S(1)} %get-tuple-element.104), channel_id=1, source_target_pairs={{0,3},{1,0},{2,1},{3,2},{4,7},{5,4},{6,5},{7,6},{8,11},{9,8},{10,9... | collective-permute-start | bytes 491528 | tf_op jit(solution)/shard_map/ppermute | solution.py:25
  119.1 28.6 %collective-permute-start.18 = (bf16[128,2048]{1,0:T(8,128)(2,1)S(1)}, bf16[128,2048]{1,0:T(8,128)(2,1)}, u32[]{:S(2)}, u32[]{:S(2)}) collective-permute-start(bf16[128,2048]{1,0:T(8,128)(2,1)S(1)} %bitcast.296), channel_id=1, source_target_pairs={{0,1},{1,2},{2,3},{3,0},{4,5},{5,6},{6,7},{7,4},{8,9},{9,10},{10,1... | collective-permute-start | bytes 1572872 | tf_op jit(solution)/shard_map/ppermute | solution.py:25
  119.7 48.0 %collective-permute-start.19 = (bf16[128,2048]{1,0:T(8,128)(2,1)S(1)}, bf16[128,2048]{1,0:T(8,128)(2,1)}, u32[]{:S(2)}, u32[]{:S(2)}) collective-permute-start(bf16[128,2048]{1,0:T(8,128)(2,1)S(1)} %bitcast.297), channel_id=1, source_target_pairs={{0,2},{1,3},{2,0},{3,1},{4,6},{5,7},{6,4},{7,5},{8,10},{9,11},{10,... | collective-permute-start | bytes 1572872 | tf_op jit(solution)/shard_map/ppermute | solution.py:25
  129.0 38.7 %collective-permute-start.20 = (bf16[128,2048]{1,0:T(8,128)(2,1)S(1)}, bf16[128,2048]{1,0:T(8,128)(2,1)}, u32[]{:S(2)}, u32[]{:S(2)}) collective-permute-start(bf16[128,2048]{1,0:T(8,128)(2,1)S(1)} %bitcast.298), channel_id=1, source_target_pairs={{0,3},{1,0},{2,1},{3,2},{4,7},{5,4},{6,5},{7,6},{8,11},{9,8},{10,9... | collective-permute-start | bytes 1572872 | tf_op jit(solution)/shard_map/ppermute | solution.py:25
  135.3 70.5 %copy-start.4 = (f32[512,1024]{1,0:T(8,128)}, f32[512,1024]{1,0:T(8,128)S(1)}, u32[]{:S(2)}) copy-start(f32[512,1024]{1,0:T(8,128)S(1)} %get-tuple-element.216.rate_ref) | copy-start | bytes 6291460
  167.7 63.2 %all-gather.10.cloned.1.call-start = ((), (), s32[]{:S(2)}) async-start(), calls=%async_computation.4 | async-start | bytes 1179648 | tf_op jit(solution)/shard_map/all_gather | solution.py:1027
  192.7 149.7 %reduce-scatter.2.cloned.1.call-start = ((), (), s32[]{:S(2)}) async-start(), calls=%async_computation.1 | async-start | bytes 9437184 | tf_op jit(solution)/shard_map/reduce_scatter | solution.py:1047
  253.9 237.6 %all-gather.6.cloned.1.call-start = ((), (), s32[]{:S(2)}) async-start(), calls=%async_computation.2 | async-start | bytes 4718592 | tf_op jit(solution)/shard_map/all_gather | solution.py:1141
  254.1 38.9 %collective-permute-start.24 = (bf16[2,128,2048]{2,1,0:T(8,128)(2,1)}, bf16[2,128,2048]{2,1,0:T(8,128)(2,1)}, u32[]{:S(2)}, u32[]{:S(2)}) collective-permute-start(bf16[2,128,2048]{2,1,0:T(8,128)(2,1)} %get-tuple-element.127), channel_id=1, source_target_pairs={{0,1},{1,0},{2,3},{3,2},{4,5},{5,4},{6,7},{7,6},{8,9},{9,8},{10,11... | collective-permute-start | bytes 3145736 | tf_op jit(solution)/shard_map/ppermute | solution.py:84
  301.3 9.0 %collective-permute-start.25 = (bf16[160,512]{1,0:T(8,128)(2,1)S(1)}, bf16[160,512]{1,0:T(8,128)(2,1)S(1)}, u32[]{:S(2)}, u32[]{:S(2)}) collective-permute-start(bf16[160,512]{1,0:T(8,128)(2,1)S(1)} %fusion.65), channel_id=1, source_target_pairs={{0,1},{1,2},{2,3},{3,0},{4,5},{5,6},{6,7},{7,4},{8,9},{9,10},{10,1... | collective-permute-start | bytes 491528 | tf_op jit(solution)/shard_map/ppermute | solution.py:25
  301.8 14.4 %collective-permute-start.26 = (bf16[160,512]{1,0:T(8,128)(2,1)S(1)}, bf16[160,512]{1,0:T(8,128)(2,1)S(1)}, u32[]{:S(2)}, u32[]{:S(2)}) collective-permute-start(bf16[160,512]{1,0:T(8,128)(2,1)S(1)} %fusion.65), channel_id=1, source_target_pairs={{0,2},{1,3},{2,0},{3,1},{4,6},{5,7},{6,4},{7,5},{8,10},{9,11},{10,... | collective-permute-start | bytes 491528 | tf_op jit(solution)/shard_map/ppermute | solution.py:25
  304.2 12.0 %collective-permute-start.27 = (bf16[160,512]{1,0:T(8,128)(2,1)S(1)}, bf16[160,512]{1,0:T(8,128)(2,1)S(1)}, u32[]{:S(2)}, u32[]{:S(2)}) collective-permute-start(bf16[160,512]{1,0:T(8,128)(2,1)S(1)} %fusion.65), channel_id=1, source_target_pairs={{0,3},{1,0},{2,1},{3,2},{4,7},{5,4},{6,5},{7,6},{8,11},{9,8},{10,9... | collective-permute-start | bytes 491528 | tf_op jit(solution)/shard_map/ppermute | solution.py:25
  322.1 3.1 collective-permute-start.28
  328.4 16.5 %collective-permute-start.29 = (bf16[512,2048]{1,0:T(8,128)(2,1)S(1)}, bf16[512,2048]{1,0:T(8,128)(2,1)}, u32[]{:S(2)}, u32[]{:S(2)}) collective-permute-start(bf16[512,2048]{1,0:T(8,128)(2,1)S(1)} %away_product.1), channel_id=1, source_target_pairs={{0,4},{4,0},{8,12},{12,8},{16,20},{20,16},{24,28},{28,24},{1,5},{5... | collective-permute-start | bytes 6291464 | tf_op jit(solution)/shard_map/ppermute | solution.py:84
  342.4 2.5 collective-permute-start.30
  351.4 23.1 %collective-permute-start.31 = (bf16[2,160,1024]{2,1,0:T(8,128)(2,1)}, bf16[2,160,1024]{2,1,0:T(8,128)(2,1)}, u32[]{:S(2)}, u32[]{:S(2)}) collective-permute-start(bf16[2,160,1024]{2,1,0:T(8,128)(2,1)} %get-tuple-element.235), channel_id=1, source_target_pairs={{0,8},{4,12},{8,0},{12,4},{16,24},{20,28},{24,16},{28,20},{1,9},{5... | collective-permute-start | bytes 1966088 | tf_op jit(solution)/shard_map/ppermute | solution.py:84
  353.0 22.8 %collective-permute-start.32 = (bf16[2,160,1024]{2,1,0:T(8,128)(2,1)}, bf16[2,160,1024]{2,1,0:T(8,128)(2,1)}, u32[]{:S(2)}, u32[]{:S(2)}) collective-permute-start(bf16[2,160,1024]{2,1,0:T(8,128)(2,1)} %get-tuple-element.234), channel_id=1, source_target_pairs={{0,16},{4,20},{8,24},{12,28},{16,0},{20,4},{24,8},{28,12},{1,17},{... | collective-permute-start | bytes 1966088 | tf_op jit(solution)/shard_map/ppermute | solution.py:84
  353.3 26.4 %collective-permute-start.35 = (bf16[128,2048]{1,0:T(8,128)(2,1)}, bf16[128,2048]{1,0:T(8,128)(2,1)S(1)}, u32[]{:S(2)}, u32[]{:S(2)}) collective-permute-start(bf16[128,2048]{1,0:T(8,128)(2,1)} %fusion.23), channel_id=1, source_target_pairs={{0,2},{1,3},{2,0},{3,1},{4,6},{5,7},{6,4},{7,5},{8,10},{9,11},{10,... | collective-permute-start | bytes 1572872 | tf_op jit(solution)/shard_map/ppermute | solution.py:84
  377.9 16.3 %collective-permute-start.34 = (bf16[160,1024]{1,0:T(8,128)(2,1)S(1)}, bf16[160,1024]{1,0:T(8,128)(2,1)S(1)}, u32[]{:S(2)}, u32[]{:S(2)}) collective-permute-start(bf16[160,1024]{1,0:T(8,128)(2,1)S(1)} %fusion.32), channel_id=1, source_target_pairs={{0,8},{4,12},{8,0},{12,4},{16,24},{20,28},{24,16},{28,20},{1,9},{5... | collective-permute-start | bytes 983048 | tf_op jit(solution)/shard_map/ppermute | solution.py:84
  378.4 15.8 %collective-permute-start.33 = (bf16[160,1024]{1,0:T(8,128)(2,1)S(1)}, bf16[160,1024]{1,0:T(8,128)(2,1)S(1)}, u32[]{:S(2)}, u32[]{:S(2)}) collective-permute-start(bf16[160,1024]{1,0:T(8,128)(2,1)S(1)} %fusion.31), channel_id=1, source_target_pairs={{0,16},{4,20},{8,24},{12,28},{16,0},{20,4},{24,8},{28,12},{1,17},{... | collective-permute-start | bytes 983048 | tf_op jit(solution)/shard_map/ppermute | solution.py:84
  381.9 37.4 %collective-permute-start.38 = (bf16[2,128,2048]{2,1,0:T(8,128)(2,1)S(1)}, bf16[2,128,2048]{2,1,0:T(8,128)(2,1)S(1)}, u32[]{:S(2)}, u32[]{:S(2)}) collective-permute-start(bf16[2,128,2048]{2,1,0:T(8,128)(2,1)S(1)} %get-tuple-element.151), channel_id=1, source_target_pairs={{0,1},{1,0},{2,3},{3,2},{4,5},{5,4},{6,7},{7,6},{8,9},{9,8},{10,11... | collective-permute-start | bytes 3145736 | tf_op jit(solution)/shard_map/ppermute | solution.py:84
  394.4 9.1 %collective-permute-start.36 = (bf16[128,2048]{1,0:T(8,128)(2,1)S(1)}, bf16[128,2048]{1,0:T(8,128)(2,1)S(1)}, u32[]{:S(2)}, u32[]{:S(2)}) collective-permute-start(bf16[128,2048]{1,0:T(8,128)(2,1)S(1)} %fusion.22), channel_id=1, source_target_pairs={{0,0},{2,1},{4,4},{6,5},{8,8},{10,9},{12,12},{14,13},{16,16},{18,1... | collective-permute-start | bytes 1572872 | tf_op jit(solution)/shard_map/ppermute | solution.py:158
  395.1 24.2 %collective-permute-start.37 = (bf16[128,2048]{1,0:T(8,128)(2,1)S(1)}, bf16[128,2048]{1,0:T(8,128)(2,1)S(1)}, u32[]{:S(2)}, u32[]{:S(2)}) collective-permute-start(bf16[128,2048]{1,0:T(8,128)(2,1)S(1)} %fusion.22), channel_id=1, source_target_pairs={{1,0},{3,1},{5,4},{7,5},{9,8},{11,9},{13,12},{15,13},{17,16},{19,1... | collective-permute-start | bytes 1572872 | tf_op jit(solution)/shard_map/ppermute | solution.py:158
  396.4 22.9 %collective-permute-start.40 = (bf16[128,2048]{1,0:T(8,128)(2,1)S(1)}, bf16[128,2048]{1,0:T(8,128)(2,1)S(1)}, u32[]{:S(2)}, u32[]{:S(2)}) collective-permute-start(bf16[128,2048]{1,0:T(8,128)(2,1)S(1)} %copy-done.46), channel_id=1, source_target_pairs={{0,2},{2,3},{4,6},{6,7},{8,10},{10,11},{12,14},{14,15},{16,18},{18... | collective-permute-start | bytes 1572872 | tf_op jit(solution)/shard_map/ppermute | solution.py:158
  402.8 16.7 %collective-permute-start.41 = (bf16[128,2048]{1,0:T(8,128)(2,1)S(1)}, bf16[128,2048]{1,0:T(8,128)(2,1)S(1)}, u32[]{:S(2)}, u32[]{:S(2)}) collective-permute-start(bf16[128,2048]{1,0:T(8,128)(2,1)S(1)} %copy-done.46), channel_id=1, source_target_pairs={{1,2},{3,3},{5,6},{7,7},{9,10},{11,11},{13,14},{15,15},{17,18},{19... | collective-permute-start | bytes 1572872 | tf_op jit(solution)/shard_map/ppermute | solution.py:158
  421.4 26.9 %collective-permute-start.42 = (bf16[2,144,2048]{2,1,0:T(8,128)(2,1)}, bf16[2,144,2048]{2,1,0:T(8,128)(2,1)}, u32[]{:S(2)}, u32[]{:S(2)}) collective-permute-start(bf16[2,144,2048]{2,1,0:T(8,128)(2,1)} %pad_maximum_fusion.1.refs_0_), channel_id=1, source_target_pairs={{0,16},{4,20},{8,24},{12,28},{16,0},{20,4},{24,8},{28,12},{1,17},{... | collective-permute-start | bytes 3538952 | tf_op jit(solution)/shard_map/ppermute | solution.py:84
  423.1 26.7 %collective-permute-start.43 = (bf16[2,144,2048]{2,1,0:T(8,128)(2,1)}, bf16[2,144,2048]{2,1,0:T(8,128)(2,1)}, u32[]{:S(2)}, u32[]{:S(2)}) collective-permute-start(bf16[2,144,2048]{2,1,0:T(8,128)(2,1)} %pad_maximum_fusion.1.refs_0_), channel_id=1, source_target_pairs={{0,8},{4,12},{8,0},{12,4},{16,24},{20,28},{24,16},{28,20},{1,9},{5... | collective-permute-start | bytes 3538952 | tf_op jit(solution)/shard_map/ppermute | solution.py:84
  423.5 54.9 %collective-permute-start.44 = (bf16[2,144,2048]{2,1,0:T(8,128)(2,1)}, bf16[2,144,2048]{2,1,0:T(8,128)(2,1)}, u32[]{:S(2)}, u32[]{:S(2)}) collective-permute-start(bf16[2,144,2048]{2,1,0:T(8,128)(2,1)} %pad_maximum_fusion.1.refs_0_), channel_id=1, source_target_pairs={{0,4},{4,0},{8,12},{12,8},{16,20},{20,16},{24,28},{28,24},{1,5},{5... | collective-permute-start | bytes 3538952 | tf_op jit(solution)/shard_map/ppermute | solution.py:84
  448.4 31.9 %collective-permute-start.45 = (bf16[2,144,2048]{2,1,0:T(8,128)(2,1)}, bf16[2,144,2048]{2,1,0:T(8,128)(2,1)}, u32[]{:S(2)}, u32[]{:S(2)}) collective-permute-start(bf16[2,144,2048]{2,1,0:T(8,128)(2,1)} %collective-permute-done.42.refs_1_), channel_id=1, source_target_pairs={{0,4},{4,0},{8,12},{12,8},{16,20},{20,16},{24,28},{28,24},{1,5},{5... | collective-permute-start | bytes 3538952 | tf_op jit(solution)/shard_map/ppermute | solution.py:84
  449.8 30.4 %collective-permute-start.46 = (bf16[2,144,2048]{2,1,0:T(8,128)(2,1)}, bf16[2,144,2048]{2,1,0:T(8,128)(2,1)}, u32[]{:S(2)}, u32[]{:S(2)}) collective-permute-start(bf16[2,144,2048]{2,1,0:T(8,128)(2,1)} %collective-permute-done.43.refs_2_), channel_id=1, source_target_pairs={{0,4},{4,0},{8,12},{12,8},{16,20},{20,16},{24,28},{28,24},{1,5},{5... | collective-permute-start | bytes 3538952 | tf_op jit(solution)/shard_map/ppermute | solution.py:84
  449.8 10.4 %collective-permute-start.47 = (bf16[1,512]{1,0:T(2,128)(2,1)S(1)}, bf16[1,512]{1,0:T(2,128)(2,1)S(1)}, u32[]{:S(2)}, u32[]{:S(2)}) collective-permute-start(bf16[1,512]{1,0:T(2,128)(2,1)S(1)} %get-tuple-element.245), channel_id=1, source_target_pairs={{0,1},{1,2},{2,3},{3,0},{4,5},{5,6},{6,7},{7,4},{8,9},{9,10},{10,1... | collective-permute-start | bytes 3080 | tf_op jit(solution)/shard_map/ppermute | solution.py:25
  458.2 7.2 %collective-permute-start.48 = (bf16[1,512]{1,0:T(2,128)(2,1)S(1)}, bf16[1,512]{1,0:T(2,128)(2,1)S(1)}, u32[]{:S(2)}, u32[]{:S(2)}) collective-permute-start(bf16[1,512]{1,0:T(2,128)(2,1)S(1)} %get-tuple-element.247), channel_id=1, source_target_pairs={{0,2},{1,3},{2,0},{3,1},{4,6},{5,7},{6,4},{7,5},{8,10},{9,11},{10,... | collective-permute-start | bytes 3080 | tf_op jit(solution)/shard_map/ppermute | solution.py:25
  460.2 5.7 %collective-permute-start.49 = (bf16[1,512]{1,0:T(2,128)(2,1)S(1)}, bf16[1,512]{1,0:T(2,128)(2,1)S(1)}, u32[]{:S(2)}, u32[]{:S(2)}) collective-permute-start(bf16[1,512]{1,0:T(2,128)(2,1)S(1)} %get-tuple-element.246), channel_id=1, source_target_pairs={{0,3},{1,0},{2,1},{3,2},{4,7},{5,4},{6,5},{7,6},{8,11},{9,8},{10,9... | collective-permute-start | bytes 3080 | tf_op jit(solution)/shard_map/ppermute | solution.py:25
  465.4 24.5 %collective-permute-start.39 = (bf16[128,2048]{1,0:T(8,128)(2,1)}, bf16[128,2048]{1,0:T(8,128)(2,1)}, u32[]{:S(2)}, u32[]{:S(2)}) collective-permute-start(bf16[128,2048]{1,0:T(8,128)(2,1)} %fusion.24), channel_id=1, source_target_pairs={{0,2},{1,3},{2,0},{3,1},{4,6},{5,7},{6,4},{7,5},{8,10},{9,11},{10,... | collective-permute-start | bytes 1572872 | tf_op jit(solution)/shard_map/ppermute | solution.py:84
  466.0 3.7 collective-permute-start.50
  469.6 3.6 collective-permute-start.51
  473.2 4.0 collective-permute-start.52
  477.2 21.6 %collective-permute-start.53 = (bf16[2,144,1024]{2,1,0:T(8,128)(2,1)}, bf16[2,144,1024]{2,1,0:T(8,128)(2,1)S(1)}, u32[]{:S(2)}, u32[]{:S(2)}) collective-permute-start(bf16[2,144,1024]{2,1,0:T(8,128)(2,1)} %slice.404), channel_id=1, source_target_pairs={{0,8},{4,12},{8,0},{12,4},{16,24},{20,28},{24,16},{28,20},{1,9},{5... | collective-permute-start | bytes 1769480 | tf_op jit(solution)/shard_map/ppermute | solution.py:84
  478.4 20.4 %collective-permute-start.54 = (bf16[2,144,1024]{2,1,0:T(8,128)(2,1)}, bf16[2,144,1024]{2,1,0:T(8,128)(2,1)}, u32[]{:S(2)}, u32[]{:S(2)}) collective-permute-start(bf16[2,144,1024]{2,1,0:T(8,128)(2,1)} %slice.405), channel_id=1, source_target_pairs={{0,16},{4,20},{8,24},{12,28},{16,0},{20,4},{24,8},{28,12},{1,17},{... | collective-permute-start | bytes 1769480 | tf_op jit(solution)/shard_map/ppermute | solution.py:84
  498.8 3.3 collective-permute-start.55
  498.9 3.2 collective-permute-start.56
  (67 other events, 438.6 us)
Sparse Core Ops, SparseCore 0:
  167.8 36.0 all-gather.7
  206.3 23.5 all-gather.9
  254.0 71.3 reduce-scatter.1
  344.9 50.5 all-gather.5
